TPU v7x, 32 devices: a whole 2x2x4 slice. The times are simulated.
32 devices in a mesh: groups: 2 (over x), pages: 16 (over z, y, core).
Axes of the slice: x: 2, y: 2, z: 4, core: 2. Of those that a mesh axis runs over, the one named last changes fastest.
Arguments:
- queries: bfloat16 [2, 512, 8192], P(None, 'groups'), parts along dimension 1, may hold values from -14 to 14
- kv_cache: bfloat16 [256, 128, 2, 1024], P(('groups', 'pages')), parts along dimension 0, may hold values from -14 to 14
- w_out: bfloat16 [8192, 8192], P('pages'), may hold values from -0.0625 to 0.0625
- slot_page_before: int32 [256], P(('groups', 'pages')), parts along dimension 0, may hold values from -1 to 127, as said below
- slot_page_after: int32 [256], P(('groups', 'pages')), parts along dimension 0, may hold values from -1 to 127, as said below
- move_out: int32 [32, 4], P(('groups', 'pages')), parts along dimension 0, may hold values from -1 to 7, as said below
- move_in: int32 [32, 4], P(('groups', 'pages')), parts along dimension 0, may hold values from -1 to 7, as said below
- positions: int32 [2, 512], P(None, 'groups'), parts along dimension 1, may hold values from 0 to 16383, as said below
Outputs:
- attn_output: bfloat16 [2, 512, 8192], P(None, ('groups', 'pages')), parts along dimension 1
- cache_after: bfloat16 [256, 128, 2, 1024], P(('groups', 'pages')), parts along dimension 0
There are 2 independent parts, one for each index of `groups`. A program takes and returns all parts, laid end to end along the dimension named above; an argument that names none is the same for every part. Nothing has to cross between parts.
Inputs may be any that keep to these rules, and one draw needn't show every extreme that they name: `slot_page_before`: the logical page held by each slot; -1 marks a free slot; the live pages are the last ones of the sequence, numbered consecutively up to 127, each in exactly one slot; an owner's free slots are its last ones. `slot_page_after`: pages that are not sent keep their slot, each sent page sits in the slot that move_in names at its new owner, and a slot that sent its page is free. `move_out`: entry [j, o - 1] is a slot of owner j holding a live page, sent to owner (j + o) mod 16, or -1; the slots of one row differ; an owner sends at most one page to each of its next 4 owners. `move_in`: entry [j, o - 1] is a slot of owner j that is free before the moves, or -1, which it is exactly where move_out[(j - o) mod 16, o - 1] is -1; the slots of one row differ. Each row holds 256 consecutive positions; row 1 ends at the last position of the last live page; at most 256 positions lie between the end of row 0 and the start of row 1; all lie within the live pages.
All inputs are finite; a program needn't handle non-finite values.
Results may differ from a plain program's by a relative error of at most 0.0055.
Values may be sent and summed in bfloat16 or wider, within the bound.
No kernel may reach another device: no remote copies, remote signals or barrier semaphores. Data moves between devices by JAX's collectives and lax.ppermute only.
A program may use at most 192 MiB of HBM per device.

v0:
```python
import functools

import jax
import jax.numpy as jnp
from jax import lax
from jax.experimental import pallas as pl
from jax.experimental.pallas import tpu as pltpu
from jax.sharding import PartitionSpec as P

HEADS = 64
KV_HEADS = 8
HEAD_DIM = 128
PAGE_TOK = 128
BLOCK = 256
MOVE_WIN = 4
GROUP = HEADS // KV_HEADS

FLOOR = -1e30
FAR = 1 << 30
SCALE = HEAD_DIM**-0.5 * 1.4426950408889634

WIDE = 16
NARROW = 8
FIRST_SLOTS = 5
COLUMN_PARTS = 2

ANY = pl.BlockSpec(memory_space=pl.ANY)


def permute_to(x, n, target):
    return lax.ppermute(x, "pages", [(i, target(i)) for i in range(n)])


def head_of(j):
    half = KV_HEADS // 2
    return (j % 2) * half + j // 2


def place_of(p):
    return (p % 2) * 4 + (p // 2 % 2) * 2 + p // 4


def split_heads_kernel(kv_ref, ids_ref, out_ref, buf, in_sems, out_sems, *, first, count):
    extra = ids_ref.shape[0]
    loads = []
    for d in range(KV_HEADS):
        lanes = pl.ds(head_of(d) * HEAD_DIM, HEAD_DIM)
        row = [
            pltpu.make_async_copy(
                kv_ref.at[first + i, :, :, lanes],
                buf.at[d, pl.ds(i * PAGE_TOK, PAGE_TOK)],
                in_sems.at[d, i],
            )
            for i in range(count)
        ]
        row.append(
            pltpu.make_async_copy(
                ids_ref, buf.at[d, pl.ds(count * PAGE_TOK, extra)], in_sems.at[d, count]
            )
        )
        loads.append(row)
    stores = [
        pltpu.make_async_copy(buf.at[d], out_ref.at[d], out_sems.at[d])
        for d in range(KV_HEADS)
    ]
    for row in loads:
        for load in row:
            load.start()
    for row, store in zip(loads, stores):
        for load in row:
            load.wait()
        store.start()
    for store in stores:
        store.wait()


def split_heads(kv_cache, ids, first, count):
    shape = (KV_HEADS, count * PAGE_TOK + ids.shape[0], 2, HEAD_DIM)
    return pl.pallas_call(
        functools.partial(split_heads_kernel, first=first, count=count),
        out_shape=jax.ShapeDtypeStruct(shape, kv_cache.dtype),
        in_specs=[ANY, ANY],
        out_specs=ANY,
        scratch_shapes=[
            pltpu.VMEM(shape, kv_cache.dtype),
            pltpu.SemaphoreType.DMA((KV_HEADS, count + 1)),
            pltpu.SemaphoreType.DMA((KV_HEADS,)),
        ],
        name="split_heads",
    )(kv_cache, ids)


def outgoing_kernel(move_out, kv_ref, *refs):
    outs = refs[:MOVE_WIN]
    buf, in_sems, out_sems = refs[MOVE_WIN:]
    loads = [
        pltpu.make_async_copy(
            kv_ref.at[jnp.maximum(move_out[o], 0)], buf.at[o], in_sems.at[o]
        )
        for o in range(MOVE_WIN)
    ]
    stores = [
        pltpu.make_async_copy(buf.at[o], outs[o], out_sems.at[o]) for o in range(MOVE_WIN)
    ]
    for load in loads:
        load.start()
    for load, store in zip(loads, stores):
        load.wait()
        store.start()
    for store in stores:
        store.wait()


def outgoing_pages(kv_cache, move_out):
    page = jax.ShapeDtypeStruct(kv_cache.shape[1:], kv_cache.dtype)
    return pl.pallas_call(
        outgoing_kernel,
        out_shape=(page,) * MOVE_WIN,
        grid_spec=pltpu.PrefetchScalarGridSpec(
            num_scalar_prefetch=1,
            grid=(),
            in_specs=[ANY],
            out_specs=(ANY,) * MOVE_WIN,
            scratch_shapes=[
                pltpu.VMEM((MOVE_WIN,) + kv_cache.shape[1:], kv_cache.dtype),
                pltpu.SemaphoreType.DMA((MOVE_WIN,)),
                pltpu.SemaphoreType.DMA((MOVE_WIN,)),
            ],
        ),
        name="outgoing_pages",
    )(move_out, kv_cache)


def arrange_kernel(page_after, move_in, kv_ref, *refs):
    arrived = refs[:MOVE_WIN]
    _, out_ref, buf, zero_ref, in_sems, out_sems = refs[MOVE_WIN:]
    slots = out_ref.shape[0]
    filled = []
    for s in range(slots):
        taken = jnp.zeros((), jnp.bool_)
        for o in reversed(range(MOVE_WIN)):
            lands = move_in[o] == s

            @pl.when(lands & jnp.logical_not(taken))
            def _():
                pltpu.make_async_copy(arrived[o], buf.at[s], in_sems.at[s]).start()

            taken = taken | lands
        kept = page_after[s] >= 0

        @pl.when(kept & jnp.logical_not(taken))
        def _():
            pltpu.make_async_copy(kv_ref.at[s], buf.at[s], in_sems.at[s]).start()

        filled.append(kept | taken)
    zero_ref[...] = jnp.zeros(zero_ref.shape, zero_ref.dtype)
    for s in range(slots):

        @pl.when(filled[s])
        def _():
            pltpu.make_async_copy(kv_ref.at[s], buf.at[s], in_sems.at[s]).wait()
            pltpu.make_async_copy(buf.at[s], out_ref.at[s], out_sems.at[s]).start()

        @pl.when(jnp.logical_not(filled[s]))
        def _():
            pltpu.make_async_copy(zero_ref, out_ref.at[s], out_sems.at[s]).start()

    for s in range(slots):
        pltpu.make_async_copy(zero_ref, out_ref.at[s], out_sems.at[s]).wait()


def arrange_pages(kv_cache, arrived, page_after, move_in, after):
    slots = kv_cache.shape[0]
    return pl.pallas_call(
        arrange_kernel,
        out_shape=jax.ShapeDtypeStruct(kv_cache.shape, kv_cache.dtype),
        grid_spec=pltpu.PrefetchScalarGridSpec(
            num_scalar_prefetch=2,
            grid=(),
            in_specs=[ANY] * (2 + MOVE_WIN),
            out_specs=ANY,
            scratch_shapes=[
                pltpu.VMEM(kv_cache.shape, kv_cache.dtype),
                pltpu.VMEM(kv_cache.shape[1:], kv_cache.dtype),
                pltpu.SemaphoreType.DMA((slots,)),
                pltpu.SemaphoreType.DMA((slots,)),
            ],
        ),
        name="arrange_pages",
    )(page_after, move_in, kv_cache, *arrived, after)


def rows_kernel(place, q_ref, out_ref, *, ways, tok_rows):
    tok = out_ref.shape[1] // GROUP
    gp = GROUP // ways
    head = place[0]
    t_rel = pl.program_id(0) // 2
    t = place[1] ^ t_rel
    for p in range(KV_HEADS):
        kx = place_of(p)
        at = pl.multiple_of(((kx ^ head) * ways + t) * tok_rows, tok_rows)
        for gx in range(GROUP):
            g = ((gx // gp) ^ t) * gp + gx % gp
            lanes = pl.ds(pl.multiple_of(g * HEAD_DIM, HEAD_DIM), HEAD_DIM)
            to = gx * tok + p * tok_rows
            out_ref[0, to : to + tok_rows, :] = q_ref[0, pl.ds(at, tok_rows), lanes]


def query_rows(queries, place, ways, tok_rows):
    width = GROUP * HEAD_DIM
    tok = KV_HEADS * tok_rows
    dtype = queries.dtype
    if tok_rows % 16:
        queries = lax.dynamic_slice_in_dim(queries, place[0] * width, width, axis=2)
        queries = queries.astype(jnp.float32)
        column = lambda i, place: (i % 2, 0, 0)
    else:
        column = lambda i, place: (i % 2, 0, place[0])
    return pl.pallas_call(
        functools.partial(rows_kernel, ways=ways, tok_rows=tok_rows),
        out_shape=jax.ShapeDtypeStruct((2 * ways, GROUP * tok, HEAD_DIM), queries.dtype),
        grid_spec=pltpu.PrefetchScalarGridSpec(
            num_scalar_prefetch=1,
            grid=(2 * ways,),
            in_specs=[pl.BlockSpec((1, queries.shape[1], width), column)],
            out_specs=pl.BlockSpec((1, GROUP * tok, HEAD_DIM), lambda i, place: (i, 0, 0)),
        ),
        name="query_rows",
    )(place, queries).astype(dtype)


def three_parts(x):
    high = x.astype(jnp.bfloat16)
    rest = x - high.astype(jnp.float32)
    mid = rest.astype(jnp.bfloat16)
    low = (rest - mid.astype(jnp.float32)).astype(jnp.bfloat16)
    return high, mid, low


def attend_kernel(
    place, x_ref, q_ref, *refs, first_slot, first, last, rows, tok, ways, tok_rows, block
):
    n_in = 0 if first else 2
    carried = refs[:n_in]
    outs = refs[n_in : n_in + (ways if last else 2)]
    k_s, v_s, acc_s, m_s, ids_s, order, pages, ids, counts, sem = refs[n_in + len(outs) :]
    step = pl.program_id(0)
    sources = x_ref.shape[0]
    src_slots = x_ref.shape[1] // (2 * PAGE_TOK)
    n_slots = sources * src_slots
    head, way = place[0], place[1]

    @pl.when(step == 0)
    def _():
        end = src_slots * 2 * PAGE_TOK
        extra = x_ref.shape[1] - end
        row = lax.broadcasted_iota(jnp.int32, (extra, HEAD_DIM), 0)
        col = lax.broadcasted_iota(jnp.int32, (extra, HEAD_DIM), 1)
        for src in range(sources):
            tail = x_ref[src, end : end + extra, :].astype(jnp.float32)
            line = jnp.sum(jnp.where(row == 2 * col, tail, 0.0), axis=0, keepdims=True)
            ids_s[src : src + 1, :] = line.astype(jnp.int32)
        copy = pltpu.make_async_copy(ids_s, ids, sem)
        copy.start()
        copy.wait()
        lowest = jnp.minimum(place[2], place[3])

        def fully(page):
            return (page >= 0) & (page * PAGE_TOK + (PAGE_TOK - 1) <= lowest)

        def put_full(i, count):
            page = ids[i // src_slots, first_slot + i % src_slots]
            pages[i] = page
            yes = fully(page)

            @pl.when(yes)
            def _():
                order[count] = i

            return count + yes.astype(jnp.int32)

        def put_rest(i, count):
            yes = (pages[i] >= 0) & jnp.logical_not(fully(pages[i]))

            @pl.when(yes)
            def _():
                order[count] = i

            return count + yes.astype(jnp.int32)

        n_full = lax.fori_loop(0, n_slots, put_full, 0)
        n_live = lax.fori_loop(0, n_slots, put_rest, n_full)
        counts[0] = n_full
        counts[1] = n_live

        row = lax.broadcasted_iota(jnp.int32, (2 * PAGE_TOK, 2 * PAGE_TOK), 0)
        col = lax.broadcasted_iota(jnp.int32, (2 * PAGE_TOK, 2 * PAGE_TOK), 1)
        want = jnp.where(row < PAGE_TOK, 2 * row, 2 * (row - PAGE_TOK) + 1)
        pick = jnp.where(col == want, 1.0, 0.0).astype(jnp.bfloat16)
        ones = jnp.ones((PAGE_TOK, HEAD_DIM), jnp.bfloat16)

        def split_step(i, carry):
            for s in range(NARROW):
                at = i * NARROW + s
                slot = order[jnp.minimum(at, n_live - 1)]
                both = jnp.dot(
                    pick,
                    x_ref[
                        slot // src_slots,
                        pl.ds(
                            pl.multiple_of(slot % src_slots * 2 * PAGE_TOK, 2 * PAGE_TOK),
                            2 * PAGE_TOK,
                        ),
                        :,
                    ],
                    preferred_element_type=jnp.float32,
                ).astype(jnp.bfloat16)
                to = pl.ds(pl.multiple_of(at * PAGE_TOK, PAGE_TOK), PAGE_TOK)
                k_s[to, :] = both[:PAGE_TOK]
                v_s[to, :HEAD_DIM] = both[PAGE_TOK:]
                v_s[to, HEAD_DIM:] = ones
            return carry

        lax.fori_loop(0, (n_live + NARROW - 1) // NARROW, split_step, 0)

    n_full, n_live = counts[0], counts[1]
    total = GROUP * tok
    if first:
        m_s[...] = jnp.full(m_s.shape, FLOOR, jnp.float32)
        acc_s[...] = jnp.zeros(acc_s.shape, jnp.float32)
    else:
        acc_s[...] = carried[0][0]
        m_s[...] = carried[1][0]

    if block is None:
        t_rel, b = step // 2, step % 2
    else:
        t_rel, b = step, block
    line = lax.broadcasted_iota(jnp.int32, (tok, PAGE_TOK), 0)
    p = line // tok_rows
    kx = place_of(p)
    token = ((kx ^ head) * ways + (t_rel ^ way)) * tok_rows + line % tok_rows
    q_at = token + jnp.where(b == 0, place[2], place[3])

    def tile_step(at, size, masked):
        span_k = pl.ds(pl.multiple_of(at * PAGE_TOK, PAGE_TOK), size * PAGE_TOK)
        keys = k_s[span_k, :]
        values = v_s[span_k, :]
        if masked:
            lane = lax.broadcasted_iota(jnp.int32, (tok, PAGE_TOK), 1)
            visible = []
            for s in range(size):
                slot = order[jnp.minimum(at + s, n_live - 1)]
                start = jnp.where(at + s < n_live, pages[slot] * PAGE_TOK, FAR)
                seen = lane + start <= q_at
                visible.append(jnp.concatenate([seen] * (rows // tok), axis=0))

        def score(part):
            return lax.dot_general(
                q_ref[0, part * rows : (part + 1) * rows, :],
                keys,
                (((1,), (1,)), ((), ())),
                preferred_element_type=jnp.float32,
            )

        def soften(part, scores):
            span = slice(part * rows, (part + 1) * rows)
            pieces = [scores[:, s * PAGE_TOK : (s + 1) * PAGE_TOK] for s in range(size)]
            if masked:
                pieces = [jnp.where(v, x, FLOOR) for v, x in zip(visible, pieces)]
            peak = functools.reduce(jnp.maximum, pieces)
            m_old = m_s[span, :]
            m_new = jnp.maximum(m_old, jnp.max(peak, axis=1, keepdims=True) * SCALE)
            shift = jnp.maximum(m_new, 0.5 * FLOOR * SCALE) if masked else m_new
            weights = jnp.concatenate(
                [jnp.exp2(x * SCALE - shift).astype(jnp.bfloat16) for x in pieces], axis=1
            )
            m_s[span, :] = m_new
            return weights, jnp.exp2(m_old - m_new)

        def gather(part, weights, alpha):
            span = slice(part * rows, (part + 1) * rows)
            mixed = jnp.dot(weights, values, preferred_element_type=jnp.float32)
            acc_s[span, :HEAD_DIM] = acc_s[span, :HEAD_DIM] * alpha + mixed[:, :HEAD_DIM]
            acc_s[span, HEAD_DIM:] = acc_s[span, HEAD_DIM:] * alpha + mixed[:, HEAD_DIM:]

        parts = total // rows
        scores = score(0)
        waiting = None
        for part in range(parts):
            following = score(part + 1) if part + 1 < parts else None
            weights, alpha = soften(part, scores)
            if waiting is not None:
                gather(*waiting)
            waiting = (part, weights, alpha)
            scores = following
        gather(*waiting)

    n_wide = n_full // WIDE
    n_open = (n_full - n_wide * WIDE) // NARROW
    base = n_wide * WIDE
    done = base + n_open * NARROW
    n_masked = (n_live - done + NARROW - 1) // NARROW

    def wide(i, carry):
        tile_step(i * WIDE, WIDE, False)
        return carry

    def narrow(i, carry):
        tile_step(base + i * NARROW, NARROW, False)
        return carry

    def masked(i, carry):
        tile_step(done + i * NARROW, NARROW, True)
        return carry

    lax.fori_loop(0, n_wide, wide, 0)
    lax.fori_loop(0, n_open, narrow, 0)
    lax.fori_loop(0, n_masked, masked, 0)

    if not last:
        outs[0][0] = acc_s[...]
        outs[1][0] = m_s[...]
    else:
        row = lax.broadcasted_iota(jnp.int32, (tok, HEAD_DIM), 0)
        col = lax.broadcasted_iota(jnp.int32, (tok, HEAD_DIM), 1)
        eye = row == col
        lines = []
        for ref, lanes in ((m_s, slice(0, HEAD_DIM)), (acc_s, slice(HEAD_DIM, 2 * HEAD_DIM))):
            for g in range(GROUP):
                span = slice(g * tok, (g + 1) * tok)
                lines.append(
                    jnp.sum(jnp.where(eye, ref[span, lanes], 0.0), axis=0, keepdims=True)
                )
        stats = jnp.concatenate(lines, axis=0)
        for w in range(ways):

            @pl.when(step == w)
            def _():
                outs[w][:total, :] = acc_s[:, :HEAD_DIM].astype(jnp.bfloat16)
                for i, piece in enumerate(three_parts(stats)):
                    at = total + i * 2 * GROUP
                    outs[w][at : at + 2 * GROUP, :] = piece


def attend(place, x, first_slot, q, carried, block, tok_rows, rows):
    sources = x.shape[0]
    src_slots = x.shape[1] // (2 * PAGE_TOK)
    steps, total, _ = q.shape
    tok = total // GROUP
    first = carried is None
    last = block is not None
    ways = steps // 2
    n_slots = -(-sources * src_slots // WIDE) * WIDE
    if last:
        grid = ways
        at = lambda i, *_: (2 * i + block, 0, 0)
    else:
        grid = steps
        at = lambda i, *_: (i, 0, 0)
    in_specs = [
        pl.BlockSpec(x.shape, lambda i, *_: (0, 0, 0)),
        pl.BlockSpec((1, total, HEAD_DIM), at),
    ]
    sent = total + 3 * 2 * GROUP
    if last:
        out_shape = (jax.ShapeDtypeStruct((sent, HEAD_DIM), jnp.bfloat16),) * ways
        out_specs = (pl.BlockSpec((sent, HEAD_DIM), lambda i, *_: (0, 0)),) * ways
    else:
        out_shape = (
            jax.ShapeDtypeStruct((steps, total, 2 * HEAD_DIM), jnp.float32),
            jax.ShapeDtypeStruct((steps, total, HEAD_DIM), jnp.float32),
        )
        out_specs = (
            pl.BlockSpec((1, total, 2 * HEAD_DIM), at),
            pl.BlockSpec((1, total, HEAD_DIM), at),
        )
    extra = ()
    if not first:
        extra = tuple(carried)
        in_specs += [
            pl.BlockSpec((1, total, 2 * HEAD_DIM), at),
            pl.BlockSpec((1, total, HEAD_DIM), at),
        ]
    flops = 8 * grid * total * sources * src_slots * PAGE_TOK * HEAD_DIM
    return pl.pallas_call(
        functools.partial(
            attend_kernel,
            first_slot=first_slot,
            first=first,
            last=last,
            rows=rows,
            tok=tok,
            ways=ways,
            tok_rows=tok_rows,
            block=block,
        ),
        out_shape=out_shape,
        grid_spec=pltpu.PrefetchScalarGridSpec(
            num_scalar_prefetch=1,
            grid=(grid,),
            in_specs=in_specs,
            out_specs=out_specs,
            scratch_shapes=[
                pltpu.VMEM((n_slots * PAGE_TOK, HEAD_DIM), jnp.bfloat16),
                pltpu.VMEM((n_slots * PAGE_TOK, 2 * HEAD_DIM), jnp.bfloat16),
                pltpu.VMEM((total, 2 * HEAD_DIM), jnp.float32),
                pltpu.VMEM((total, HEAD_DIM), jnp.float32),
                pltpu.VMEM((sources, HEAD_DIM), jnp.int32),
                pltpu.SMEM((n_slots,), jnp.int32),
                pltpu.SMEM((n_slots,), jnp.int32),
                pltpu.SMEM((sources, HEAD_DIM), jnp.int32),
                pltpu.SMEM((2,), jnp.int32),
                pltpu.SemaphoreType.DMA(()),
            ],
        ),
        cost_estimate=pl.CostEstimate(
            flops=flops, transcendentals=flops // (8 * HEAD_DIM), bytes_accessed=x.size * 2
        ),
        name="attend_last" if last else "attend_first",
    )(place, x, q, *extra)


def merge(parts, a_ref, tok):
    total = GROUP * tok
    row = lax.broadcasted_iota(jnp.int32, (tok, HEAD_DIM), 0)
    col = lax.broadcasted_iota(jnp.int32, (tok, HEAD_DIM), 1)
    eye = row == col
    stats = []
    for part in parts:
        pieces = [
            part[total + i * 2 * GROUP : total + (i + 1) * 2 * GROUP, :].astype(jnp.float32)
            for i in range(3)
        ]
        stats.append((pieces[0] + pieces[1]) + pieces[2])
    tops = functools.reduce(jnp.maximum, [s[:GROUP] for s in stats])
    factors = [jnp.exp2(s[:GROUP] - tops) for s in stats]
    totals = sum(f * s[GROUP:] for f, s in zip(factors, stats))
    for g in range(GROUP):
        span = slice(g * tok, (g + 1) * tok)
        mixed = 0.0
        for f, part in zip(factors, parts):
            ratio = jnp.where(eye, f[g : g + 1] / totals[g : g + 1], 0.0)
            mixed += jnp.sum(ratio, axis=1, keepdims=True) * part[span, :].astype(jnp.float32)
        a_ref[:, g * HEAD_DIM : (g + 1) * HEAD_DIM] = mixed.astype(jnp.bfloat16)


def project_kernel(*refs, n_parts, n_ws, tok, y_first):
    parts = refs[:n_parts]
    ws = refs[n_parts : n_parts + n_ws]
    outs = refs[n_parts + n_ws :]
    keep_ref, send_ref = outs[:2]
    if n_parts == n_ws:
        a_ref = outs[2]

        @pl.when(pl.program_id(0) == 0)
        def _():
            merge(parts, a_ref, tok)

    else:
        a_ref = parts[0]
    depth = a_ref.shape[1] // n_ws
    total = 0.0
    for s in range(n_ws):
        total += jnp.dot(
            a_ref[:, s * depth : (s + 1) * depth], ws[s][...], preferred_element_type=jnp.float32
        )
    if y_first:
        keep, send = total[: tok // 2], total[tok // 2 :]
    else:
        quarters = [total[i * tok // 4 : (i + 1) * tok // 4] for i in range(4)]
        keep = jnp.concatenate(quarters[0::2], axis=0)
        send = jnp.concatenate(quarters[1::2], axis=0)
    keep_ref[...] = keep
    send_ref[...] = send.astype(jnp.bfloat16)


def project(parts, ws, tok, column_part, y_first, width=1024):
    columns = ws[0].shape[1] // COLUMN_PARTS
    steps = columns // width
    fixed = lambda i: (0, 0)
    half = tok // 2
    depth = sum(w.shape[0] for w in ws)
    merging = len(parts) == len(ws)
    out_shape = [
        jax.ShapeDtypeStruct((half, columns), jnp.float32),
        jax.ShapeDtypeStruct((half, columns), jnp.bfloat16),
    ]
    out_specs = [
        pl.BlockSpec((half, width), lambda i: (0, i)),
        pl.BlockSpec((half, width), lambda i: (0, i)),
    ]
    if merging:
        out_shape.append(jax.ShapeDtypeStruct((tok, depth), jnp.bfloat16))
        out_specs.append(pl.BlockSpec((tok, depth), fixed))
    return pl.pallas_call(
        functools.partial(
            project_kernel, n_parts=len(parts), n_ws=len(ws), tok=tok, y_first=y_first
        ),
        out_shape=out_shape,
        grid=(steps,),
        in_specs=[pl.BlockSpec(o.shape, fixed) for o in parts]
        + [
            pl.BlockSpec((w.shape[0], width), lambda i: (0, column_part * steps + i)) for w in ws
        ],
        out_specs=out_specs,
        cost_estimate=pl.CostEstimate(
            flops=2 * tok * depth * columns, transcendentals=0, bytes_accessed=2 * depth * columns
        ),
        name="project",
    )(*parts, *ws)


def local(
    queries, kv_cache, w_out, slot_page_before, slot_page_after, move_out, move_in, positions
):
    n = lax.axis_size("pages")
    slots = kv_cache.shape[0]
    ways = n // KV_HEADS
    tok_rows = BLOCK // n
    tok = BLOCK // ways
    me = lax.axis_index("pages")
    way = me // KV_HEADS
    head = head_of(me % KV_HEADS)
    groups = [[a * KV_HEADS + b for b in range(KV_HEADS)] for a in range(ways)]

    def exchange(x):
        return lax.all_to_all(x, "pages", 0, 0, axis_index_groups=groups, tiled=True)

    ids = jnp.broadcast_to(slot_page_before[:, None, None], (slots, 2, HEAD_DIM))
    ids = ids.astype(kv_cache.dtype)
    cuts = [(0, FIRST_SLOTS), (FIRST_SLOTS, slots - FIRST_SLOTS)]
    arrived = []
    for at, count in cuts:
        piece = split_heads(kv_cache, ids, at, count)
        got = exchange(piece)
        arrived.append(got.reshape(KV_HEADS, -1, HEAD_DIM))
    place = jnp.stack([head, way, positions[0, 0], positions[1, 0]]).astype(jnp.int32)
    q = query_rows(queries, place, ways, tok_rows)

    leaving = outgoing_pages(kv_cache, move_out[0])
    landed = []
    for o in range(1, MOVE_WIN + 1):
        landed.append(permute_to(leaving[o - 1], n, lambda i: (i + o) % n))

    ws = [w_out]
    for s in range(1, ways):
        ws.append(permute_to(w_out, n, lambda i: i ^ s))

    rows = 2 * tok
    carried = attend(place, arrived[0], 0, q, None, None, tok_rows, rows)

    def merger(i, s):
        return head_of(i % KV_HEADS) * ways + ((i // KV_HEADS) ^ s)

    partial = []
    for b in range(2):
        out = attend(place, arrived[1], FIRST_SLOTS, q, carried, b, tok_rows, rows)
        parts = []
        for s in range(ways):
            parts.append(permute_to(out[s], n, lambda i: merger(i, s)))
        partial.append(parts)

    sums = []
    for b in range(2):
        merged = partial[b]
        for c in range(COLUMN_PARTS):
            y_first = (b, c) != (0, 1)
            keep, send, *a = project(merged, ws, tok, c, y_first)
            if a:
                merged = a
            turns = (1, 2, 4) if y_first else (2, 1, 4)
            got = permute_to(send, n, lambda i: i ^ (turns[0] * ways))
            sums.append((keep, got, turns))
    cache_after = arrange_pages(kv_cache, landed, slot_page_after, move_in[0], send)

    results = []
    for keep, got, turns in sums:
        for turn in turns[1:]:
            total = keep + got.astype(jnp.float32)
            half = total.shape[0] // 2
            keep = total[:half]
            got = permute_to(
                total[half:].astype(jnp.bfloat16), n, lambda i: i ^ (turn * ways)
            )
        results.append((keep + got.astype(jnp.float32)).astype(jnp.bfloat16))
    out = jnp.stack(
        [
            jnp.concatenate(results[b * COLUMN_PARTS : (b + 1) * COLUMN_PARTS], axis=1)
            for b in range(2)
        ]
    )
    return (out, cache_after)


def solution(mesh):
    in_specs = (
        P(None, "groups", None),
        P(("groups", "pages"), None, None, None),
        P("pages", None),
        P(("groups", "pages")),
        P(("groups", "pages")),
        P(("groups", "pages"), None),
        P(("groups", "pages"), None),
        P(None, "groups"),
    )
    out_specs = (P(None, ("groups", "pages"), None), P(("groups", "pages"), None, None, None))
    return jax.shard_map(local, mesh=mesh, in_specs=in_specs, out_specs=out_specs, check_vma=False)
```

profile of v0, /device:TPU:0, one launch (start us, length us, event | category | flops | bytes accessed | tf_op | source)
XLA Modules:
  0.0 245.1 jit_solution(13566983521229736888)
XLA Ops:
  2.0 3.6 %split_heads.3 = bf16[8,648,2,128]{3,2,1,0:T(2,128)(2,1)} custom-call(bf16[8,128,2,1024]{3,2,1,0:T(2,128)(2,1)} %kv_ref.7, bf16[8,2,128]{2,1,0:T(2,128)(2,1)} %broadcast_in_dim.2.ids_ref), custom_call_target="tpu_custom_call" | custom-call | tf_op jit(solution)/shard_map/split_heads/pallas_call | solution.py:79
  5.5 5.3 %all-to-all-start.1 = ((bf16[8,648,2,128]{3,2,1,0:T(2,128)(2,1)}), bf16[8,648,2,128]{3,2,1,0:T(2,128)(2,1)S(1)}, u32[]{:S(2)}, u32[]{:S(2)}) async-start(bf16[8,648,2,128]{3,2,1,0:T(2,128)(2,1)} %split_heads.3), calls=%async_computation.1 | async-start | bytes 5308416 | tf_op jit(solution)/shard_map/all_to_all | solution.py:628
  11.3 2.7 %split_heads.2 = bf16[8,392,2,128]{3,2,1,0:T(2,128)(2,1)} custom-call(bf16[8,128,2,1024]{3,2,1,0:T(2,128)(2,1)} %kv_ref.7, bf16[8,2,128]{2,1,0:T(2,128)(2,1)} %broadcast_in_dim.2.ids_ref), custom_call_target="tpu_custom_call" | custom-call | tf_op jit(solution)/shard_map/split_heads/pallas_call | solution.py:79
  14.1 28.4 %all-to-all-done.1 = bf16[8,648,2,128]{3,2,1,0:T(2,128)(2,1)S(1)} async-done(((bf16[8,648,2,128]{3,2,1,0:T(2,128)(2,1)}), bf16[8,648,2,128]{3,2,1,0:T(2,128)(2,1)S(1)}, u32[]{:S(2)}, u32[]{:S(2)}) %all-to-all-start.1) | async-done | bytes 2654240 | tf_op jit(solution)/shard_map/all_to_all | solution.py:628
  42.5 4.3 %all-to-all-start = ((bf16[8,392,2,128]{3,2,1,0:T(2,128)(2,1)}), bf16[8,392,2,128]{3,2,1,0:T(2,128)(2,1)}, u32[]{:S(2)}, u32[]{:S(2)}) async-start(bf16[8,392,2,128]{3,2,1,0:T(2,128)(2,1)} %split_heads.2), calls=%async_computation | async-start | bytes 3211264 | tf_op jit(solution)/shard_map/all_to_all | solution.py:628
  49.3 4.3 %query_rows.1.q_ref = bf16[4,1024,128]{2,1,0:T(8,128)(2,1)} custom-call(s32[4]{0:T(128)} %pad_add_fusion.place, bf16[2,256,8192]{2,1,0:T(8,128)(2,1)} %q_ref.1), custom_call_target="tpu_custom_call" | custom-call | tf_op jit(solution)/shard_map/query_rows/pallas_call | solution.py:219
  53.7 37.4 %attend_first.1 = (f32[4,1024,256]{2,1,0:T(8,128)}, f32[4,1024,128]{2,1,0:T(8,128)}) custom-call(s32[4]{0:T(128)} %pad_add_fusion.place, bf16[8,1296,128]{2,1,0:T(8,128)(2,1)} %bitcast.12, bf16[4,1024,128]{2,1,0:T(8,128)(2,1)} %query_rows.1.q_ref), custom_call_target="tpu_custom_call" | custom-call | flops 21474836480 | bytes 2654208 | tf_op jit(solution)/shard_map/attend_first/pallas_call | solution.py:486
  91.1 9.9 %attend_last.3 = (bf16[1072,128]{1,0:T(8,128)(2,1)}, bf16[1072,128]{1,0:T(8,128)(2,1)}) custom-call(s32[4]{0:T(128)} %pad_add_fusion.place, bf16[8,784,128]{2,1,0:T(8,128)(2,1)} %bitcast.4.x_ref, bf16[4,1024,128]{2,1,0:T(8,128)(2,1)} %query_rows.1.q_ref, f32[4,1024,256]{2,1,0:T(8,128)} %get-tuple-element.22.refs_0_, f32[4,1024,128]{2,1,0:T(8,128)} %get-tuple-element.23.refs_1_), custom_call_target="tpu_custom_call" | custom-call | flops 6442450944 | bytes 1605632 | tf_op jit(solution)/shard_map/attend_last/pallas_call | solution.py:486
  102.6 3.1 %collective-permute-start.10 = (bf16[1072,128]{1,0:T(8,128)(2,1)}, bf16[1072,128]{1,0:T(8,128)(2,1)S(1)}, u32[]{:S(2)}, u32[]{:S(2)}) collective-permute-start(bf16[1072,128]{1,0:T(8,128)(2,1)} %get-tuple-element.32), channel_id=1, source_target_pairs={{0,1},{1,9},{2,3},{3,11},{4,5},{5,13},{6,7},{7,15},{8,0},{9,8},{10... | collective-permute-start | bytes 823304 | tf_op jit(solution)/shard_map/ppermute | solution.py:31
  105.7 9.9 %attend_last.2 = (bf16[1072,128]{1,0:T(8,128)(2,1)}, bf16[1072,128]{1,0:T(8,128)(2,1)}) custom-call(s32[4]{0:T(128)} %pad_add_fusion.place, bf16[8,784,128]{2,1,0:T(8,128)(2,1)} %bitcast.4.x_ref, bf16[4,1024,128]{2,1,0:T(8,128)(2,1)} %query_rows.1.q_ref, f32[4,1024,256]{2,1,0:T(8,128)} %get-tuple-element.22.refs_0_, f32[4,1024,128]{2,1,0:T(8,128)} %get-tuple-element.23.refs_1_), custom_call_target="tpu_custom_call" | custom-call | flops 6442450944 | bytes 1605632 | tf_op jit(solution)/shard_map/attend_last/pallas_call | solution.py:486
  117.8 3.1 %outgoing_pages.1 = (bf16[128,2,1024]{2,1,0:T(2,128)(2,1)}, bf16[128,2,1024]{2,1,0:T(2,128)(2,1)}, bf16[128,2,1024]{2,1,0:T(2,128)(2,1)}, bf16[128,2,1024]{2,1,0:T(2,128)(2,1)}) custom-call(s32[4]{0:T(128)} %bitcast.13, bf16[8,128,2,1024]{3,2,1,0:T(2,128)(2,1)} %kv_ref.7), custom_call_target="tpu_custom_call" | custom-call | tf_op jit(solution)/shard_map/outgoing_pages/pallas_call | solution.py:116
  123.4 42.2 %collective-permute-start.19 = (bf16[128,2,1024]{2,1,0:T(2,128)(2,1)}, bf16[128,2,1024]{2,1,0:T(2,128)(2,1)S(1)}, u32[]{:S(2)}, u32[]{:S(2)}) collective-permute-start(bf16[128,2,1024]{2,1,0:T(2,128)(2,1)} %get-tuple-element.40), channel_id=1, source_target_pairs={{0,3},{1,4},{2,5},{3,6},{4,7},{5,8},{6,9},{7,10},{8,11},{9,12},{10... | collective-permute-start | bytes 1572872 | tf_op jit(solution)/shard_map/ppermute | solution.py:31
  165.6 6.3 %project.6 = (f32[64,4096]{1,0:T(8,128)}, bf16[64,4096]{1,0:T(8,128)(2,1)}, bf16[128,1024]{1,0:T(8,128)(2,1)}) custom-call(bf16[1072,128]{1,0:T(8,128)(2,1)} %copy-done.9, bf16[1072,128]{1,0:T(8,128)(2,1)} %copy-done.11, bf16[512,8192]{1,0:T(8,128)(2,1)} %refs_1_.3, bf16[512,8192]{1,0:T(8,128)(2,1)} %collective-permute-done.2.refs_3_.refs_2_), custom_call_target="tpu_custom_call" | custom-call | flops 1073741824 | bytes 8388608 | tf_op jit(solution)/shard_map/project/pallas_call | solution.py:596
  172.6 6.3 %project.4 = (f32[64,4096]{1,0:T(8,128)}, bf16[64,4096]{1,0:T(8,128)(2,1)}, bf16[128,1024]{1,0:T(8,128)(2,1)}) custom-call(bf16[1072,128]{1,0:T(8,128)(2,1)} %copy-done.10, bf16[1072,128]{1,0:T(8,128)(2,1)} %copy-done.12, bf16[512,8192]{1,0:T(8,128)(2,1)} %refs_1_.3, bf16[512,8192]{1,0:T(8,128)(2,1)} %collective-permute-done.2.refs_3_.refs_2_), custom_call_target="tpu_custom_call" | custom-call | flops 1073741824 | bytes 8388608 | tf_op jit(solution)/shard_map/project/pallas_call | solution.py:596
  178.9 6.2 %project.5 = (f32[64,4096]{1,0:T(8,128)}, bf16[64,4096]{1,0:T(8,128)(2,1)}) custom-call(bf16[128,1024]{1,0:T(8,128)(2,1)} %get-tuple-element.28.refs_0_, bf16[512,8192]{1,0:T(8,128)(2,1)} %refs_1_.3, bf16[512,8192]{1,0:T(8,128)(2,1)} %collective-permute-done.2.refs_3_.refs_2_), custom_call_target="tpu_custom_call" | custom-call | flops 1073741824 | bytes 8388608 | tf_op jit(solution)/shard_map/project/pallas_call | solution.py:596
  185.1 6.1 %project.7 = (f32[64,4096]{1,0:T(8,128)}, bf16[64,4096]{1,0:T(8,128)(2,1)}) custom-call(bf16[128,1024]{1,0:T(8,128)(2,1)} %get-tuple-element.35.refs_0_, bf16[512,8192]{1,0:T(8,128)(2,1)} %refs_1_.3, bf16[512,8192]{1,0:T(8,128)(2,1)} %collective-permute-done.2.refs_3_.refs_2_), custom_call_target="tpu_custom_call" | custom-call | flops 1073741824 | bytes 8388608 | tf_op jit(solution)/shard_map/project/pallas_call | solution.py:596
  194.4 4.0 %arrange_pages.1 = bf16[8,128,2,1024]{3,2,1,0:T(2,128)(2,1)} custom-call(s32[8]{0:T(128)} %page_after.1, s32[4]{0:T(128)} %bitcast.14, bf16[8,128,2,1024]{3,2,1,0:T(2,128)(2,1)} %kv_ref.7, bf16[128,2,1024]{2,1,0:T(2,128)(2,1)} %copy-done.5, bf16[128,2,1024]{2,1,0:T(2,128)(2,1)} %copy-done.6, bf16[128,2,1024]{2,1,0:T(2,128)(2,1)} %copy-done.7, ...), custom_call_target="tpu_custom_call" | custom-call | tf_op jit(solution)/shard_map/arrange_pages/pallas_call | solution.py:174
  201.7 4.7 %collective-permute-done.3 = bf16[64,4096]{1,0:T(8,128)(2,1)} collective-permute-done((bf16[64,4096]{1,0:T(8,128)(2,1)}, bf16[64,4096]{1,0:T(8,128)(2,1)}, u32[]{:S(2)}, u32[]{:S(2)}) %collective-permute-start.3) | collective-permute-done | bytes 524320 | tf_op jit(solution)/shard_map/ppermute | solution.py:31
  210.4 7.3 %collective-permute-done.14 = bf16[64,4096]{1,0:T(8,128)(2,1)} collective-permute-done((bf16[64,4096]{1,0:T(8,128)(2,1)}, bf16[64,4096]{1,0:T(8,128)(2,1)}, u32[]{:S(2)}, u32[]{:S(2)}) %collective-permute-start.14) | collective-permute-done | bytes 524320 | tf_op jit(solution)/shard_map/ppermute | solution.py:31
  219.2 4.2 %collective-permute-start.13 = (bf16[16,4096]{1,0:T(8,128)(2,1)S(1)}, bf16[16,4096]{1,0:T(8,128)(2,1)S(1)}, u32[]{:S(2)}, u32[]{:S(2)}) collective-permute-start(bf16[16,4096]{1,0:T(8,128)(2,1)S(1)} %slice.125), channel_id=1, source_target_pairs={{0,8},{1,9},{2,10},{3,11},{4,12},{5,13},{6,14},{7,15},{8,0},{9,1},... | collective-permute-start | bytes 393224 | tf_op jit(solution)/shard_map/ppermute | solution.py:31
  223.7 3.0 %collective-permute-start.8 = (bf16[16,4096]{1,0:T(8,128)(2,1)S(1)}, bf16[16,4096]{1,0:T(8,128)(2,1)S(1)}, u32[]{:S(2)}, u32[]{:S(2)}) collective-permute-start(bf16[16,4096]{1,0:T(8,128)(2,1)S(1)} %slice.126), channel_id=1, source_target_pairs={{0,8},{1,9},{2,10},{3,11},{4,12},{5,13},{6,14},{7,15},{8,0},{9,1},... | collective-permute-start | bytes 393224 | tf_op jit(solution)/shard_map/ppermute | solution.py:31
  228.1 2.5 %collective-permute-start.16 = (bf16[16,4096]{1,0:T(8,128)(2,1)S(1)}, bf16[16,4096]{1,0:T(8,128)(2,1)S(1)}, u32[]{:S(2)}, u32[]{:S(2)}) collective-permute-start(bf16[16,4096]{1,0:T(8,128)(2,1)S(1)} %slice.124), channel_id=1, source_target_pairs={{0,8},{1,9},{2,10},{3,11},{4,12},{5,13},{6,14},{7,15},{8,0},{9,1},... | collective-permute-start | bytes 393224 | tf_op jit(solution)/shard_map/ppermute | solution.py:31
  230.6 7.0 %collective-permute-done.13 = bf16[16,4096]{1,0:T(8,128)(2,1)S(1)} collective-permute-done((bf16[16,4096]{1,0:T(8,128)(2,1)S(1)}, bf16[16,4096]{1,0:T(8,128)(2,1)S(1)}, u32[]{:S(2)}, u32[]{:S(2)}) %collective-permute-start.13) | collective-permute-done | bytes 131104 | tf_op jit(solution)/shard_map/ppermute | solution.py:31
  237.6 2.8 %collective-permute-done.5 = bf16[16,4096]{1,0:T(8,128)(2,1)S(1)} collective-permute-done((bf16[16,4096]{1,0:T(8,128)(2,1)S(1)}, bf16[16,4096]{1,0:T(8,128)(2,1)S(1)}, u32[]{:S(2)}, u32[]{:S(2)}) %collective-permute-start.5) | collective-permute-done | bytes 131104 | tf_op jit(solution)/shard_map/ppermute | solution.py:31
  (89 shorter events, 29.6 us)
Async XLA Ops:
  5.5 37.0 %all-to-all-start.1 = ((bf16[8,648,2,128]{3,2,1,0:T(2,128)(2,1)}), bf16[8,648,2,128]{3,2,1,0:T(2,128)(2,1)S(1)}, u32[]{:S(2)}, u32[]{:S(2)}) async-start(bf16[8,648,2,128]{3,2,1,0:T(2,128)(2,1)} %split_heads.3), calls=%async_computation.1 | async-start | bytes 5308416 | tf_op jit(solution)/shard_map/all_to_all | solution.py:628
  10.8 154.7 %collective-permute-start.2 = (bf16[512,8192]{1,0:T(8,128)(2,1)}, bf16[512,8192]{1,0:T(8,128)(2,1)}, u32[]{:S(2)}, u32[]{:S(2)}) collective-permute-start(bf16[512,8192]{1,0:T(8,128)(2,1)} %refs_1_.3), channel_id=1, source_target_pairs={{0,1},{1,0},{2,3},{3,2},{4,5},{5,4},{6,7},{7,6},{8,9},{9,8},{10,11... | collective-permute-start | bytes 25165832 | tf_op jit(solution)/shard_map/ppermute | solution.py:31
  42.5 48.6 %all-to-all-start = ((bf16[8,392,2,128]{3,2,1,0:T(2,128)(2,1)}), bf16[8,392,2,128]{3,2,1,0:T(2,128)(2,1)}, u32[]{:S(2)}, u32[]{:S(2)}) async-start(bf16[8,392,2,128]{3,2,1,0:T(2,128)(2,1)} %split_heads.2), calls=%async_computation | async-start | bytes 3211264 | tf_op jit(solution)/shard_map/all_to_all | solution.py:628
  101.0 20.0 %collective-permute-start.9 = (bf16[1072,128]{1,0:T(8,128)(2,1)}, bf16[1072,128]{1,0:T(8,128)(2,1)S(1)}, u32[]{:S(2)}, u32[]{:S(2)}) collective-permute-start(bf16[1072,128]{1,0:T(8,128)(2,1)} %get-tuple-element.31), channel_id=1, source_target_pairs={{0,0},{1,8},{2,2},{3,10},{4,4},{5,12},{6,6},{7,14},{8,1},{9,9},{10... | collective-permute-start | bytes 823304 | tf_op jit(solution)/shard_map/ppermute | solution.py:31
  102.6 18.4 %collective-permute-start.10 = (bf16[1072,128]{1,0:T(8,128)(2,1)}, bf16[1072,128]{1,0:T(8,128)(2,1)S(1)}, u32[]{:S(2)}, u32[]{:S(2)}) collective-permute-start(bf16[1072,128]{1,0:T(8,128)(2,1)} %get-tuple-element.32), channel_id=1, source_target_pairs={{0,1},{1,9},{2,3},{3,11},{4,5},{5,13},{6,7},{7,15},{8,0},{9,8},{10... | collective-permute-start | bytes 823304 | tf_op jit(solution)/shard_map/ppermute | solution.py:31
  115.6 7.8 %collective-permute-start = (bf16[1072,128]{1,0:T(8,128)(2,1)}, bf16[1072,128]{1,0:T(8,128)(2,1)S(1)}, u32[]{:S(2)}, u32[]{:S(2)}) collective-permute-start(bf16[1072,128]{1,0:T(8,128)(2,1)} %get-tuple-element.24), channel_id=1, source_target_pairs={{0,0},{1,8},{2,2},{3,10},{4,4},{5,12},{6,6},{7,14},{8,1},{9,9},{10... | collective-permute-start | bytes 823304 | tf_op jit(solution)/shard_map/ppermute | solution.py:31
  117.2 54.7 %collective-permute-start.1 = (bf16[1072,128]{1,0:T(8,128)(2,1)}, bf16[1072,128]{1,0:T(8,128)(2,1)S(1)}, u32[]{:S(2)}, u32[]{:S(2)}) collective-permute-start(bf16[1072,128]{1,0:T(8,128)(2,1)} %get-tuple-element.25), channel_id=1, source_target_pairs={{0,1},{1,9},{2,3},{3,11},{4,5},{5,13},{6,7},{7,15},{8,0},{9,8},{10... | collective-permute-start | bytes 823304 | tf_op jit(solution)/shard_map/ppermute | solution.py:31
  121.0 70.3 %collective-permute-start.17 = (bf16[128,2,1024]{2,1,0:T(2,128)(2,1)}, bf16[128,2,1024]{2,1,0:T(2,128)(2,1)S(1)}, u32[]{:S(2)}, u32[]{:S(2)}) collective-permute-start(bf16[128,2,1024]{2,1,0:T(2,128)(2,1)} %get-tuple-element.38), channel_id=1, source_target_pairs={{0,1},{1,2},{2,3},{3,4},{4,5},{5,6},{6,7},{7,8},{8,9},{9,10},{10,1... | collective-permute-start | bytes 1572872 | tf_op jit(solution)/shard_map/ppermute | solution.py:31
  121.1 71.7 %collective-permute-start.18 = (bf16[128,2,1024]{2,1,0:T(2,128)(2,1)}, bf16[128,2,1024]{2,1,0:T(2,128)(2,1)S(1)}, u32[]{:S(2)}, u32[]{:S(2)}) collective-permute-start(bf16[128,2,1024]{2,1,0:T(2,128)(2,1)} %get-tuple-element.39), channel_id=1, source_target_pairs={{0,2},{1,3},{2,4},{3,5},{4,6},{5,7},{6,8},{7,9},{8,10},{9,11},{10,... | collective-permute-start | bytes 1572872 | tf_op jit(solution)/shard_map/ppermute | solution.py:31
  123.4 48.5 %copy-start.10 = (bf16[1072,128]{1,0:T(8,128)(2,1)}, bf16[1072,128]{1,0:T(8,128)(2,1)S(1)}, u32[]{:S(2)}) copy-start(bf16[1072,128]{1,0:T(8,128)(2,1)S(1)} %collective-permute-done.refs_0_) | copy-start | bytes 823300
  123.4 69.4 %collective-permute-start.19 = (bf16[128,2,1024]{2,1,0:T(2,128)(2,1)}, bf16[128,2,1024]{2,1,0:T(2,128)(2,1)S(1)}, u32[]{:S(2)}, u32[]{:S(2)}) collective-permute-start(bf16[128,2,1024]{2,1,0:T(2,128)(2,1)} %get-tuple-element.40), channel_id=1, source_target_pairs={{0,3},{1,4},{2,5},{3,6},{4,7},{5,8},{6,9},{7,10},{8,11},{9,12},{10... | collective-permute-start | bytes 1572872 | tf_op jit(solution)/shard_map/ppermute | solution.py:31
  165.6 28.0 %collective-permute-start.20 = (bf16[128,2,1024]{2,1,0:T(2,128)(2,1)}, bf16[128,2,1024]{2,1,0:T(2,128)(2,1)S(1)}, u32[]{:S(2)}, u32[]{:S(2)}) collective-permute-start(bf16[128,2,1024]{2,1,0:T(2,128)(2,1)} %get-tuple-element.41), channel_id=1, source_target_pairs={{0,4},{1,5},{2,6},{3,7},{4,8},{5,9},{6,10},{7,11},{8,12},{9,13},{1... | collective-permute-start | bytes 1572872 | tf_op jit(solution)/shard_map/ppermute | solution.py:31
  171.9 26.6 %collective-permute-start.11 = (bf16[64,4096]{1,0:T(8,128)(2,1)}, bf16[64,4096]{1,0:T(8,128)(2,1)}, u32[]{:S(2)}, u32[]{:S(2)}) collective-permute-start(bf16[64,4096]{1,0:T(8,128)(2,1)} %get-tuple-element.34), channel_id=1, source_target_pairs={{0,2},{1,3},{2,0},{3,1},{4,6},{5,7},{6,4},{7,5},{8,10},{9,11},{10,... | collective-permute-start | bytes 1572872 | tf_op jit(solution)/shard_map/ppermute | solution.py:31
  191.3 15.2 %collective-permute-start.3 = (bf16[64,4096]{1,0:T(8,128)(2,1)}, bf16[64,4096]{1,0:T(8,128)(2,1)}, u32[]{:S(2)}, u32[]{:S(2)}) collective-permute-start(bf16[64,4096]{1,0:T(8,128)(2,1)} %get-tuple-element.27), channel_id=1, source_target_pairs={{0,2},{1,3},{2,0},{3,1},{4,6},{5,7},{6,4},{7,5},{8,10},{9,11},{10,... | collective-permute-start | bytes 1572872 | tf_op jit(solution)/shard_map/ppermute | solution.py:31
  192.8 15.2 %collective-permute-start.6 = (bf16[64,4096]{1,0:T(8,128)(2,1)}, bf16[64,4096]{1,0:T(8,128)(2,1)}, u32[]{:S(2)}, u32[]{:S(2)}) collective-permute-start(bf16[64,4096]{1,0:T(8,128)(2,1)} %get-tuple-element.30), channel_id=1, source_target_pairs={{0,4},{1,5},{2,6},{3,7},{4,0},{5,1},{6,2},{7,3},{8,12},{9,13},{10,... | collective-permute-start | bytes 1572872 | tf_op jit(solution)/shard_map/ppermute | solution.py:31
  192.8 24.9 %collective-permute-start.14 = (bf16[64,4096]{1,0:T(8,128)(2,1)}, bf16[64,4096]{1,0:T(8,128)(2,1)}, u32[]{:S(2)}, u32[]{:S(2)}) collective-permute-start(bf16[64,4096]{1,0:T(8,128)(2,1)} %get-tuple-element.37.refs_4_), channel_id=1, source_target_pairs={{0,2},{1,3},{2,0},{3,1},{4,6},{5,7},{6,4},{7,5},{8,10},{9,11},{10,... | collective-permute-start | bytes 1572872 | tf_op jit(solution)/shard_map/ppermute | solution.py:31
  199.8 19.3 %collective-permute-start.12 = (bf16[32,4096]{1,0:T(8,128)(2,1)S(1)}, bf16[32,4096]{1,0:T(8,128)(2,1)S(1)}, u32[]{:S(2)}, u32[]{:S(2)}) collective-permute-start(bf16[32,4096]{1,0:T(8,128)(2,1)S(1)} %slice.121), channel_id=1, source_target_pairs={{0,4},{1,5},{2,6},{3,7},{4,0},{5,1},{6,2},{7,3},{8,12},{9,13},{10,... | collective-permute-start | bytes 786440 | tf_op jit(solution)/shard_map/ppermute | solution.py:31
  207.6 15.8 %collective-permute-start.4 = (bf16[32,4096]{1,0:T(8,128)(2,1)S(1)}, bf16[32,4096]{1,0:T(8,128)(2,1)S(1)}, u32[]{:S(2)}, u32[]{:S(2)}) collective-permute-start(bf16[32,4096]{1,0:T(8,128)(2,1)S(1)} %slice.123), channel_id=1, source_target_pairs={{0,4},{1,5},{2,6},{3,7},{4,0},{5,1},{6,2},{7,3},{8,12},{9,13},{10,... | collective-permute-start | bytes 786440 | tf_op jit(solution)/shard_map/ppermute | solution.py:31
  209.1 14.5 %collective-permute-start.7 = (bf16[32,4096]{1,0:T(8,128)(2,1)S(1)}, bf16[32,4096]{1,0:T(8,128)(2,1)S(1)}, u32[]{:S(2)}, u32[]{:S(2)}) collective-permute-start(bf16[32,4096]{1,0:T(8,128)(2,1)S(1)} %slice.122), channel_id=1, source_target_pairs={{0,2},{1,3},{2,0},{3,1},{4,6},{5,7},{6,4},{7,5},{8,10},{9,11},{10,... | collective-permute-start | bytes 786440 | tf_op jit(solution)/shard_map/ppermute | solution.py:31
  218.9 9.2 %collective-permute-start.15 = (bf16[32,4096]{1,0:T(8,128)(2,1)S(1)}, bf16[32,4096]{1,0:T(8,128)(2,1)S(1)}, u32[]{:S(2)}, u32[]{:S(2)}) collective-permute-start(bf16[32,4096]{1,0:T(8,128)(2,1)S(1)} %slice.120), channel_id=1, source_target_pairs={{0,4},{1,5},{2,6},{3,7},{4,0},{5,1},{6,2},{7,3},{8,12},{9,13},{10,... | collective-permute-start | bytes 786440 | tf_op jit(solution)/shard_map/ppermute | solution.py:31
  219.2 18.3 %collective-permute-start.13 = (bf16[16,4096]{1,0:T(8,128)(2,1)S(1)}, bf16[16,4096]{1,0:T(8,128)(2,1)S(1)}, u32[]{:S(2)}, u32[]{:S(2)}) collective-permute-start(bf16[16,4096]{1,0:T(8,128)(2,1)S(1)} %slice.125), channel_id=1, source_target_pairs={{0,8},{1,9},{2,10},{3,11},{4,12},{5,13},{6,14},{7,15},{8,0},{9,1},... | collective-permute-start | bytes 393224 | tf_op jit(solution)/shard_map/ppermute | solution.py:31
  223.5 16.8 %collective-permute-start.5 = (bf16[16,4096]{1,0:T(8,128)(2,1)S(1)}, bf16[16,4096]{1,0:T(8,128)(2,1)S(1)}, u32[]{:S(2)}, u32[]{:S(2)}) collective-permute-start(bf16[16,4096]{1,0:T(8,128)(2,1)S(1)} %slice.127), channel_id=1, source_target_pairs={{0,8},{1,9},{2,10},{3,11},{4,12},{5,13},{6,14},{7,15},{8,0},{9,1},... | collective-permute-start | bytes 393224 | tf_op jit(solution)/shard_map/ppermute | solution.py:31
  223.7 19.1 %collective-permute-start.8 = (bf16[16,4096]{1,0:T(8,128)(2,1)S(1)}, bf16[16,4096]{1,0:T(8,128)(2,1)S(1)}, u32[]{:S(2)}, u32[]{:S(2)}) collective-permute-start(bf16[16,4096]{1,0:T(8,128)(2,1)S(1)} %slice.126), channel_id=1, source_target_pairs={{0,8},{1,9},{2,10},{3,11},{4,12},{5,13},{6,14},{7,15},{8,0},{9,1},... | collective-permute-start | bytes 393224 | tf_op jit(solution)/shard_map/ppermute | solution.py:31
  228.1 16.1 %collective-permute-start.16 = (bf16[16,4096]{1,0:T(8,128)(2,1)S(1)}, bf16[16,4096]{1,0:T(8,128)(2,1)S(1)}, u32[]{:S(2)}, u32[]{:S(2)}) collective-permute-start(bf16[16,4096]{1,0:T(8,128)(2,1)S(1)} %slice.124), channel_id=1, source_target_pairs={{0,8},{1,9},{2,10},{3,11},{4,12},{5,13},{6,14},{7,15},{8,0},{9,1},... | collective-permute-start | bytes 393224 | tf_op jit(solution)/shard_map/ppermute | solution.py:31
  (13 other events, 188.2 us)
where the time goes:
time: 246 us; the launch traced here: 245 us
  Pallas kernels  99.9 us (41%)
  starting transfers between devices  77.5 us (32%)
  waiting for transfers between devices  55.4 us (23%)
  other arithmetic  8.46 us (3%)
  local copies, waits for them, and re-layouts  2.85 us (1%)
    ppermute x21, starting transfers between devices, permute_to(): return lax.ppermute(x, 'pages', [(i, target(i)) for i in range(n)])  67.9 us
    pallas_call x3, Pallas kernels, attend(): pl.pallas_call(functools.partial(attend_kernel, first_slot=first_slot, fi...  57.2 us
    all_to_all x2, waiting for transfers between devices, exchange(): lax.all_to_all(x, 'pages', 0, 0, axis_index_groups=groups, tiled=True)  28.4 us
    ppermute x21, waiting for transfers between devices, permute_to(): return lax.ppermute(x, 'pages', [(i, target(i)) for i in range(n)])  26.9 us
    pallas_call x4, Pallas kernels, project(): pl.pallas_call(functools.partial(project_kernel, n_parts=len(parts), n_ws...  24.9 us
    all_to_all x2, starting transfers between devices, exchange(): lax.all_to_all(x, 'pages', 0, 0, axis_index_groups=groups, tiled=True)  9.59 us
    pallas_call x2, Pallas kernels, split_heads(): pl.pallas_call(functools.partial(split_heads_kernel, first=first, count=c...  6.32 us
  transfers between devices with their start and end apart: 23, of which 8 were waited for; matrix products, arithmetic and copies ran while one was open for 3% of the time, Pallas kernels for 39%

commit v1 on v0

--- a/solution.py
+++ b/solution.py
@@ -21,7 +21,7 @@
 
 WIDE = 16
 NARROW = 8
-FIRST_SLOTS = 5
+FIRST_SLOTS = 3
 COLUMN_PARTS = 2
 
 ANY = pl.BlockSpec(memory_space=pl.ANY)
@@ -243,7 +243,11 @@
     n_in = 0 if first else 2
     carried = refs[:n_in]
     outs = refs[n_in : n_in + (ways if last else 2)]
-    k_s, v_s, acc_s, m_s, ids_s, order, pages, ids, counts, sem = refs[n_in + len(outs) :]
+    k_s, v_s, *sums, ids_s, order, rest, pages, ids, counts, sem = refs[n_in + len(outs) :]
+    if last:
+        acc_s, m_s = sums
+    else:
+        acc_s, m_s = outs[0].at[0], outs[1].at[0]
     step = pl.program_id(0)
     sources = x_ref.shape[0]
     src_slots = x_ref.shape[1] // (2 * PAGE_TOK)
@@ -268,28 +272,23 @@
         def fully(page):
             return (page >= 0) & (page * PAGE_TOK + (PAGE_TOK - 1) <= lowest)
 
-        def put_full(i, count):
+        n_full = jnp.int32(0)
+        n_rest = jnp.int32(0)
+        for i in range(n_slots):
             page = ids[i // src_slots, first_slot + i % src_slots]
             pages[i] = page
             yes = fully(page)
-
-            @pl.when(yes)
-            def _():
-                order[count] = i
-
-            return count + yes.astype(jnp.int32)
-
-        def put_rest(i, count):
-            yes = (pages[i] >= 0) & jnp.logical_not(fully(pages[i]))
-
-            @pl.when(yes)
-            def _():
-                order[count] = i
-
-            return count + yes.astype(jnp.int32)
-
-        n_full = lax.fori_loop(0, n_slots, put_full, 0)
-        n_live = lax.fori_loop(0, n_slots, put_rest, n_full)
+            order[n_full] = i
+            rest[n_rest] = i
+            n_full += yes.astype(jnp.int32)
+            n_rest += ((page >= 0) & jnp.logical_not(yes)).astype(jnp.int32)
+
+        def append(i, carry):
+            order[n_full + i] = rest[i]
+            return carry
+
+        lax.fori_loop(0, n_rest, append, 0)
+        n_live = n_full + n_rest
         counts[0] = n_full
         counts[1] = n_live
 
@@ -418,10 +417,7 @@
     lax.fori_loop(0, n_open, narrow, 0)
     lax.fori_loop(0, n_masked, masked, 0)
 
-    if not last:
-        outs[0][0] = acc_s[...]
-        outs[1][0] = m_s[...]
-    else:
+    if last:
         row = lax.broadcasted_iota(jnp.int32, (tok, HEAD_DIM), 0)
         col = lax.broadcasted_iota(jnp.int32, (tok, HEAD_DIM), 1)
         eye = row == col
@@ -476,6 +472,12 @@
             pl.BlockSpec((1, total, HEAD_DIM), at),
         )
     extra = ()
+    sums = ()
+    if last:
+        sums = (
+            pltpu.VMEM((total, 2 * HEAD_DIM), jnp.float32),
+            pltpu.VMEM((total, HEAD_DIM), jnp.float32),
+        )
     if not first:
         extra = tuple(carried)
         in_specs += [
@@ -504,10 +506,10 @@
             scratch_shapes=[
                 pltpu.VMEM((n_slots * PAGE_TOK, HEAD_DIM), jnp.bfloat16),
                 pltpu.VMEM((n_slots * PAGE_TOK, 2 * HEAD_DIM), jnp.bfloat16),
-                pltpu.VMEM((total, 2 * HEAD_DIM), jnp.float32),
-                pltpu.VMEM((total, HEAD_DIM), jnp.float32),
+                *sums,
                 pltpu.VMEM((sources, HEAD_DIM), jnp.int32),
-                pltpu.SMEM((n_slots,), jnp.int32),
+                pltpu.SMEM((n_slots + 1,), jnp.int32),
+                pltpu.SMEM((n_slots + 1,), jnp.int32),
                 pltpu.SMEM((n_slots,), jnp.int32),
                 pltpu.SMEM((sources, HEAD_DIM), jnp.int32),
                 pltpu.SMEM((2,), jnp.int32),
@@ -665,7 +667,7 @@
     for b in range(2):
         merged = partial[b]
         for c in range(COLUMN_PARTS):
-            y_first = (b, c) != (0, 1)
+            y_first = (b, c) != (1, 1)
             keep, send, *a = project(merged, ws, tok, c, y_first)
             if a:
                 merged = a

time: 246 us -> 235 us (0.955)
  the two profiles are of different devices: /device:TPU:0 before, /device:TPU:2 now
where the time goes in v1:
time: 235 us; the launch traced here: 234 us
  Pallas kernels  98.6 us (42%)
  starting transfers between devices  70.5 us (30%)
  waiting for transfers between devices  48.8 us (21%)
  other arithmetic  8.48 us (4%)
  local copies, waits for them, and re-layouts  6.11 us (3%)
    ppermute x21, starting transfers between devices, permute_to(): return lax.ppermute(x, 'pages', [(i, target(i)) for i in range(n)])  63.1 us
    pallas_call x3, Pallas kernels, attend(): pl.pallas_call(functools.partial(attend_kernel, first_slot=first_slot, fi...  55.2 us
    ppermute x21, waiting for transfers between devices, permute_to(): return lax.ppermute(x, 'pages', [(i, target(i)) for i in range(n)])  31.2 us
    pallas_call x4, Pallas kernels, project(): pl.pallas_call(functools.partial(project_kernel, n_parts=len(parts), n_ws...  25 us
    all_to_all x2, waiting for transfers between devices, exchange(): lax.all_to_all(x, 'pages', 0, 0, axis_index_groups=groups, tiled=True)  17.5 us
    all_to_all x2, starting transfers between devices, exchange(): lax.all_to_all(x, 'pages', 0, 0, axis_index_groups=groups, tiled=True)  7.45 us
    pallas_call x2, Pallas kernels, split_heads(): pl.pallas_call(functools.partial(split_heads_kernel, first=first, count=c...  6.36 us
    add x8, other arithmetic, local(): total = keep + got.astype(jnp.float32)  4.86 us
  transfers between devices with their start and end apart: 23, of which 9 were waited for; matrix products, arithmetic and copies ran while one was open for 3% of the time, Pallas kernels for 41%

profile of v1, /device:TPU:2, one launch (start us, length us, event | category | flops | bytes accessed | tf_op | source)
XLA Modules:
  0.0 233.5 jit_solution(11594691792971403245)
XLA Ops:
  2.0 2.8 %split_heads.3 = bf16[8,392,2,128]{3,2,1,0:T(2,128)(2,1)} custom-call(bf16[8,128,2,1024]{3,2,1,0:T(2,128)(2,1)} %kv_ref.7, bf16[8,2,128]{2,1,0:T(2,128)(2,1)} %broadcast_in_dim.2.ids_ref), custom_call_target="tpu_custom_call" | custom-call | tf_op jit(solution)/shard_map/split_heads/pallas_call | solution.py:79
  4.8 3.8 %all-to-all-start.1 = ((bf16[8,392,2,128]{3,2,1,0:T(2,128)(2,1)}), bf16[8,392,2,128]{3,2,1,0:T(2,128)(2,1)S(1)}, u32[]{:S(2)}, u32[]{:S(2)}) async-start(bf16[8,392,2,128]{3,2,1,0:T(2,128)(2,1)} %split_heads.3), calls=%async_computation.1 | async-start | bytes 3211264 | tf_op jit(solution)/shard_map/all_to_all | solution.py:630
  9.1 3.5 %split_heads.2 = bf16[8,648,2,128]{3,2,1,0:T(2,128)(2,1)} custom-call(bf16[8,128,2,1024]{3,2,1,0:T(2,128)(2,1)} %kv_ref.7, bf16[8,2,128]{2,1,0:T(2,128)(2,1)} %broadcast_in_dim.2.ids_ref), custom_call_target="tpu_custom_call" | custom-call | tf_op jit(solution)/shard_map/split_heads/pallas_call | solution.py:79
  12.7 16.4 %all-to-all-done.1 = bf16[8,392,2,128]{3,2,1,0:T(2,128)(2,1)S(1)} async-done(((bf16[8,392,2,128]{3,2,1,0:T(2,128)(2,1)}), bf16[8,392,2,128]{3,2,1,0:T(2,128)(2,1)S(1)}, u32[]{:S(2)}, u32[]{:S(2)}) %all-to-all-start.1) | async-done | bytes 1605664 | tf_op jit(solution)/shard_map/all_to_all | solution.py:630
  30.2 3.6 %all-to-all-start = ((bf16[8,648,2,128]{3,2,1,0:T(2,128)(2,1)}), bf16[8,648,2,128]{3,2,1,0:T(2,128)(2,1)S(1)}, u32[]{:S(2)}, u32[]{:S(2)}) async-start(bf16[8,648,2,128]{3,2,1,0:T(2,128)(2,1)} %split_heads.2), calls=%async_computation | async-start | bytes 5308416 | tf_op jit(solution)/shard_map/all_to_all | solution.py:630
  36.4 4.3 %query_rows.1.q_ref = bf16[4,1024,128]{2,1,0:T(8,128)(2,1)} custom-call(s32[4]{0:T(128)} %pad_add_fusion.place, bf16[2,256,8192]{2,1,0:T(8,128)(2,1)} %q_ref.1), custom_call_target="tpu_custom_call" | custom-call | tf_op jit(solution)/shard_map/query_rows/pallas_call | solution.py:219
  40.7 23.6 %attend_first.1 = (f32[4,1024,256]{2,1,0:T(8,128)}, f32[4,1024,128]{2,1,0:T(8,128)}) custom-call(s32[4]{0:T(128)} %pad_add_fusion.place, bf16[8,784,128]{2,1,0:T(8,128)(2,1)} %bitcast.14, bf16[4,1024,128]{2,1,0:T(8,128)(2,1)} %query_rows.1.q_ref), custom_call_target="tpu_custom_call" | custom-call | flops 12884901888 | bytes 1605632 | tf_op jit(solution)/shard_map/attend_first/pallas_call | solution.py:488
  67.0 15.8 %attend_last.3 = (bf16[1072,128]{1,0:T(8,128)(2,1)}, bf16[1072,128]{1,0:T(8,128)(2,1)}) custom-call(s32[4]{0:T(128)} %pad_add_fusion.place, bf16[8,1296,128]{2,1,0:T(8,128)(2,1)} %bitcast.12, bf16[4,1024,128]{2,1,0:T(8,128)(2,1)} %query_rows.1.q_ref, f32[4,1024,256]{2,1,0:T(8,128)} %get-tuple-element.22.refs_0_, f32[4,1024,128]{2,1,0:T(8,128)} %get-tuple-element.23.refs_1_), custom_call_target="tpu_custom_call" | custom-call | flops 10737418240 | bytes 2654208 | tf_op jit(solution)/shard_map/attend_last/pallas_call | solution.py:488
  84.4 3.1 %collective-permute-start.10 = (bf16[1072,128]{1,0:T(8,128)(2,1)}, bf16[1072,128]{1,0:T(8,128)(2,1)S(1)}, u32[]{:S(2)}, u32[]{:S(2)}) collective-permute-start(bf16[1072,128]{1,0:T(8,128)(2,1)} %get-tuple-element.32), channel_id=1, source_target_pairs={{0,1},{1,9},{2,3},{3,11},{4,5},{5,13},{6,7},{7,15},{8,0},{9,8},{10... | collective-permute-start | bytes 823304 | tf_op jit(solution)/shard_map/ppermute | solution.py:31
  87.5 15.8 %attend_last.2 = (bf16[1072,128]{1,0:T(8,128)(2,1)}, bf16[1072,128]{1,0:T(8,128)(2,1)}) custom-call(s32[4]{0:T(128)} %pad_add_fusion.place, bf16[8,1296,128]{2,1,0:T(8,128)(2,1)} %bitcast.13, bf16[4,1024,128]{2,1,0:T(8,128)(2,1)} %query_rows.1.q_ref, f32[4,1024,256]{2,1,0:T(8,128)} %get-tuple-element.22.refs_0_, f32[4,1024,128]{2,1,0:T(8,128)} %get-tuple-element.23.refs_1_), custom_call_target="tpu_custom_call" | custom-call | flops 10737418240 | bytes 2654208 | tf_op jit(solution)/shard_map/attend_last/pallas_call | solution.py:488
  105.4 3.7 %outgoing_pages.1 = (bf16[128,2,1024]{2,1,0:T(2,128)(2,1)}, bf16[128,2,1024]{2,1,0:T(2,128)(2,1)}, bf16[128,2,1024]{2,1,0:T(2,128)(2,1)}, bf16[128,2,1024]{2,1,0:T(2,128)(2,1)}) custom-call(s32[4]{0:T(128)} %bitcast.15, bf16[8,128,2,1024]{3,2,1,0:T(2,128)(2,1)} %kv_ref.7), custom_call_target="tpu_custom_call" | custom-call | tf_op jit(solution)/shard_map/outgoing_pages/pallas_call | solution.py:116
  110.1 42.9 %collective-permute-start.19 = (bf16[128,2,1024]{2,1,0:T(2,128)(2,1)}, bf16[128,2,1024]{2,1,0:T(2,128)(2,1)S(1)}, u32[]{:S(2)}, u32[]{:S(2)}) collective-permute-start(bf16[128,2,1024]{2,1,0:T(2,128)(2,1)} %get-tuple-element.40), channel_id=1, source_target_pairs={{0,3},{1,4},{2,5},{3,6},{4,7},{5,8},{6,9},{7,10},{8,11},{9,12},{10... | collective-permute-start | bytes 1572872 | tf_op jit(solution)/shard_map/ppermute | solution.py:31
  153.0 6.3 %project.6 = (f32[64,4096]{1,0:T(8,128)}, bf16[64,4096]{1,0:T(8,128)(2,1)}, bf16[128,1024]{1,0:T(8,128)(2,1)}) custom-call(bf16[1072,128]{1,0:T(8,128)(2,1)} %copy-done.10, bf16[1072,128]{1,0:T(8,128)(2,1)} %copy-done.12, bf16[512,8192]{1,0:T(8,128)(2,1)} %refs_1_.3, bf16[512,8192]{1,0:T(8,128)(2,1)} %collective-permute-done.2.refs_3_.refs_2_), custom_call_target="tpu_custom_call" | custom-call | flops 1073741824 | bytes 8388608 | tf_op jit(solution)/shard_map/project/pallas_call | solution.py:598
  160.0 6.3 %project.4 = (f32[64,4096]{1,0:T(8,128)}, bf16[64,4096]{1,0:T(8,128)(2,1)}, bf16[128,1024]{1,0:T(8,128)(2,1)}) custom-call(bf16[1072,128]{1,0:T(8,128)(2,1)} %copy-done.11, bf16[1072,128]{1,0:T(8,128)(2,1)} %copy-done.13, bf16[512,8192]{1,0:T(8,128)(2,1)} %refs_1_.3, bf16[512,8192]{1,0:T(8,128)(2,1)} %collective-permute-done.2.refs_3_.refs_2_), custom_call_target="tpu_custom_call" | custom-call | flops 1073741824 | bytes 8388608 | tf_op jit(solution)/shard_map/project/pallas_call | solution.py:598
  166.3 6.2 %project.5 = (f32[64,4096]{1,0:T(8,128)}, bf16[64,4096]{1,0:T(8,128)(2,1)}) custom-call(bf16[128,1024]{1,0:T(8,128)(2,1)} %get-tuple-element.28.refs_0_, bf16[512,8192]{1,0:T(8,128)(2,1)} %refs_1_.3, bf16[512,8192]{1,0:T(8,128)(2,1)} %collective-permute-done.2.refs_3_.refs_2_), custom_call_target="tpu_custom_call" | custom-call | flops 1073741824 | bytes 8388608 | tf_op jit(solution)/shard_map/project/pallas_call | solution.py:598
  172.5 6.2 %project.7 = (f32[64,4096]{1,0:T(8,128)}, bf16[64,4096]{1,0:T(8,128)(2,1)}) custom-call(bf16[128,1024]{1,0:T(8,128)(2,1)} %get-tuple-element.35.refs_0_, bf16[512,8192]{1,0:T(8,128)(2,1)} %refs_1_.3, bf16[512,8192]{1,0:T(8,128)(2,1)} %collective-permute-done.2.refs_3_.refs_2_), custom_call_target="tpu_custom_call" | custom-call | flops 1073741824 | bytes 8388608 | tf_op jit(solution)/shard_map/project/pallas_call | solution.py:598
  182.5 4.0 %arrange_pages.1 = bf16[8,128,2,1024]{3,2,1,0:T(2,128)(2,1)} custom-call(s32[8]{0:T(128)} %page_after.1, s32[4]{0:T(128)} %bitcast.16, bf16[8,128,2,1024]{3,2,1,0:T(2,128)(2,1)} %kv_ref.7, bf16[128,2,1024]{2,1,0:T(2,128)(2,1)} %copy-done.6, bf16[128,2,1024]{2,1,0:T(2,128)(2,1)} %copy-done.7, bf16[128,2,1024]{2,1,0:T(2,128)(2,1)} %copy-done.8, ...), custom_call_target="tpu_custom_call" | custom-call | tf_op jit(solution)/shard_map/arrange_pages/pallas_call | solution.py:174
  189.0 4.9 %collective-permute-done.3 = bf16[64,4096]{1,0:T(8,128)(2,1)} collective-permute-done((bf16[64,4096]{1,0:T(8,128)(2,1)}, bf16[64,4096]{1,0:T(8,128)(2,1)}, u32[]{:S(2)}, u32[]{:S(2)}) %collective-permute-start.3) | collective-permute-done | bytes 524320 | tf_op jit(solution)/shard_map/ppermute | solution.py:31
  195.4 8.5 %collective-permute-done.6 = bf16[64,4096]{1,0:T(8,128)(2,1)} collective-permute-done((bf16[64,4096]{1,0:T(8,128)(2,1)}, bf16[64,4096]{1,0:T(8,128)(2,1)}, u32[]{:S(2)}, u32[]{:S(2)}) %collective-permute-start.6) | collective-permute-done | bytes 524320 | tf_op jit(solution)/shard_map/ppermute | solution.py:31
  207.6 3.7 %collective-permute-start.13 = (bf16[16,4096]{1,0:T(8,128)(2,1)S(1)}, bf16[16,4096]{1,0:T(8,128)(2,1)S(1)}, u32[]{:S(2)}, u32[]{:S(2)}) collective-permute-start(bf16[16,4096]{1,0:T(8,128)(2,1)S(1)} %slice.125), channel_id=1, source_target_pairs={{0,8},{1,9},{2,10},{3,11},{4,12},{5,13},{6,14},{7,15},{8,0},{9,1},... | collective-permute-start | bytes 393224 | tf_op jit(solution)/shard_map/ppermute | solution.py:31
  211.5 3.6 %collective-permute-done.7 = bf16[32,4096]{1,0:T(8,128)(2,1)S(1)} collective-permute-done((bf16[32,4096]{1,0:T(8,128)(2,1)S(1)}, bf16[32,4096]{1,0:T(8,128)(2,1)S(1)}, u32[]{:S(2)}, u32[]{:S(2)}) %collective-permute-start.7) | collective-permute-done | bytes 262176 | tf_op jit(solution)/shard_map/ppermute | solution.py:31
  218.4 7.7 %collective-permute-done.13 = bf16[16,4096]{1,0:T(8,128)(2,1)S(1)} collective-permute-done((bf16[16,4096]{1,0:T(8,128)(2,1)S(1)}, bf16[16,4096]{1,0:T(8,128)(2,1)S(1)}, u32[]{:S(2)}, u32[]{:S(2)}) %collective-permute-start.13) | collective-permute-done | bytes 131104 | tf_op jit(solution)/shard_map/ppermute | solution.py:31
  226.1 2.8 %collective-permute-done.5 = bf16[16,4096]{1,0:T(8,128)(2,1)S(1)} collective-permute-done((bf16[16,4096]{1,0:T(8,128)(2,1)S(1)}, bf16[16,4096]{1,0:T(8,128)(2,1)S(1)}, u32[]{:S(2)}, u32[]{:S(2)}) %collective-permute-start.5) | collective-permute-done | bytes 131104 | tf_op jit(solution)/shard_map/ppermute | solution.py:31
  228.9 2.4 %collective-permute-done.8 = bf16[16,4096]{1,0:T(8,128)(2,1)S(1)} collective-permute-done((bf16[16,4096]{1,0:T(8,128)(2,1)S(1)}, bf16[16,4096]{1,0:T(8,128)(2,1)S(1)}, u32[]{:S(2)}, u32[]{:S(2)}) %collective-permute-start.8) | collective-permute-done | bytes 131104 | tf_op jit(solution)/shard_map/ppermute | solution.py:31
  (91 shorter events, 30.5 us)
Async XLA Ops:
  4.8 24.3 %all-to-all-start.1 = ((bf16[8,392,2,128]{3,2,1,0:T(2,128)(2,1)}), bf16[8,392,2,128]{3,2,1,0:T(2,128)(2,1)S(1)}, u32[]{:S(2)}, u32[]{:S(2)}) async-start(bf16[8,392,2,128]{3,2,1,0:T(2,128)(2,1)} %split_heads.3), calls=%async_computation.1 | async-start | bytes 3211264 | tf_op jit(solution)/shard_map/all_to_all | solution.py:630
  8.6 144.3 %collective-permute-start.2 = (bf16[512,8192]{1,0:T(8,128)(2,1)}, bf16[512,8192]{1,0:T(8,128)(2,1)}, u32[]{:S(2)}, u32[]{:S(2)}) collective-permute-start(bf16[512,8192]{1,0:T(8,128)(2,1)} %refs_1_.3), channel_id=1, source_target_pairs={{0,1},{1,0},{2,3},{3,2},{4,5},{5,4},{6,7},{7,6},{8,9},{9,8},{10,11... | collective-permute-start | bytes 25165832 | tf_op jit(solution)/shard_map/ppermute | solution.py:31
  30.2 35.2 %all-to-all-start = ((bf16[8,648,2,128]{3,2,1,0:T(2,128)(2,1)}), bf16[8,648,2,128]{3,2,1,0:T(2,128)(2,1)S(1)}, u32[]{:S(2)}, u32[]{:S(2)}) async-start(bf16[8,648,2,128]{3,2,1,0:T(2,128)(2,1)} %split_heads.2), calls=%async_computation | async-start | bytes 5308416 | tf_op jit(solution)/shard_map/all_to_all | solution.py:630
  82.8 26.3 %collective-permute-start.9 = (bf16[1072,128]{1,0:T(8,128)(2,1)}, bf16[1072,128]{1,0:T(8,128)(2,1)S(1)}, u32[]{:S(2)}, u32[]{:S(2)}) collective-permute-start(bf16[1072,128]{1,0:T(8,128)(2,1)} %get-tuple-element.31), channel_id=1, source_target_pairs={{0,0},{1,8},{2,2},{3,10},{4,4},{5,12},{6,6},{7,14},{8,1},{9,9},{10... | collective-permute-start | bytes 823304 | tf_op jit(solution)/shard_map/ppermute | solution.py:31
  84.4 24.7 %collective-permute-start.10 = (bf16[1072,128]{1,0:T(8,128)(2,1)}, bf16[1072,128]{1,0:T(8,128)(2,1)S(1)}, u32[]{:S(2)}, u32[]{:S(2)}) collective-permute-start(bf16[1072,128]{1,0:T(8,128)(2,1)} %get-tuple-element.32), channel_id=1, source_target_pairs={{0,1},{1,9},{2,3},{3,11},{4,5},{5,13},{6,7},{7,15},{8,0},{9,8},{10... | collective-permute-start | bytes 823304 | tf_op jit(solution)/shard_map/ppermute | solution.py:31
  103.3 6.8 %collective-permute-start = (bf16[1072,128]{1,0:T(8,128)(2,1)}, bf16[1072,128]{1,0:T(8,128)(2,1)S(1)}, u32[]{:S(2)}, u32[]{:S(2)}) collective-permute-start(bf16[1072,128]{1,0:T(8,128)(2,1)} %get-tuple-element.24), channel_id=1, source_target_pairs={{0,0},{1,8},{2,2},{3,10},{4,4},{5,12},{6,6},{7,14},{8,1},{9,9},{10... | collective-permute-start | bytes 823304 | tf_op jit(solution)/shard_map/ppermute | solution.py:31
  104.9 54.3 %collective-permute-start.1 = (bf16[1072,128]{1,0:T(8,128)(2,1)}, bf16[1072,128]{1,0:T(8,128)(2,1)S(1)}, u32[]{:S(2)}, u32[]{:S(2)}) collective-permute-start(bf16[1072,128]{1,0:T(8,128)(2,1)} %get-tuple-element.25), channel_id=1, source_target_pairs={{0,1},{1,9},{2,3},{3,11},{4,5},{5,13},{6,7},{7,15},{8,0},{9,8},{10... | collective-permute-start | bytes 823304 | tf_op jit(solution)/shard_map/ppermute | solution.py:31
  109.1 69.6 %collective-permute-start.17 = (bf16[128,2,1024]{2,1,0:T(2,128)(2,1)}, bf16[128,2,1024]{2,1,0:T(2,128)(2,1)S(1)}, u32[]{:S(2)}, u32[]{:S(2)}) collective-permute-start(bf16[128,2,1024]{2,1,0:T(2,128)(2,1)} %get-tuple-element.38), channel_id=1, source_target_pairs={{0,1},{1,2},{2,3},{3,4},{4,5},{5,6},{6,7},{7,8},{8,9},{9,10},{10,1... | collective-permute-start | bytes 1572872 | tf_op jit(solution)/shard_map/ppermute | solution.py:31
  109.2 71.0 %collective-permute-start.18 = (bf16[128,2,1024]{2,1,0:T(2,128)(2,1)}, bf16[128,2,1024]{2,1,0:T(2,128)(2,1)S(1)}, u32[]{:S(2)}, u32[]{:S(2)}) collective-permute-start(bf16[128,2,1024]{2,1,0:T(2,128)(2,1)} %get-tuple-element.39), channel_id=1, source_target_pairs={{0,2},{1,3},{2,4},{3,5},{4,6},{5,7},{6,8},{7,9},{8,10},{9,11},{10,... | collective-permute-start | bytes 1572872 | tf_op jit(solution)/shard_map/ppermute | solution.py:31
  110.1 49.2 %copy-start.11 = (bf16[1072,128]{1,0:T(8,128)(2,1)}, bf16[1072,128]{1,0:T(8,128)(2,1)S(1)}, u32[]{:S(2)}) copy-start(bf16[1072,128]{1,0:T(8,128)(2,1)S(1)} %collective-permute-done.refs_0_) | copy-start | bytes 823300
  110.1 70.7 %collective-permute-start.19 = (bf16[128,2,1024]{2,1,0:T(2,128)(2,1)}, bf16[128,2,1024]{2,1,0:T(2,128)(2,1)S(1)}, u32[]{:S(2)}, u32[]{:S(2)}) collective-permute-start(bf16[128,2,1024]{2,1,0:T(2,128)(2,1)} %get-tuple-element.40), channel_id=1, source_target_pairs={{0,3},{1,4},{2,5},{3,6},{4,7},{5,8},{6,9},{7,10},{8,11},{9,12},{10... | collective-permute-start | bytes 1572872 | tf_op jit(solution)/shard_map/ppermute | solution.py:31
  153.0 28.1 %collective-permute-start.20 = (bf16[128,2,1024]{2,1,0:T(2,128)(2,1)}, bf16[128,2,1024]{2,1,0:T(2,128)(2,1)S(1)}, u32[]{:S(2)}, u32[]{:S(2)}) collective-permute-start(bf16[128,2,1024]{2,1,0:T(2,128)(2,1)} %get-tuple-element.41), channel_id=1, source_target_pairs={{0,4},{1,5},{2,6},{3,7},{4,8},{5,9},{6,10},{7,11},{8,12},{9,13},{1... | collective-permute-start | bytes 1572872 | tf_op jit(solution)/shard_map/ppermute | solution.py:31
  159.3 27.2 %collective-permute-start.11 = (bf16[64,4096]{1,0:T(8,128)(2,1)}, bf16[64,4096]{1,0:T(8,128)(2,1)}, u32[]{:S(2)}, u32[]{:S(2)}) collective-permute-start(bf16[64,4096]{1,0:T(8,128)(2,1)} %get-tuple-element.34), channel_id=1, source_target_pairs={{0,2},{1,3},{2,0},{3,1},{4,6},{5,7},{6,4},{7,5},{8,10},{9,11},{10,... | collective-permute-start | bytes 1572872 | tf_op jit(solution)/shard_map/ppermute | solution.py:31
  178.7 15.2 %collective-permute-start.3 = (bf16[64,4096]{1,0:T(8,128)(2,1)}, bf16[64,4096]{1,0:T(8,128)(2,1)}, u32[]{:S(2)}, u32[]{:S(2)}) collective-permute-start(bf16[64,4096]{1,0:T(8,128)(2,1)} %get-tuple-element.27), channel_id=1, source_target_pairs={{0,2},{1,3},{2,0},{3,1},{4,6},{5,7},{6,4},{7,5},{8,10},{9,11},{10,... | collective-permute-start | bytes 1572872 | tf_op jit(solution)/shard_map/ppermute | solution.py:31
  180.2 23.7 %collective-permute-start.6 = (bf16[64,4096]{1,0:T(8,128)(2,1)}, bf16[64,4096]{1,0:T(8,128)(2,1)}, u32[]{:S(2)}, u32[]{:S(2)}) collective-permute-start(bf16[64,4096]{1,0:T(8,128)(2,1)} %get-tuple-element.30), channel_id=1, source_target_pairs={{0,2},{1,3},{2,0},{3,1},{4,6},{5,7},{6,4},{7,5},{8,10},{9,11},{10,... | collective-permute-start | bytes 1572872 | tf_op jit(solution)/shard_map/ppermute | solution.py:31
  180.8 24.6 %collective-permute-start.14 = (bf16[64,4096]{1,0:T(8,128)(2,1)}, bf16[64,4096]{1,0:T(8,128)(2,1)}, u32[]{:S(2)}, u32[]{:S(2)}) collective-permute-start(bf16[64,4096]{1,0:T(8,128)(2,1)} %get-tuple-element.37.refs_4_), channel_id=1, source_target_pairs={{0,4},{1,5},{2,6},{3,7},{4,0},{5,1},{6,2},{7,3},{8,12},{9,13},{10,... | collective-permute-start | bytes 1572872 | tf_op jit(solution)/shard_map/ppermute | solution.py:31
  187.8 19.7 %collective-permute-start.12 = (bf16[32,4096]{1,0:T(8,128)(2,1)S(1)}, bf16[32,4096]{1,0:T(8,128)(2,1)S(1)}, u32[]{:S(2)}, u32[]{:S(2)}) collective-permute-start(bf16[32,4096]{1,0:T(8,128)(2,1)S(1)} %slice.121), channel_id=1, source_target_pairs={{0,4},{1,5},{2,6},{3,7},{4,0},{5,1},{6,2},{7,3},{8,12},{9,13},{10,... | collective-permute-start | bytes 786440 | tf_op jit(solution)/shard_map/ppermute | solution.py:31
  195.1 16.3 %collective-permute-start.4 = (bf16[32,4096]{1,0:T(8,128)(2,1)S(1)}, bf16[32,4096]{1,0:T(8,128)(2,1)S(1)}, u32[]{:S(2)}, u32[]{:S(2)}) collective-permute-start(bf16[32,4096]{1,0:T(8,128)(2,1)S(1)} %slice.123), channel_id=1, source_target_pairs={{0,4},{1,5},{2,6},{3,7},{4,0},{5,1},{6,2},{7,3},{8,12},{9,13},{10,... | collective-permute-start | bytes 786440 | tf_op jit(solution)/shard_map/ppermute | solution.py:31
  205.1 10.1 %collective-permute-start.7 = (bf16[32,4096]{1,0:T(8,128)(2,1)S(1)}, bf16[32,4096]{1,0:T(8,128)(2,1)S(1)}, u32[]{:S(2)}, u32[]{:S(2)}) collective-permute-start(bf16[32,4096]{1,0:T(8,128)(2,1)S(1)} %slice.122), channel_id=1, source_target_pairs={{0,4},{1,5},{2,6},{3,7},{4,0},{5,1},{6,2},{7,3},{8,12},{9,13},{10,... | collective-permute-start | bytes 786440 | tf_op jit(solution)/shard_map/ppermute | solution.py:31
  206.6 9.8 %collective-permute-start.15 = (bf16[32,4096]{1,0:T(8,128)(2,1)S(1)}, bf16[32,4096]{1,0:T(8,128)(2,1)S(1)}, u32[]{:S(2)}, u32[]{:S(2)}) collective-permute-start(bf16[32,4096]{1,0:T(8,128)(2,1)S(1)} %slice.120), channel_id=1, source_target_pairs={{0,2},{1,3},{2,0},{3,1},{4,6},{5,7},{6,4},{7,5},{8,10},{9,11},{10,... | collective-permute-start | bytes 786440 | tf_op jit(solution)/shard_map/ppermute | solution.py:31
  207.6 18.4 %collective-permute-start.13 = (bf16[16,4096]{1,0:T(8,128)(2,1)S(1)}, bf16[16,4096]{1,0:T(8,128)(2,1)S(1)}, u32[]{:S(2)}, u32[]{:S(2)}) collective-permute-start(bf16[16,4096]{1,0:T(8,128)(2,1)S(1)} %slice.125), channel_id=1, source_target_pairs={{0,8},{1,9},{2,10},{3,11},{4,12},{5,13},{6,14},{7,15},{8,0},{9,1},... | collective-permute-start | bytes 393224 | tf_op jit(solution)/shard_map/ppermute | solution.py:31
  211.4 17.4 %collective-permute-start.5 = (bf16[16,4096]{1,0:T(8,128)(2,1)S(1)}, bf16[16,4096]{1,0:T(8,128)(2,1)S(1)}, u32[]{:S(2)}, u32[]{:S(2)}) collective-permute-start(bf16[16,4096]{1,0:T(8,128)(2,1)S(1)} %slice.127), channel_id=1, source_target_pairs={{0,8},{1,9},{2,10},{3,11},{4,12},{5,13},{6,14},{7,15},{8,0},{9,1},... | collective-permute-start | bytes 393224 | tf_op jit(solution)/shard_map/ppermute | solution.py:31
  215.2 16.0 %collective-permute-start.8 = (bf16[16,4096]{1,0:T(8,128)(2,1)S(1)}, bf16[16,4096]{1,0:T(8,128)(2,1)S(1)}, u32[]{:S(2)}, u32[]{:S(2)}) collective-permute-start(bf16[16,4096]{1,0:T(8,128)(2,1)S(1)} %slice.126), channel_id=1, source_target_pairs={{0,8},{1,9},{2,10},{3,11},{4,12},{5,13},{6,14},{7,15},{8,0},{9,1},... | collective-permute-start | bytes 393224 | tf_op jit(solution)/shard_map/ppermute | solution.py:31
  216.4 16.2 %collective-permute-start.16 = (bf16[16,4096]{1,0:T(8,128)(2,1)S(1)}, bf16[16,4096]{1,0:T(8,128)(2,1)S(1)}, u32[]{:S(2)}, u32[]{:S(2)}) collective-permute-start(bf16[16,4096]{1,0:T(8,128)(2,1)S(1)} %slice.124), channel_id=1, source_target_pairs={{0,8},{1,9},{2,10},{3,11},{4,12},{5,13},{6,14},{7,15},{8,0},{9,1},... | collective-permute-start | bytes 393224 | tf_op jit(solution)/shard_map/ppermute | solution.py:31
  (14 other events, 171.7 us)

commit v2 on v1

--- a/solution.py
+++ b/solution.py
@@ -21,7 +21,7 @@
 
 WIDE = 16
 NARROW = 8
-FIRST_SLOTS = 3
+FIRST_SLOTS = 5
 COLUMN_PARTS = 2
 
 ANY = pl.BlockSpec(memory_space=pl.ANY)
@@ -238,7 +238,7 @@
 
 
 def attend_kernel(
-    place, x_ref, q_ref, *refs, first_slot, first, last, rows, tok, ways, tok_rows, block
+    place, x_ref, q_ref, after_ref, *refs, first_slot, first, last, rows, tok, ways, tok_rows, block
 ):
     n_in = 0 if first else 2
     carried = refs[:n_in]
@@ -331,15 +331,11 @@
         acc_s[...] = carried[0][0]
         m_s[...] = carried[1][0]
 
-    if block is None:
-        t_rel, b = step // 2, step % 2
-    else:
-        t_rel, b = step, block
     line = lax.broadcasted_iota(jnp.int32, (tok, PAGE_TOK), 0)
     p = line // tok_rows
     kx = place_of(p)
-    token = ((kx ^ head) * ways + (t_rel ^ way)) * tok_rows + line % tok_rows
-    q_at = token + jnp.where(b == 0, place[2], place[3])
+    token = ((kx ^ head) * ways + (step ^ way)) * tok_rows + line % tok_rows
+    q_at = token + place[2 + block]
 
     def tile_step(at, size, masked):
         span_k = pl.ds(pl.multiple_of(at * PAGE_TOK, PAGE_TOK), size * PAGE_TOK)
@@ -439,24 +435,19 @@
                     outs[w][at : at + 2 * GROUP, :] = piece
 
 
-def attend(place, x, first_slot, q, carried, block, tok_rows, rows):
+def attend(place, x, first_slot, q, after, carried, block, last, tok_rows, rows):
     sources = x.shape[0]
     src_slots = x.shape[1] // (2 * PAGE_TOK)
     steps, total, _ = q.shape
     tok = total // GROUP
     first = carried is None
-    last = block is not None
     ways = steps // 2
     n_slots = -(-sources * src_slots // WIDE) * WIDE
-    if last:
-        grid = ways
-        at = lambda i, *_: (2 * i + block, 0, 0)
-    else:
-        grid = steps
-        at = lambda i, *_: (i, 0, 0)
+    straight = lambda i, *_: (i, 0, 0)
     in_specs = [
         pl.BlockSpec(x.shape, lambda i, *_: (0, 0, 0)),
-        pl.BlockSpec((1, total, HEAD_DIM), at),
+        pl.BlockSpec((1, total, HEAD_DIM), lambda i, *_: (2 * i + block, 0, 0)),
+        ANY,
     ]
     sent = total + 3 * 2 * GROUP
     if last:
@@ -464,12 +455,12 @@
         out_specs = (pl.BlockSpec((sent, HEAD_DIM), lambda i, *_: (0, 0)),) * ways
     else:
         out_shape = (
-            jax.ShapeDtypeStruct((steps, total, 2 * HEAD_DIM), jnp.float32),
-            jax.ShapeDtypeStruct((steps, total, HEAD_DIM), jnp.float32),
+            jax.ShapeDtypeStruct((ways, total, 2 * HEAD_DIM), jnp.float32),
+            jax.ShapeDtypeStruct((ways, total, HEAD_DIM), jnp.float32),
         )
         out_specs = (
-            pl.BlockSpec((1, total, 2 * HEAD_DIM), at),
-            pl.BlockSpec((1, total, HEAD_DIM), at),
+            pl.BlockSpec((1, total, 2 * HEAD_DIM), straight),
+            pl.BlockSpec((1, total, HEAD_DIM), straight),
         )
     extra = ()
     sums = ()
@@ -481,10 +472,10 @@
     if not first:
         extra = tuple(carried)
         in_specs += [
-            pl.BlockSpec((1, total, 2 * HEAD_DIM), at),
-            pl.BlockSpec((1, total, HEAD_DIM), at),
+            pl.BlockSpec((1, total, 2 * HEAD_DIM), straight),
+            pl.BlockSpec((1, total, HEAD_DIM), straight),
         ]
-    flops = 8 * grid * total * sources * src_slots * PAGE_TOK * HEAD_DIM
+    flops = 8 * ways * total * sources * src_slots * PAGE_TOK * HEAD_DIM
     return pl.pallas_call(
         functools.partial(
             attend_kernel,
@@ -500,7 +491,7 @@
         out_shape=out_shape,
         grid_spec=pltpu.PrefetchScalarGridSpec(
             num_scalar_prefetch=1,
-            grid=(grid,),
+            grid=(ways,),
             in_specs=in_specs,
             out_specs=out_specs,
             scratch_shapes=[
@@ -520,7 +511,7 @@
             flops=flops, transcendentals=flops // (8 * HEAD_DIM), bytes_accessed=x.size * 2
         ),
         name="attend_last" if last else "attend_first",
-    )(place, x, q, *extra)
+    )(place, x, q, after, *extra)
 
 
 def merge(parts, a_ref, tok):
@@ -650,14 +641,18 @@
         ws.append(permute_to(w_out, n, lambda i: i ^ s))
 
     rows = 2 * tok
-    carried = attend(place, arrived[0], 0, q, None, None, tok_rows, rows)
 
     def merger(i, s):
         return head_of(i % KV_HEADS) * ways + ((i // KV_HEADS) ^ s)
 
     partial = []
+    after = leaving[0]
     for b in range(2):
-        out = attend(place, arrived[1], FIRST_SLOTS, q, carried, b, tok_rows, rows)
+        carried = attend(place, arrived[0], 0, q, after, None, b, False, tok_rows, rows)
+        out = attend(
+            place, arrived[1], FIRST_SLOTS, q, after, carried, b, True, tok_rows, rows
+        )
+        after = out[0]
         parts = []
         for s in range(ways):
             parts.append(permute_to(out[s], n, lambda i: merger(i, s)))
@@ -667,7 +662,7 @@
     for b in range(2):
         merged = partial[b]
         for c in range(COLUMN_PARTS):
-            y_first = (b, c) != (1, 1)
+            y_first = (b, c) != (0, 1)
             keep, send, *a = project(merged, ws, tok, c, y_first)
             if a:
                 merged = a

time: 235 us -> 242 us (1.030)
  the two profiles are of different devices: /device:TPU:2 before, /device:TPU:0 now
where the time goes in v2:
time: 242 us; the launch traced here: 241 us
  Pallas kernels  104 us (43%)
  waiting for transfers between devices  73.1 us (30%)
  starting transfers between devices  52.3 us (22%)
  other arithmetic  8.55 us (4%)
    pallas_call x4, Pallas kernels, attend(): pl.pallas_call(functools.partial(attend_kernel, first_slot=first_slot, fi...  61.1 us
    ppermute x21, waiting for transfers between devices, permute_to(): return lax.ppermute(x, 'pages', [(i, target(i)) for i in range(n)])  44.6 us
    ppermute x21, starting transfers between devices, permute_to(): return lax.ppermute(x, 'pages', [(i, target(i)) for i in range(n)])  42.7 us
    all_to_all x2, waiting for transfers between devices, exchange(): lax.all_to_all(x, 'pages', 0, 0, axis_index_groups=groups, tiled=True)  28.4 us
    pallas_call x4, Pallas kernels, project(): pl.pallas_call(functools.partial(project_kernel, n_parts=len(parts), n_ws...  25 us
    all_to_all x2, starting transfers between devices, exchange(): lax.all_to_all(x, 'pages', 0, 0, axis_index_groups=groups, tiled=True)  9.6 us
    pallas_call x2, Pallas kernels, split_heads(): pl.pallas_call(functools.partial(split_heads_kernel, first=first, count=c...  6.3 us
    add x8, other arithmetic, local(): total = keep + got.astype(jnp.float32)  4.99 us
  transfers between devices with their start and end apart: 23, of which 8 were waited for; matrix products, arithmetic and copies ran while one was open for 3% of the time, Pallas kernels for 42%

profile of v2, /device:TPU:0, one launch (start us, length us, event | category | flops | bytes accessed | tf_op | source)
XLA Modules:
  0.0 241.1 jit_solution(1189353155046209110)
XLA Ops:
  2.0 3.6 %split_heads.3 = bf16[8,648,2,128]{3,2,1,0:T(2,128)(2,1)} custom-call(bf16[8,128,2,1024]{3,2,1,0:T(2,128)(2,1)} %kv_ref.7, bf16[8,2,128]{2,1,0:T(2,128)(2,1)} %broadcast_in_dim.2.ids_ref), custom_call_target="tpu_custom_call" | custom-call | tf_op jit(solution)/shard_map/split_heads/pallas_call | solution.py:79
  5.5 5.3 %all-to-all-start.1 = ((bf16[8,648,2,128]{3,2,1,0:T(2,128)(2,1)}), bf16[8,648,2,128]{3,2,1,0:T(2,128)(2,1)S(1)}, u32[]{:S(2)}, u32[]{:S(2)}) async-start(bf16[8,648,2,128]{3,2,1,0:T(2,128)(2,1)} %split_heads.3), calls=%async_computation.1 | async-start | bytes 5308416 | tf_op jit(solution)/shard_map/all_to_all | solution.py:621
  14.1 28.4 %all-to-all-done.1 = bf16[8,648,2,128]{3,2,1,0:T(2,128)(2,1)S(1)} async-done(((bf16[8,648,2,128]{3,2,1,0:T(2,128)(2,1)}), bf16[8,648,2,128]{3,2,1,0:T(2,128)(2,1)S(1)}, u32[]{:S(2)}, u32[]{:S(2)}) %all-to-all-start.1) | async-done | bytes 2654240 | tf_op jit(solution)/shard_map/all_to_all | solution.py:621
  42.5 4.3 %all-to-all-start = ((bf16[8,392,2,128]{3,2,1,0:T(2,128)(2,1)}), bf16[8,392,2,128]{3,2,1,0:T(2,128)(2,1)}, u32[]{:S(2)}, u32[]{:S(2)}) async-start(bf16[8,392,2,128]{3,2,1,0:T(2,128)(2,1)} %split_heads.2), calls=%async_computation | async-start | bytes 3211264 | tf_op jit(solution)/shard_map/all_to_all | solution.py:621
  46.9 3.1 %outgoing_pages.1 = (bf16[128,2,1024]{2,1,0:T(2,128)(2,1)}, bf16[128,2,1024]{2,1,0:T(2,128)(2,1)}, bf16[128,2,1024]{2,1,0:T(2,128)(2,1)}, bf16[128,2,1024]{2,1,0:T(2,128)(2,1)}) custom-call(s32[4]{0:T(128)} %bitcast.14, bf16[8,128,2,1024]{3,2,1,0:T(2,128)(2,1)} %kv_ref.7), custom_call_target="tpu_custom_call" | custom-call | tf_op jit(solution)/shard_map/outgoing_pages/pallas_call | solution.py:116
  52.5 4.3 %query_rows.1.q_ref = bf16[4,1024,128]{2,1,0:T(8,128)(2,1)} custom-call(s32[4]{0:T(128)} %pad_add_fusion.place, bf16[2,256,8192]{2,1,0:T(8,128)(2,1)} %q_ref.1), custom_call_target="tpu_custom_call" | custom-call | tf_op jit(solution)/shard_map/query_rows/pallas_call | solution.py:219
  56.9 21.2 %attend_first.2 = (f32[2,1024,256]{2,1,0:T(8,128)}, f32[2,1024,128]{2,1,0:T(8,128)}) custom-call(s32[4]{0:T(128)} %pad_add_fusion.place, bf16[8,1296,128]{2,1,0:T(8,128)(2,1)} %bitcast.12, bf16[4,1024,128]{2,1,0:T(8,128)(2,1)} %query_rows.1.q_ref, bf16[128,2,1024]{2,1,0:T(2,128)(2,1)} %get-tuple-element.24.after_ref), custom_call_target="tpu_custom_call" | custom-call | flops 10737418240 | bytes 2654208 | tf_op jit(solution)/shard_map/attend_first/pallas_call | solution.py:479
  78.1 9.1 %attend_last.2 = (bf16[1072,128]{1,0:T(8,128)(2,1)}, bf16[1072,128]{1,0:T(8,128)(2,1)}) custom-call(s32[4]{0:T(128)} %pad_add_fusion.place, bf16[8,784,128]{2,1,0:T(8,128)(2,1)} %bitcast.4.x_ref, bf16[4,1024,128]{2,1,0:T(8,128)(2,1)} %query_rows.1.q_ref, bf16[128,2,1024]{2,1,0:T(2,128)(2,1)} %get-tuple-element.24.after_ref, ...), custom_call_target="tpu_custom_call" | custom-call | flops 6442450944 | bytes 1605632 | tf_op jit(solution)/shard_map/attend_last/pallas_call | solution.py:479
  87.7 21.4 %attend_first.3 = (f32[2,1024,256]{2,1,0:T(8,128)}, f32[2,1024,128]{2,1,0:T(8,128)}) custom-call(s32[4]{0:T(128)} %pad_add_fusion.place, bf16[8,1296,128]{2,1,0:T(8,128)(2,1)} %bitcast.13, bf16[4,1024,128]{2,1,0:T(8,128)(2,1)} %query_rows.1.q_ref, bf16[1072,128]{1,0:T(8,128)(2,1)} %get-tuple-element.27.after_ref), custom_call_target="tpu_custom_call" | custom-call | flops 10737418240 | bytes 2654208 | tf_op jit(solution)/shard_map/attend_first/pallas_call | solution.py:479
  109.2 9.3 %attend_last.3 = (bf16[1072,128]{1,0:T(8,128)(2,1)}, bf16[1072,128]{1,0:T(8,128)(2,1)}) custom-call(s32[4]{0:T(128)} %pad_add_fusion.place, bf16[8,784,128]{2,1,0:T(8,128)(2,1)} %bitcast.4.x_ref, bf16[4,1024,128]{2,1,0:T(8,128)(2,1)} %query_rows.1.q_ref, bf16[1072,128]{1,0:T(8,128)(2,1)} %get-tuple-element.27.after_ref, ...), custom_call_target="tpu_custom_call" | custom-call | flops 6442450944 | bytes 1605632 | tf_op jit(solution)/shard_map/attend_last/pallas_call | solution.py:479
  123.8 3.7 %collective-permute-start.17 = (bf16[128,2,1024]{2,1,0:T(2,128)(2,1)}, bf16[128,2,1024]{2,1,0:T(2,128)(2,1)S(1)}, u32[]{:S(2)}, u32[]{:S(2)}) collective-permute-start(bf16[128,2,1024]{2,1,0:T(2,128)(2,1)} %get-tuple-element.24.after_ref), channel_id=1, source_target_pairs={{0,1},{1,2},{2,3},{3,4},{4,5},{5,6},{6,7},{7,8},{8,9},{9,10},{10,1... | collective-permute-start | bytes 1572872 | tf_op jit(solution)/shard_map/ppermute | solution.py:31
  129.1 12.6 %collective-permute-done.10.refs_1_ = bf16[1072,128]{1,0:T(8,128)(2,1)S(1)} collective-permute-done((bf16[1072,128]{1,0:T(8,128)(2,1)}, bf16[1072,128]{1,0:T(8,128)(2,1)S(1)}, u32[]{:S(2)}, u32[]{:S(2)}) %collective-permute-start.10) | collective-permute-done | bytes 274464 | tf_op jit(solution)/shard_map/ppermute | solution.py:31
  141.7 15.1 %collective-permute-start.19 = (bf16[128,2,1024]{2,1,0:T(2,128)(2,1)}, bf16[128,2,1024]{2,1,0:T(2,128)(2,1)S(1)}, u32[]{:S(2)}, u32[]{:S(2)}) collective-permute-start(bf16[128,2,1024]{2,1,0:T(2,128)(2,1)} %get-tuple-element.44), channel_id=1, source_target_pairs={{0,3},{1,4},{2,5},{3,6},{4,7},{5,8},{6,9},{7,10},{8,11},{9,12},{10... | collective-permute-start | bytes 1572872 | tf_op jit(solution)/shard_map/ppermute | solution.py:31
  156.8 6.3 %project.6 = (f32[64,4096]{1,0:T(8,128)}, bf16[64,4096]{1,0:T(8,128)(2,1)}, bf16[128,1024]{1,0:T(8,128)(2,1)}) custom-call(bf16[1072,128]{1,0:T(8,128)(2,1)} %copy-done.11, bf16[1072,128]{1,0:T(8,128)(2,1)} %copy-done.12, bf16[512,8192]{1,0:T(8,128)(2,1)} %refs_1_.3, bf16[512,8192]{1,0:T(8,128)(2,1)} %collective-permute-done.2.refs_3_.refs_2_), custom_call_target="tpu_custom_call" | custom-call | flops 1073741824 | bytes 8388608 | tf_op jit(solution)/shard_map/project/pallas_call | solution.py:589
  163.1 4.2 %collective-permute-start.11 = (bf16[64,4096]{1,0:T(8,128)(2,1)}, bf16[64,4096]{1,0:T(8,128)(2,1)}, u32[]{:S(2)}, u32[]{:S(2)}) collective-permute-start(bf16[64,4096]{1,0:T(8,128)(2,1)} %get-tuple-element.39), channel_id=1, source_target_pairs={{0,2},{1,3},{2,0},{3,1},{4,6},{5,7},{6,4},{7,5},{8,10},{9,11},{10,... | collective-permute-start | bytes 1572872 | tf_op jit(solution)/shard_map/ppermute | solution.py:31
  167.3 6.3 %project.4 = (f32[64,4096]{1,0:T(8,128)}, bf16[64,4096]{1,0:T(8,128)(2,1)}, bf16[128,1024]{1,0:T(8,128)(2,1)}) custom-call(bf16[1072,128]{1,0:T(8,128)(2,1)} %copy-done.10, bf16[1072,128]{1,0:T(8,128)(2,1)} %copy-done.9, bf16[512,8192]{1,0:T(8,128)(2,1)} %refs_1_.3, bf16[512,8192]{1,0:T(8,128)(2,1)} %collective-permute-done.2.refs_3_.refs_2_), custom_call_target="tpu_custom_call" | custom-call | flops 1073741824 | bytes 8388608 | tf_op jit(solution)/shard_map/project/pallas_call | solution.py:589
  173.6 6.2 %project.5 = (f32[64,4096]{1,0:T(8,128)}, bf16[64,4096]{1,0:T(8,128)(2,1)}) custom-call(bf16[128,1024]{1,0:T(8,128)(2,1)} %get-tuple-element.31.refs_0_, bf16[512,8192]{1,0:T(8,128)(2,1)} %refs_1_.3, bf16[512,8192]{1,0:T(8,128)(2,1)} %collective-permute-done.2.refs_3_.refs_2_), custom_call_target="tpu_custom_call" | custom-call | flops 1073741824 | bytes 8388608 | tf_op jit(solution)/shard_map/project/pallas_call | solution.py:589
  179.8 6.2 %project.7 = (f32[64,4096]{1,0:T(8,128)}, bf16[64,4096]{1,0:T(8,128)(2,1)}) custom-call(bf16[128,1024]{1,0:T(8,128)(2,1)} %get-tuple-element.40.refs_0_, bf16[512,8192]{1,0:T(8,128)(2,1)} %refs_1_.3, bf16[512,8192]{1,0:T(8,128)(2,1)} %collective-permute-done.2.refs_3_.refs_2_), custom_call_target="tpu_custom_call" | custom-call | flops 1073741824 | bytes 8388608 | tf_op jit(solution)/shard_map/project/pallas_call | solution.py:589
  189.0 4.0 %arrange_pages.1 = bf16[8,128,2,1024]{3,2,1,0:T(2,128)(2,1)} custom-call(s32[8]{0:T(128)} %page_after.1, s32[4]{0:T(128)} %bitcast.15, bf16[8,128,2,1024]{3,2,1,0:T(2,128)(2,1)} %kv_ref.7, bf16[128,2,1024]{2,1,0:T(2,128)(2,1)} %copy-done.5, bf16[128,2,1024]{2,1,0:T(2,128)(2,1)} %copy-done.6, bf16[128,2,1024]{2,1,0:T(2,128)(2,1)} %copy-done.7, ...), custom_call_target="tpu_custom_call" | custom-call | tf_op jit(solution)/shard_map/arrange_pages/pallas_call | solution.py:174
  196.3 4.9 %collective-permute-done.3 = bf16[64,4096]{1,0:T(8,128)(2,1)} collective-permute-done((bf16[64,4096]{1,0:T(8,128)(2,1)}, bf16[64,4096]{1,0:T(8,128)(2,1)}, u32[]{:S(2)}, u32[]{:S(2)}) %collective-permute-start.3) | collective-permute-done | bytes 524320 | tf_op jit(solution)/shard_map/ppermute | solution.py:31
  204.5 8.0 %collective-permute-done.14 = bf16[64,4096]{1,0:T(8,128)(2,1)} collective-permute-done((bf16[64,4096]{1,0:T(8,128)(2,1)}, bf16[64,4096]{1,0:T(8,128)(2,1)}, u32[]{:S(2)}, u32[]{:S(2)}) %collective-permute-start.14) | collective-permute-done | bytes 524320 | tf_op jit(solution)/shard_map/ppermute | solution.py:31
  213.8 3.8 %collective-permute-start.13 = (bf16[16,4096]{1,0:T(8,128)(2,1)S(1)}, bf16[16,4096]{1,0:T(8,128)(2,1)S(1)}, u32[]{:S(2)}, u32[]{:S(2)}) collective-permute-start(bf16[16,4096]{1,0:T(8,128)(2,1)S(1)} %slice.125), channel_id=1, source_target_pairs={{0,8},{1,9},{2,10},{3,11},{4,12},{5,13},{6,14},{7,15},{8,0},{9,1},... | collective-permute-start | bytes 393224 | tf_op jit(solution)/shard_map/ppermute | solution.py:31
  220.8 5.0 %collective-permute-done.15 = bf16[32,4096]{1,0:T(8,128)(2,1)S(1)} collective-permute-done((bf16[32,4096]{1,0:T(8,128)(2,1)S(1)}, bf16[32,4096]{1,0:T(8,128)(2,1)S(1)}, u32[]{:S(2)}, u32[]{:S(2)}) %collective-permute-start.15) | collective-permute-done | bytes 262176 | tf_op jit(solution)/shard_map/ppermute | solution.py:31
  226.0 10.3 %collective-permute-done.5 = bf16[16,4096]{1,0:T(8,128)(2,1)S(1)} collective-permute-done((bf16[16,4096]{1,0:T(8,128)(2,1)S(1)}, bf16[16,4096]{1,0:T(8,128)(2,1)S(1)}, u32[]{:S(2)}, u32[]{:S(2)}) %collective-permute-start.5) | collective-permute-done | bytes 131104 | tf_op jit(solution)/shard_map/ppermute | solution.py:31
  (92 shorter events, 33.5 us)
Async XLA Ops:
  5.5 37.0 %all-to-all-start.1 = ((bf16[8,648,2,128]{3,2,1,0:T(2,128)(2,1)}), bf16[8,648,2,128]{3,2,1,0:T(2,128)(2,1)S(1)}, u32[]{:S(2)}, u32[]{:S(2)}) async-start(bf16[8,648,2,128]{3,2,1,0:T(2,128)(2,1)} %split_heads.3), calls=%async_computation.1 | async-start | bytes 5308416 | tf_op jit(solution)/shard_map/all_to_all | solution.py:621
  10.8 145.9 %collective-permute-start.2 = (bf16[512,8192]{1,0:T(8,128)(2,1)}, bf16[512,8192]{1,0:T(8,128)(2,1)}, u32[]{:S(2)}, u32[]{:S(2)}) collective-permute-start(bf16[512,8192]{1,0:T(8,128)(2,1)} %refs_1_.3), channel_id=1, source_target_pairs={{0,1},{1,0},{2,3},{3,2},{4,5},{5,4},{6,7},{7,6},{8,9},{9,8},{10,11... | collective-permute-start | bytes 25165832 | tf_op jit(solution)/shard_map/ppermute | solution.py:31
  42.5 35.6 %all-to-all-start = ((bf16[8,392,2,128]{3,2,1,0:T(2,128)(2,1)}), bf16[8,392,2,128]{3,2,1,0:T(2,128)(2,1)}, u32[]{:S(2)}, u32[]{:S(2)}) async-start(bf16[8,392,2,128]{3,2,1,0:T(2,128)(2,1)} %split_heads.2), calls=%async_computation | async-start | bytes 3211264 | tf_op jit(solution)/shard_map/all_to_all | solution.py:621
  87.2 36.5 %collective-permute-start.1 = (bf16[1072,128]{1,0:T(8,128)(2,1)}, bf16[1072,128]{1,0:T(8,128)(2,1)S(1)}, u32[]{:S(2)}, u32[]{:S(2)}) collective-permute-start(bf16[1072,128]{1,0:T(8,128)(2,1)} %get-tuple-element.28), channel_id=1, source_target_pairs={{0,1},{1,9},{2,3},{3,11},{4,5},{5,13},{6,7},{7,15},{8,0},{9,8},{10... | collective-permute-start | bytes 823304 | tf_op jit(solution)/shard_map/ppermute | solution.py:31
  118.5 9.0 %collective-permute-start.9 = (bf16[1072,128]{1,0:T(8,128)(2,1)}, bf16[1072,128]{1,0:T(8,128)(2,1)S(1)}, u32[]{:S(2)}, u32[]{:S(2)}) collective-permute-start(bf16[1072,128]{1,0:T(8,128)(2,1)} %get-tuple-element.36), channel_id=1, source_target_pairs={{0,0},{1,8},{2,2},{3,10},{4,4},{5,12},{6,6},{7,14},{8,1},{9,9},{10... | collective-permute-start | bytes 823304 | tf_op jit(solution)/shard_map/ppermute | solution.py:31
  120.1 21.6 %collective-permute-start.10 = (bf16[1072,128]{1,0:T(8,128)(2,1)}, bf16[1072,128]{1,0:T(8,128)(2,1)S(1)}, u32[]{:S(2)}, u32[]{:S(2)}) collective-permute-start(bf16[1072,128]{1,0:T(8,128)(2,1)} %get-tuple-element.37), channel_id=1, source_target_pairs={{0,1},{1,9},{2,3},{3,11},{4,5},{5,13},{6,7},{7,15},{8,0},{9,8},{10... | collective-permute-start | bytes 823304 | tf_op jit(solution)/shard_map/ppermute | solution.py:31
  123.1 40.0 %collective-permute-start = (bf16[1072,128]{1,0:T(8,128)(2,1)S(1)}, bf16[1072,128]{1,0:T(8,128)(2,1)S(1)}, u32[]{:S(2)}, u32[]{:S(2)}) collective-permute-start(bf16[1072,128]{1,0:T(8,128)(2,1)S(1)} %copy-done.14), channel_id=1, source_target_pairs={{0,0},{1,8},{2,2},{3,10},{4,4},{5,12},{6,6},{7,14},{8,1},{9,9},{10... | collective-permute-start | bytes 823304 | tf_op jit(solution)/shard_map/ppermute | solution.py:31
  123.8 39.3 %copy-start.9 = (bf16[1072,128]{1,0:T(8,128)(2,1)}, bf16[1072,128]{1,0:T(8,128)(2,1)S(1)}, u32[]{:S(2)}) copy-start(bf16[1072,128]{1,0:T(8,128)(2,1)S(1)} %collective-permute-done.1.refs_1_) | copy-start | bytes 823300
  123.8 64.4 %collective-permute-start.17 = (bf16[128,2,1024]{2,1,0:T(2,128)(2,1)}, bf16[128,2,1024]{2,1,0:T(2,128)(2,1)S(1)}, u32[]{:S(2)}, u32[]{:S(2)}) collective-permute-start(bf16[128,2,1024]{2,1,0:T(2,128)(2,1)} %get-tuple-element.24.after_ref), channel_id=1, source_target_pairs={{0,1},{1,2},{2,3},{3,4},{4,5},{5,6},{6,7},{7,8},{8,9},{9,10},{10,1... | collective-permute-start | bytes 1572872 | tf_op jit(solution)/shard_map/ppermute | solution.py:31
  127.5 58.5 %collective-permute-start.18 = (bf16[128,2,1024]{2,1,0:T(2,128)(2,1)}, bf16[128,2,1024]{2,1,0:T(2,128)(2,1)S(1)}, u32[]{:S(2)}, u32[]{:S(2)}) collective-permute-start(bf16[128,2,1024]{2,1,0:T(2,128)(2,1)} %get-tuple-element.43), channel_id=1, source_target_pairs={{0,2},{1,3},{2,4},{3,5},{4,6},{5,7},{6,8},{7,9},{8,10},{9,11},{10,... | collective-permute-start | bytes 1572872 | tf_op jit(solution)/shard_map/ppermute | solution.py:31
  141.7 45.0 %collective-permute-start.19 = (bf16[128,2,1024]{2,1,0:T(2,128)(2,1)}, bf16[128,2,1024]{2,1,0:T(2,128)(2,1)S(1)}, u32[]{:S(2)}, u32[]{:S(2)}) collective-permute-start(bf16[128,2,1024]{2,1,0:T(2,128)(2,1)} %get-tuple-element.44), channel_id=1, source_target_pairs={{0,3},{1,4},{2,5},{3,6},{4,7},{5,8},{6,9},{7,10},{8,11},{9,12},{10... | collective-permute-start | bytes 1572872 | tf_op jit(solution)/shard_map/ppermute | solution.py:31
  156.8 29.9 %collective-permute-start.20 = (bf16[128,2,1024]{2,1,0:T(2,128)(2,1)}, bf16[128,2,1024]{2,1,0:T(2,128)(2,1)S(1)}, u32[]{:S(2)}, u32[]{:S(2)}) collective-permute-start(bf16[128,2,1024]{2,1,0:T(2,128)(2,1)} %get-tuple-element.45), channel_id=1, source_target_pairs={{0,4},{1,5},{2,6},{3,7},{4,8},{5,9},{6,10},{7,11},{8,12},{9,13},{1... | collective-permute-start | bytes 1572872 | tf_op jit(solution)/shard_map/ppermute | solution.py:31
  163.1 29.9 %collective-permute-start.11 = (bf16[64,4096]{1,0:T(8,128)(2,1)}, bf16[64,4096]{1,0:T(8,128)(2,1)}, u32[]{:S(2)}, u32[]{:S(2)}) collective-permute-start(bf16[64,4096]{1,0:T(8,128)(2,1)} %get-tuple-element.39), channel_id=1, source_target_pairs={{0,2},{1,3},{2,0},{3,1},{4,6},{5,7},{6,4},{7,5},{8,10},{9,11},{10,... | collective-permute-start | bytes 1572872 | tf_op jit(solution)/shard_map/ppermute | solution.py:31
  186.0 15.2 %collective-permute-start.3 = (bf16[64,4096]{1,0:T(8,128)(2,1)}, bf16[64,4096]{1,0:T(8,128)(2,1)}, u32[]{:S(2)}, u32[]{:S(2)}) collective-permute-start(bf16[64,4096]{1,0:T(8,128)(2,1)} %get-tuple-element.30), channel_id=1, source_target_pairs={{0,2},{1,3},{2,0},{3,1},{4,6},{5,7},{6,4},{7,5},{8,10},{9,11},{10,... | collective-permute-start | bytes 1572872 | tf_op jit(solution)/shard_map/ppermute | solution.py:31
  186.7 15.8 %collective-permute-start.6 = (bf16[64,4096]{1,0:T(8,128)(2,1)}, bf16[64,4096]{1,0:T(8,128)(2,1)}, u32[]{:S(2)}, u32[]{:S(2)}) collective-permute-start(bf16[64,4096]{1,0:T(8,128)(2,1)} %get-tuple-element.33), channel_id=1, source_target_pairs={{0,4},{1,5},{2,6},{3,7},{4,0},{5,1},{6,2},{7,3},{8,12},{9,13},{10,... | collective-permute-start | bytes 1572872 | tf_op jit(solution)/shard_map/ppermute | solution.py:31
  186.7 25.7 %collective-permute-start.14 = (bf16[64,4096]{1,0:T(8,128)(2,1)}, bf16[64,4096]{1,0:T(8,128)(2,1)}, u32[]{:S(2)}, u32[]{:S(2)}) collective-permute-start(bf16[64,4096]{1,0:T(8,128)(2,1)} %get-tuple-element.42.refs_4_), channel_id=1, source_target_pairs={{0,2},{1,3},{2,0},{3,1},{4,6},{5,7},{6,4},{7,5},{8,10},{9,11},{10,... | collective-permute-start | bytes 1572872 | tf_op jit(solution)/shard_map/ppermute | solution.py:31
  194.4 19.3 %collective-permute-start.12 = (bf16[32,4096]{1,0:T(8,128)(2,1)S(1)}, bf16[32,4096]{1,0:T(8,128)(2,1)S(1)}, u32[]{:S(2)}, u32[]{:S(2)}) collective-permute-start(bf16[32,4096]{1,0:T(8,128)(2,1)S(1)} %slice.121), channel_id=1, source_target_pairs={{0,4},{1,5},{2,6},{3,7},{4,0},{5,1},{6,2},{7,3},{8,12},{9,13},{10,... | collective-permute-start | bytes 786440 | tf_op jit(solution)/shard_map/ppermute | solution.py:31
  202.5 15.1 %collective-permute-start.4 = (bf16[32,4096]{1,0:T(8,128)(2,1)S(1)}, bf16[32,4096]{1,0:T(8,128)(2,1)S(1)}, u32[]{:S(2)}, u32[]{:S(2)}) collective-permute-start(bf16[32,4096]{1,0:T(8,128)(2,1)S(1)} %slice.123), channel_id=1, source_target_pairs={{0,4},{1,5},{2,6},{3,7},{4,0},{5,1},{6,2},{7,3},{8,12},{9,13},{10,... | collective-permute-start | bytes 786440 | tf_op jit(solution)/shard_map/ppermute | solution.py:31
  203.7 14.0 %collective-permute-start.7 = (bf16[32,4096]{1,0:T(8,128)(2,1)S(1)}, bf16[32,4096]{1,0:T(8,128)(2,1)S(1)}, u32[]{:S(2)}, u32[]{:S(2)}) collective-permute-start(bf16[32,4096]{1,0:T(8,128)(2,1)S(1)} %slice.122), channel_id=1, source_target_pairs={{0,2},{1,3},{2,0},{3,1},{4,6},{5,7},{6,4},{7,5},{8,10},{9,11},{10,... | collective-permute-start | bytes 786440 | tf_op jit(solution)/shard_map/ppermute | solution.py:31
  213.6 12.1 %collective-permute-start.15 = (bf16[32,4096]{1,0:T(8,128)(2,1)S(1)}, bf16[32,4096]{1,0:T(8,128)(2,1)S(1)}, u32[]{:S(2)}, u32[]{:S(2)}) collective-permute-start(bf16[32,4096]{1,0:T(8,128)(2,1)S(1)} %slice.120), channel_id=1, source_target_pairs={{0,4},{1,5},{2,6},{3,7},{4,0},{5,1},{6,2},{7,3},{8,12},{9,13},{10,... | collective-permute-start | bytes 786440 | tf_op jit(solution)/shard_map/ppermute | solution.py:31
  213.8 12.1 %collective-permute-start.13 = (bf16[16,4096]{1,0:T(8,128)(2,1)S(1)}, bf16[16,4096]{1,0:T(8,128)(2,1)S(1)}, u32[]{:S(2)}, u32[]{:S(2)}) collective-permute-start(bf16[16,4096]{1,0:T(8,128)(2,1)S(1)} %slice.125), channel_id=1, source_target_pairs={{0,8},{1,9},{2,10},{3,11},{4,12},{5,13},{6,14},{7,15},{8,0},{9,1},... | collective-permute-start | bytes 393224 | tf_op jit(solution)/shard_map/ppermute | solution.py:31
  217.6 18.6 %collective-permute-start.5 = (bf16[16,4096]{1,0:T(8,128)(2,1)S(1)}, bf16[16,4096]{1,0:T(8,128)(2,1)S(1)}, u32[]{:S(2)}, u32[]{:S(2)}) collective-permute-start(bf16[16,4096]{1,0:T(8,128)(2,1)S(1)} %slice.127), channel_id=1, source_target_pairs={{0,8},{1,9},{2,10},{3,11},{4,12},{5,13},{6,14},{7,15},{8,0},{9,1},... | collective-permute-start | bytes 393224 | tf_op jit(solution)/shard_map/ppermute | solution.py:31
  217.8 21.0 %collective-permute-start.8 = (bf16[16,4096]{1,0:T(8,128)(2,1)S(1)}, bf16[16,4096]{1,0:T(8,128)(2,1)S(1)}, u32[]{:S(2)}, u32[]{:S(2)}) collective-permute-start(bf16[16,4096]{1,0:T(8,128)(2,1)S(1)} %slice.126), channel_id=1, source_target_pairs={{0,8},{1,9},{2,10},{3,11},{4,12},{5,13},{6,14},{7,15},{8,0},{9,1},... | collective-permute-start | bytes 393224 | tf_op jit(solution)/shard_map/ppermute | solution.py:31
  225.8 14.4 %collective-permute-start.16 = (bf16[16,4096]{1,0:T(8,128)(2,1)S(1)}, bf16[16,4096]{1,0:T(8,128)(2,1)S(1)}, u32[]{:S(2)}, u32[]{:S(2)}) collective-permute-start(bf16[16,4096]{1,0:T(8,128)(2,1)S(1)} %slice.124), channel_id=1, source_target_pairs={{0,8},{1,9},{2,10},{3,11},{4,12},{5,13},{6,14},{7,15},{8,0},{9,1},... | collective-permute-start | bytes 393224 | tf_op jit(solution)/shard_map/ppermute | solution.py:31
  (14 other events, 112.1 us)

commit v3 on v1

--- a/solution.py
+++ b/solution.py
@@ -21,7 +21,7 @@
 
 WIDE = 16
 NARROW = 8
-FIRST_SLOTS = 3
+FIRST_SLOTS = 4
 COLUMN_PARTS = 2
 
 ANY = pl.BlockSpec(memory_space=pl.ANY)
@@ -40,11 +40,15 @@
     return (p % 2) * 4 + (p // 2 % 2) * 2 + p // 4
 
 
-def split_heads_kernel(kv_ref, ids_ref, out_ref, buf, in_sems, out_sems, *, first, count):
+def split_heads_kernel(place, kv_ref, ids_ref, *refs, first, count, apart):
+    outs = refs[: KV_HEADS if apart else 1]
+    buf, in_sems, out_sems = refs[len(outs) :]
     extra = ids_ref.shape[0]
     loads = []
+    stores = []
     for d in range(KV_HEADS):
-        lanes = pl.ds(head_of(d) * HEAD_DIM, HEAD_DIM)
+        head = head_of(place[4] ^ d) if apart else head_of(d)
+        lanes = pl.ds(pl.multiple_of(head * HEAD_DIM, HEAD_DIM), HEAD_DIM)
         row = [
             pltpu.make_async_copy(
                 kv_ref.at[first + i, :, :, lanes],
@@ -59,10 +63,8 @@
             )
         )
         loads.append(row)
-    stores = [
-        pltpu.make_async_copy(buf.at[d], out_ref.at[d], out_sems.at[d])
-        for d in range(KV_HEADS)
-    ]
+        to = outs[d] if apart else outs[0].at[d]
+        stores.append(pltpu.make_async_copy(buf.at[d], to, out_sems.at[d]))
     for row in loads:
         for load in row:
             load.start()
@@ -74,20 +76,29 @@
         store.wait()
 
 
-def split_heads(kv_cache, ids, first, count):
-    shape = (KV_HEADS, count * PAGE_TOK + ids.shape[0], 2, HEAD_DIM)
+def split_heads(place, kv_cache, ids, first, count, apart):
+    piece = (count * PAGE_TOK + ids.shape[0], 2, HEAD_DIM)
+    shape = (KV_HEADS,) + piece
+    if apart:
+        out_shape = (jax.ShapeDtypeStruct(piece, kv_cache.dtype),) * KV_HEADS
+    else:
+        out_shape = (jax.ShapeDtypeStruct(shape, kv_cache.dtype),)
     return pl.pallas_call(
-        functools.partial(split_heads_kernel, first=first, count=count),
-        out_shape=jax.ShapeDtypeStruct(shape, kv_cache.dtype),
-        in_specs=[ANY, ANY],
-        out_specs=ANY,
-        scratch_shapes=[
-            pltpu.VMEM(shape, kv_cache.dtype),
-            pltpu.SemaphoreType.DMA((KV_HEADS, count + 1)),
-            pltpu.SemaphoreType.DMA((KV_HEADS,)),
-        ],
+        functools.partial(split_heads_kernel, first=first, count=count, apart=apart),
+        out_shape=out_shape,
+        grid_spec=pltpu.PrefetchScalarGridSpec(
+            num_scalar_prefetch=1,
+            grid=(),
+            in_specs=[ANY, ANY],
+            out_specs=(ANY,) * len(out_shape),
+            scratch_shapes=[
+                pltpu.VMEM(shape, kv_cache.dtype),
+                pltpu.SemaphoreType.DMA((KV_HEADS, count + 1)),
+                pltpu.SemaphoreType.DMA((KV_HEADS,)),
+            ],
+        ),
         name="split_heads",
-    )(kv_cache, ids)
+    )(place, kv_cache, ids)
 
 
 def outgoing_kernel(move_out, kv_ref, *refs):
@@ -238,8 +249,13 @@
 
 
 def attend_kernel(
-    place, x_ref, q_ref, *refs, first_slot, first, last, rows, tok, ways, tok_rows, block
+    place, *refs, n_x, first_slot, first, last, rows, tok, ways, tok_rows, block
 ):
+    xs, q_ref, refs = refs[:n_x], refs[n_x], refs[n_x + 1 :]
+    if n_x == 1:
+        x_ref = xs[0]
+    else:
+        refs, x_ref, x_sems = refs[:-2], refs[-2], refs[-1]
     n_in = 0 if first else 2
     carried = refs[:n_in]
     outs = refs[n_in : n_in + (ways if last else 2)]
@@ -256,6 +272,14 @@
 
     @pl.when(step == 0)
     def _():
+        if n_x > 1:
+            loads = [
+                pltpu.make_async_copy(x, x_ref.at[i], x_sems.at[i]) for i, x in enumerate(xs)
+            ]
+            for load in loads:
+                load.start()
+            for load in loads:
+                load.wait()
         end = src_slots * 2 * PAGE_TOK
         extra = x_ref.shape[1] - end
         row = lax.broadcasted_iota(jnp.int32, (extra, HEAD_DIM), 0)
@@ -439,9 +463,10 @@
                     outs[w][at : at + 2 * GROUP, :] = piece
 
 
-def attend(place, x, first_slot, q, carried, block, tok_rows, rows):
-    sources = x.shape[0]
-    src_slots = x.shape[1] // (2 * PAGE_TOK)
+def attend(place, xs, first_slot, q, carried, block, tok_rows, rows):
+    sources = KV_HEADS
+    depth = xs[0].shape[-2]
+    src_slots = depth // (2 * PAGE_TOK)
     steps, total, _ = q.shape
     tok = total // GROUP
     first = carried is None
@@ -454,10 +479,16 @@
     else:
         grid = steps
         at = lambda i, *_: (i, 0, 0)
-    in_specs = [
-        pl.BlockSpec(x.shape, lambda i, *_: (0, 0, 0)),
-        pl.BlockSpec((1, total, HEAD_DIM), at),
-    ]
+    if len(xs) == 1:
+        in_specs = [pl.BlockSpec(xs[0].shape, lambda i, *_: (0, 0, 0))]
+        landing = []
+    else:
+        in_specs = [ANY] * len(xs)
+        landing = [
+            pltpu.VMEM((sources, depth, HEAD_DIM), xs[0].dtype),
+            pltpu.SemaphoreType.DMA((sources,)),
+        ]
+    in_specs.append(pl.BlockSpec((1, total, HEAD_DIM), at))
     sent = total + 3 * 2 * GROUP
     if last:
         out_shape = (jax.ShapeDtypeStruct((sent, HEAD_DIM), jnp.bfloat16),) * ways
@@ -488,6 +519,7 @@
     return pl.pallas_call(
         functools.partial(
             attend_kernel,
+            n_x=len(xs),
             first_slot=first_slot,
             first=first,
             last=last,
@@ -514,13 +546,16 @@
                 pltpu.SMEM((sources, HEAD_DIM), jnp.int32),
                 pltpu.SMEM((2,), jnp.int32),
                 pltpu.SemaphoreType.DMA(()),
+                *landing,
             ],
         ),
         cost_estimate=pl.CostEstimate(
-            flops=flops, transcendentals=flops // (8 * HEAD_DIM), bytes_accessed=x.size * 2
+            flops=flops,
+            transcendentals=flops // (8 * HEAD_DIM),
+            bytes_accessed=4 * sources * depth * HEAD_DIM,
         ),
         name="attend_last" if last else "attend_first",
-    )(place, x, q, *extra)
+    )(place, *xs, q, *extra)
 
 
 def merge(parts, a_ref, tok):
@@ -631,13 +666,15 @@
 
     ids = jnp.broadcast_to(slot_page_before[:, None, None], (slots, 2, HEAD_DIM))
     ids = ids.astype(kv_cache.dtype)
-    cuts = [(0, FIRST_SLOTS), (FIRST_SLOTS, slots - FIRST_SLOTS)]
-    arrived = []
-    for at, count in cuts:
-        piece = split_heads(kv_cache, ids, at, count)
-        got = exchange(piece)
-        arrived.append(got.reshape(KV_HEADS, -1, HEAD_DIM))
-    place = jnp.stack([head, way, positions[0, 0], positions[1, 0]]).astype(jnp.int32)
+    spots = [head, way, positions[0, 0], positions[1, 0], me % KV_HEADS]
+    place = jnp.stack(spots).astype(jnp.int32)
+    (piece,) = split_heads(slot_page_before, kv_cache, ids, 0, FIRST_SLOTS, False)
+    early = [exchange(piece).reshape(KV_HEADS, -1, HEAD_DIM)]
+    pieces = split_heads(place, kv_cache, ids, FIRST_SLOTS, slots - FIRST_SLOTS, True)
+    late = [pieces[0]]
+    for d in range(1, KV_HEADS):
+        late.append(permute_to(pieces[d], n, lambda i: i ^ d))
+    late = [x.reshape(-1, HEAD_DIM) for x in late]
     q = query_rows(queries, place, ways, tok_rows)
 
     leaving = outgoing_pages(kv_cache, move_out[0])
@@ -650,14 +687,14 @@
         ws.append(permute_to(w_out, n, lambda i: i ^ s))
 
     rows = 2 * tok
-    carried = attend(place, arrived[0], 0, q, None, None, tok_rows, rows)
+    carried = attend(place, early, 0, q, None, None, tok_rows, rows)
 
     def merger(i, s):
         return head_of(i % KV_HEADS) * ways + ((i // KV_HEADS) ^ s)
 
     partial = []
     for b in range(2):
-        out = attend(place, arrived[1], FIRST_SLOTS, q, carried, b, tok_rows, rows)
+        out = attend(place, late, FIRST_SLOTS, q, carried, b, tok_rows, rows)
         parts = []
         for s in range(ways):
             parts.append(permute_to(out[s], n, lambda i: merger(i, s)))
@@ -667,7 +704,7 @@
     for b in range(2):
         merged = partial[b]
         for c in range(COLUMN_PARTS):
-            y_first = (b, c) != (1, 1)
+            y_first = (b, c) != (0, 1)
             keep, send, *a = project(merged, ws, tok, c, y_first)
             if a:
                 merged = a

time: 235 us -> 219 us (0.932)
  starting transfers between devices: 70.5 us -> 49.3 us
  Pallas kernels: 98.6 us -> 102 us
  waiting for transfers between devices: 48.8 us -> 52.2 us
    ppermute x21 -> x28, waiting for transfers between devices: 31.2 us -> 52.2 us  [permute_to(): return lax.ppermute(x, 'pages', [(i, target(i)) for i in range(n)])]
    ppermute x21 -> x28, starting transfers between devices: 63.1 us -> 45.3 us  [permute_to(): return lax.ppermute(x, 'pages', [(i, target(i)) for i in range(n)])]
    all_to_all x2 -> x1, waiting for transfers between devices: 17.5 us -> 0.01 us  [exchange(): lax.all_to_all(x, 'pages', 0, 0, axis_index_groups=groups, tiled=True)]
    all_to_all x2 -> x1, starting transfers between devices: 7.45 us -> 3.92 us  [exchange(): lax.all_to_all(x, 'pages', 0, 0, axis_index_groups=groups, tiled=True)]
    unnamed x30 -> x38, local copies, waits for them, and re-layouts: 4.74 us -> 2.85 us
  transfers between devices with their start and end apart: 23 -> 29, of which waited for: 9 -> 9; matrix products, arithmetic and copies ran while one was open for 3% -> 4% of each run, Pallas kernels for 41% -> 47%
where the time goes in v3:
time: 219 us; the launch traced here: 218 us
  Pallas kernels  102 us (47%)
  waiting for transfers between devices  52.2 us (24%)
  starting transfers between devices  49.3 us (23%)
  other arithmetic  6.53 us (3%)
  local copies, waits for them, and re-layouts  6.3 us (3%)
    pallas_call x3, Pallas kernels, attend(): pl.pallas_call(functools.partial(attend_kernel, n_x=len(xs), first_slot=f...  57.5 us
    ppermute x28, waiting for transfers between devices, permute_to(): return lax.ppermute(x, 'pages', [(i, target(i)) for i in range(n)])  52.2 us
    ppermute x28, starting transfers between devices, permute_to(): return lax.ppermute(x, 'pages', [(i, target(i)) for i in range(n)])  45.3 us
    pallas_call x4, Pallas kernels, project(): pl.pallas_call(functools.partial(project_kernel, n_parts=len(parts), n_ws...  25 us
    pallas_call x2, Pallas kernels, split_heads(): pl.pallas_call(functools.partial(split_heads_kernel, first=first, count=c...  7.86 us
    add x8, other arithmetic, local(): total = keep + got.astype(jnp.float32)  4.86 us
  transfers between devices with their start and end apart: 29, of which 9 were waited for; matrix products, arithmetic and copies ran while one was open for 4% of the time, Pallas kernels for 47%

profile of v3, /device:TPU:2, one launch (start us, length us, event | category | flops | bytes accessed | tf_op | source)
XLA Modules:
  0.0 217.8 jit_solution(9368740649137742846)
XLA Ops:
  2.0 4.0 %split_heads.3 = bf16[8,520,2,128]{3,2,1,0:T(2,128)(2,1)} custom-call(s32[8]{0:T(128)} %place.1, bf16[8,128,2,1024]{3,2,1,0:T(2,128)(2,1)} %kv_ref.7, bf16[8,2,128]{2,1,0:T(2,128)(2,1)} %broadcast_in_dim.2.ids_ref), custom_call_target="tpu_custom_call" | custom-call | tf_op jit(solution)/shard_map/split_heads/pallas_call | solution.py:86
  6.0 3.9 %all-to-all-start = ((bf16[8,520,2,128]{3,2,1,0:T(2,128)(2,1)}), bf16[8,520,2,128]{3,2,1,0:T(2,128)(2,1)S(1)}, u32[]{:S(2)}, u32[]{:S(2)}) async-start(bf16[8,520,2,128]{3,2,1,0:T(2,128)(2,1)} %split_heads.3), calls=%async_computation | async-start | bytes 4259840 | tf_op jit(solution)/shard_map/all_to_all | solution.py:665
  12.5 3.9 %split_heads.2 = (bf16[520,2,128]{2,1,0:T(2,128)(2,1)}, bf16[520,2,128]{2,1,0:T(2,128)(2,1)}, bf16[520,2,128]{2,1,0:T(2,128)(2,1)}, bf16[520,2,128]{2,1,0:T(2,12...) custom-call(s32[5]{0:T(128)} %stack.24.place, ...), custom_call_target="tpu_custom_call" | custom-call | tf_op jit(solution)/shard_map/split_heads/pallas_call | solution.py:86
  20.4 4.4 %query_rows.1.refs_1_.refs_8_ = bf16[4,1024,128]{2,1,0:T(8,128)(2,1)} custom-call(s32[5]{0:T(128)} %stack.24.place, bf16[2,256,8192]{2,1,0:T(8,128)(2,1)} %q_ref.1), custom_call_target="tpu_custom_call" | custom-call | tf_op jit(solution)/shard_map/query_rows/pallas_call | solution.py:230
  24.9 17.3 %collective-permute-done.1 = bf16[520,2,128]{2,1,0:T(2,128)(2,1)S(1)} collective-permute-done((bf16[520,2,128]{2,1,0:T(2,128)(2,1)}, bf16[520,2,128]{2,1,0:T(2,128)(2,1)S(1)}, u32[]{:S(2)}, u32[]{:S(2)}) %collective-permute-start.1) | collective-permute-done | bytes 266272 | tf_op jit(solution)/shard_map/ppermute | solution.py:31
  43.4 3.4 %collective-permute-done.2 = bf16[520,2,128]{2,1,0:T(2,128)(2,1)S(1)} collective-permute-done((bf16[520,2,128]{2,1,0:T(2,128)(2,1)}, bf16[520,2,128]{2,1,0:T(2,128)(2,1)S(1)}, u32[]{:S(2)}, u32[]{:S(2)}) %collective-permute-start.2) | collective-permute-done | bytes 266272 | tf_op jit(solution)/shard_map/ppermute | solution.py:31
  46.8 10.3 %collective-permute-start.6 = (bf16[520,2,128]{2,1,0:T(2,128)(2,1)S(1)}, bf16[520,2,128]{2,1,0:T(2,128)(2,1)}, u32[]{:S(2)}, u32[]{:S(2)}) collective-permute-start(bf16[520,2,128]{2,1,0:T(2,128)(2,1)S(1)} %copy-done.18), channel_id=1, source_target_pairs={{0,7},{1,6},{2,5},{3,4},{4,3},{5,2},{6,1},{7,0},{8,15},{9,14},{10,... | collective-permute-start | bytes 798728 | tf_op jit(solution)/shard_map/ppermute | solution.py:31
  58.5 30.4 %attend_first.1 = (f32[4,1024,256]{2,1,0:T(8,128)}, f32[4,1024,128]{2,1,0:T(8,128)}) custom-call(s32[5]{0:T(128)} %stack.24.place, bf16[8,1040,128]{2,1,0:T(8,128)(2,1)} %bitcast.20, bf16[4,1024,128]{2,1,0:T(8,128)(2,1)} %query_rows.1.refs_1_.refs_8_), custom_call_target="tpu_custom_call" | custom-call | flops 17179869184 | bytes 4259840 | tf_op jit(solution)/shard_map/attend_first/pallas_call | solution.py:519
  89.7 13.5 %attend_last.3 = (bf16[1072,128]{1,0:T(8,128)(2,1)}, bf16[1072,128]{1,0:T(8,128)(2,1)}) custom-call(s32[5]{0:T(128)} %stack.24.place, bf16[1040,128]{1,0:T(8,128)(2,1)} %bitcast.23, bf16[1040,128]{1,0:T(8,128)(2,1)} %bitcast.25, bf16[1040,128]{1,0:T(8,128)(2,1)} %bitcast.27, bf16[1040,128]{1,0:T(8,128)(2,1)} %bitcast.29, bf16[1040,128]{1,0:T(8,128)(2,1)} %bitcast.31, ...), custom_call_target="tpu_custom_call" | custom-call | flops 8589934592 | bytes 4259840 | tf_op jit(solution)/shard_map/attend_last/pallas_call | solution.py:519
  104.8 3.1 %collective-permute-start.17 = (bf16[1072,128]{1,0:T(8,128)(2,1)}, bf16[1072,128]{1,0:T(8,128)(2,1)S(1)}, u32[]{:S(2)}, u32[]{:S(2)}) collective-permute-start(bf16[1072,128]{1,0:T(8,128)(2,1)} %get-tuple-element.48), channel_id=1, source_target_pairs={{0,1},{1,9},{2,3},{3,11},{4,5},{5,13},{6,7},{7,15},{8,0},{9,8},{10... | collective-permute-start | bytes 823304 | tf_op jit(solution)/shard_map/ppermute | solution.py:31
  107.9 13.6 %attend_last.2 = (bf16[1072,128]{1,0:T(8,128)(2,1)}, bf16[1072,128]{1,0:T(8,128)(2,1)}) custom-call(s32[5]{0:T(128)} %stack.24.place, bf16[1040,128]{1,0:T(8,128)(2,1)} %bitcast.24, bf16[1040,128]{1,0:T(8,128)(2,1)} %bitcast.26, bf16[1040,128]{1,0:T(8,128)(2,1)} %bitcast.28, bf16[1040,128]{1,0:T(8,128)(2,1)} %bitcast.30, bf16[1040,128]{1,0:T(8,128)(2,1)} %bitcast.32, ...), custom_call_target="tpu_custom_call" | custom-call | flops 8589934592 | bytes 4259840 | tf_op jit(solution)/shard_map/attend_last/pallas_call | solution.py:519
  123.5 3.7 %outgoing_pages.1 = (bf16[128,2,1024]{2,1,0:T(2,128)(2,1)}, bf16[128,2,1024]{2,1,0:T(2,128)(2,1)}, bf16[128,2,1024]{2,1,0:T(2,128)(2,1)}, bf16[128,2,1024]{2,1,0:T(2,128)(2,1)}) custom-call(s32[4]{0:T(128)} %bitcast.21, bf16[8,128,2,1024]{3,2,1,0:T(2,128)(2,1)} %kv_ref.7), custom_call_target="tpu_custom_call" | custom-call | tf_op jit(solution)/shard_map/outgoing_pages/pallas_call | solution.py:127
  131.1 6.3 %project.6 = (f32[64,4096]{1,0:T(8,128)}, bf16[64,4096]{1,0:T(8,128)(2,1)}, bf16[128,1024]{1,0:T(8,128)(2,1)}) custom-call(bf16[1072,128]{1,0:T(8,128)(2,1)} %copy-done.9, bf16[1072,128]{1,0:T(8,128)(2,1)} %copy-done.10, bf16[512,8192]{1,0:T(8,128)(2,1)} %refs_1_.3, bf16[512,8192]{1,0:T(8,128)(2,1)} %collective-permute-done.9.refs_3_.refs_2_), custom_call_target="tpu_custom_call" | custom-call | flops 1073741824 | bytes 8388608 | tf_op jit(solution)/shard_map/project/pallas_call | solution.py:633
  138.5 6.3 %project.4 = (f32[64,4096]{1,0:T(8,128)}, bf16[64,4096]{1,0:T(8,128)(2,1)}, bf16[128,1024]{1,0:T(8,128)(2,1)}) custom-call(bf16[1072,128]{1,0:T(8,128)(2,1)} %copy-done.11, bf16[1072,128]{1,0:T(8,128)(2,1)} %copy-done.12, bf16[512,8192]{1,0:T(8,128)(2,1)} %refs_1_.3, bf16[512,8192]{1,0:T(8,128)(2,1)} %collective-permute-done.9.refs_3_.refs_2_), custom_call_target="tpu_custom_call" | custom-call | flops 1073741824 | bytes 8388608 | tf_op jit(solution)/shard_map/project/pallas_call | solution.py:633
  144.9 6.2 %project.5 = (f32[64,4096]{1,0:T(8,128)}, bf16[64,4096]{1,0:T(8,128)(2,1)}) custom-call(bf16[128,1024]{1,0:T(8,128)(2,1)} %get-tuple-element.44.refs_0_, bf16[512,8192]{1,0:T(8,128)(2,1)} %refs_1_.3, bf16[512,8192]{1,0:T(8,128)(2,1)} %collective-permute-done.9.refs_3_.refs_2_), custom_call_target="tpu_custom_call" | custom-call | flops 1073741824 | bytes 8388608 | tf_op jit(solution)/shard_map/project/pallas_call | solution.py:633
  151.1 6.2 %project.7 = (f32[64,4096]{1,0:T(8,128)}, bf16[64,4096]{1,0:T(8,128)(2,1)}) custom-call(bf16[128,1024]{1,0:T(8,128)(2,1)} %get-tuple-element.51.refs_0_, bf16[512,8192]{1,0:T(8,128)(2,1)} %refs_1_.3, bf16[512,8192]{1,0:T(8,128)(2,1)} %collective-permute-done.9.refs_3_.refs_2_), custom_call_target="tpu_custom_call" | custom-call | flops 1073741824 | bytes 8388608 | tf_op jit(solution)/shard_map/project/pallas_call | solution.py:633
  160.4 6.5 %collective-permute-start.21 = (bf16[64,4096]{1,0:T(8,128)(2,1)}, bf16[64,4096]{1,0:T(8,128)(2,1)}, u32[]{:S(2)}, u32[]{:S(2)}) collective-permute-start(bf16[64,4096]{1,0:T(8,128)(2,1)} %get-tuple-element.53.refs_4_), channel_id=1, source_target_pairs={{0,2},{1,3},{2,0},{3,1},{4,6},{5,7},{6,4},{7,5},{8,10},{9,11},{10,... | collective-permute-start | bytes 1572872 | tf_op jit(solution)/shard_map/ppermute | solution.py:31
  167.7 4.0 %arrange_pages.1 = bf16[8,128,2,1024]{3,2,1,0:T(2,128)(2,1)} custom-call(s32[8]{0:T(128)} %page_after.1, s32[4]{0:T(128)} %bitcast.22, bf16[8,128,2,1024]{3,2,1,0:T(2,128)(2,1)} %kv_ref.7, bf16[128,2,1024]{2,1,0:T(2,128)(2,1)} %copy-done.5, bf16[128,2,1024]{2,1,0:T(2,128)(2,1)} %copy-done.6, bf16[128,2,1024]{2,1,0:T(2,128)(2,1)} %copy-done.7, ...), custom_call_target="tpu_custom_call" | custom-call | tf_op jit(solution)/shard_map/arrange_pages/pallas_call | solution.py:185
  173.1 5.1 %collective-permute-done.10 = bf16[64,4096]{1,0:T(8,128)(2,1)} collective-permute-done((bf16[64,4096]{1,0:T(8,128)(2,1)}, bf16[64,4096]{1,0:T(8,128)(2,1)}, u32[]{:S(2)}, u32[]{:S(2)}) %collective-permute-start.10) | collective-permute-done | bytes 524320 | tf_op jit(solution)/shard_map/ppermute | solution.py:31
  180.7 4.9 %collective-permute-start.14 = (bf16[32,4096]{1,0:T(8,128)(2,1)S(1)}, bf16[32,4096]{1,0:T(8,128)(2,1)S(1)}, u32[]{:S(2)}, u32[]{:S(2)}) collective-permute-start(bf16[32,4096]{1,0:T(8,128)(2,1)S(1)} %slice.122), channel_id=1, source_target_pairs={{0,2},{1,3},{2,0},{3,1},{4,6},{5,7},{6,4},{7,5},{8,10},{9,11},{10,... | collective-permute-start | bytes 786440 | tf_op jit(solution)/shard_map/ppermute | solution.py:31
  185.7 3.9 %collective-permute-done.21 = bf16[64,4096]{1,0:T(8,128)(2,1)} collective-permute-done((bf16[64,4096]{1,0:T(8,128)(2,1)}, bf16[64,4096]{1,0:T(8,128)(2,1)}, u32[]{:S(2)}, u32[]{:S(2)}) %collective-permute-start.21) | collective-permute-done | bytes 524320 | tf_op jit(solution)/shard_map/ppermute | solution.py:31
  191.1 2.9 %collective-permute-start.12 = (bf16[16,4096]{1,0:T(8,128)(2,1)S(1)}, bf16[16,4096]{1,0:T(8,128)(2,1)S(1)}, u32[]{:S(2)}, u32[]{:S(2)}) collective-permute-start(bf16[16,4096]{1,0:T(8,128)(2,1)S(1)} %slice.127), channel_id=1, source_target_pairs={{0,8},{1,9},{2,10},{3,11},{4,12},{5,13},{6,14},{7,15},{8,0},{9,1},... | collective-permute-start | bytes 393224 | tf_op jit(solution)/shard_map/ppermute | solution.py:31
  195.1 8.9 %collective-permute-done.22 = bf16[32,4096]{1,0:T(8,128)(2,1)S(1)} collective-permute-done((bf16[32,4096]{1,0:T(8,128)(2,1)S(1)}, bf16[32,4096]{1,0:T(8,128)(2,1)S(1)}, u32[]{:S(2)}, u32[]{:S(2)}) %collective-permute-start.22) | collective-permute-done | bytes 262176 | tf_op jit(solution)/shard_map/ppermute | solution.py:31
  204.2 8.0 %collective-permute-done.12 = bf16[16,4096]{1,0:T(8,128)(2,1)S(1)} collective-permute-done((bf16[16,4096]{1,0:T(8,128)(2,1)S(1)}, bf16[16,4096]{1,0:T(8,128)(2,1)S(1)}, u32[]{:S(2)}, u32[]{:S(2)}) %collective-permute-start.12) | collective-permute-done | bytes 131104 | tf_op jit(solution)/shard_map/ppermute | solution.py:31
  (111 shorter events, 35.9 us)
Async XLA Ops:
  0.6 127.9 %collective-permute-start.9 = (bf16[512,8192]{1,0:T(8,128)(2,1)}, bf16[512,8192]{1,0:T(8,128)(2,1)}, u32[]{:S(2)}, u32[]{:S(2)}) collective-permute-start(bf16[512,8192]{1,0:T(8,128)(2,1)} %refs_1_.3), channel_id=1, source_target_pairs={{0,1},{1,0},{2,3},{3,2},{4,5},{5,4},{6,7},{7,6},{8,9},{9,8},{10,11... | collective-permute-start | bytes 25165832 | tf_op jit(solution)/shard_map/ppermute | solution.py:31
  6.0 51.1 %all-to-all-start = ((bf16[8,520,2,128]{3,2,1,0:T(2,128)(2,1)}), bf16[8,520,2,128]{3,2,1,0:T(2,128)(2,1)S(1)}, u32[]{:S(2)}, u32[]{:S(2)}) async-start(bf16[8,520,2,128]{3,2,1,0:T(2,128)(2,1)} %split_heads.3), calls=%async_computation | async-start | bytes 4259840 | tf_op jit(solution)/shard_map/all_to_all | solution.py:665
  17.0 25.2 %collective-permute-start.1 = (bf16[520,2,128]{2,1,0:T(2,128)(2,1)}, bf16[520,2,128]{2,1,0:T(2,128)(2,1)S(1)}, u32[]{:S(2)}, u32[]{:S(2)}) collective-permute-start(bf16[520,2,128]{2,1,0:T(2,128)(2,1)} %get-tuple-element.32), channel_id=1, source_target_pairs={{0,2},{1,3},{2,0},{3,1},{4,6},{5,7},{6,4},{7,5},{8,10},{9,11},{10,... | collective-permute-start | bytes 798728 | tf_op jit(solution)/shard_map/ppermute | solution.py:31
  18.7 28.1 %collective-permute-start.2 = (bf16[520,2,128]{2,1,0:T(2,128)(2,1)}, bf16[520,2,128]{2,1,0:T(2,128)(2,1)S(1)}, u32[]{:S(2)}, u32[]{:S(2)}) collective-permute-start(bf16[520,2,128]{2,1,0:T(2,128)(2,1)} %get-tuple-element.33), channel_id=1, source_target_pairs={{0,3},{1,2},{2,1},{3,0},{4,7},{5,6},{6,5},{7,4},{8,11},{9,10},{10,... | collective-permute-start | bytes 798728 | tf_op jit(solution)/shard_map/ppermute | solution.py:31
  18.7 70.3 %collective-permute-start.3 = (bf16[520,2,128]{2,1,0:T(2,128)(2,1)}, bf16[520,2,128]{2,1,0:T(2,128)(2,1)S(1)}, u32[]{:S(2)}, u32[]{:S(2)}) collective-permute-start(bf16[520,2,128]{2,1,0:T(2,128)(2,1)} %get-tuple-element.34), channel_id=1, source_target_pairs={{0,4},{1,5},{2,6},{3,7},{4,0},{5,1},{6,2},{7,3},{8,12},{9,13},{10,... | collective-permute-start | bytes 798728 | tf_op jit(solution)/shard_map/ppermute | solution.py:31
  24.7 64.2 %collective-permute-start.4 = (bf16[520,2,128]{2,1,0:T(2,128)(2,1)}, bf16[520,2,128]{2,1,0:T(2,128)(2,1)}, u32[]{:S(2)}, u32[]{:S(2)}) collective-permute-start(bf16[520,2,128]{2,1,0:T(2,128)(2,1)} %get-tuple-element.35), channel_id=1, source_target_pairs={{0,5},{1,4},{2,7},{3,6},{4,1},{5,0},{6,3},{7,2},{8,13},{9,12},{10,... | collective-permute-start | bytes 798728 | tf_op jit(solution)/shard_map/ppermute | solution.py:31
  42.2 46.7 %collective-permute-start.5 = (bf16[520,2,128]{2,1,0:T(2,128)(2,1)}, bf16[520,2,128]{2,1,0:T(2,128)(2,1)}, u32[]{:S(2)}, u32[]{:S(2)}) collective-permute-start(bf16[520,2,128]{2,1,0:T(2,128)(2,1)} %get-tuple-element.36), channel_id=1, source_target_pairs={{0,6},{1,7},{2,4},{3,5},{4,2},{5,3},{6,0},{7,1},{8,14},{9,15},{10,... | collective-permute-start | bytes 798728 | tf_op jit(solution)/shard_map/ppermute | solution.py:31
  46.8 42.2 %collective-permute-start.6 = (bf16[520,2,128]{2,1,0:T(2,128)(2,1)S(1)}, bf16[520,2,128]{2,1,0:T(2,128)(2,1)}, u32[]{:S(2)}, u32[]{:S(2)}) collective-permute-start(bf16[520,2,128]{2,1,0:T(2,128)(2,1)S(1)} %copy-done.18), channel_id=1, source_target_pairs={{0,7},{1,6},{2,5},{3,4},{4,3},{5,2},{6,1},{7,0},{8,15},{9,14},{10,... | collective-permute-start | bytes 798728 | tf_op jit(solution)/shard_map/ppermute | solution.py:31
  103.2 24.0 %collective-permute-start.16 = (bf16[1072,128]{1,0:T(8,128)(2,1)}, bf16[1072,128]{1,0:T(8,128)(2,1)S(1)}, u32[]{:S(2)}, u32[]{:S(2)}) collective-permute-start(bf16[1072,128]{1,0:T(8,128)(2,1)} %get-tuple-element.47), channel_id=1, source_target_pairs={{0,0},{1,8},{2,2},{3,10},{4,4},{5,12},{6,6},{7,14},{8,1},{9,9},{10... | collective-permute-start | bytes 823304 | tf_op jit(solution)/shard_map/ppermute | solution.py:31
  104.8 22.5 %collective-permute-start.17 = (bf16[1072,128]{1,0:T(8,128)(2,1)}, bf16[1072,128]{1,0:T(8,128)(2,1)S(1)}, u32[]{:S(2)}, u32[]{:S(2)}) collective-permute-start(bf16[1072,128]{1,0:T(8,128)(2,1)} %get-tuple-element.48), channel_id=1, source_target_pairs={{0,1},{1,9},{2,3},{3,11},{4,5},{5,13},{6,7},{7,15},{8,0},{9,8},{10... | collective-permute-start | bytes 823304 | tf_op jit(solution)/shard_map/ppermute | solution.py:31
  123.1 14.3 %collective-permute-start.8 = (bf16[1072,128]{1,0:T(8,128)(2,1)}, bf16[1072,128]{1,0:T(8,128)(2,1)S(1)}, u32[]{:S(2)}, u32[]{:S(2)}) collective-permute-start(bf16[1072,128]{1,0:T(8,128)(2,1)} %get-tuple-element.41), channel_id=1, source_target_pairs={{0,1},{1,9},{2,3},{3,11},{4,5},{5,13},{6,7},{7,15},{8,0},{9,8},{10... | collective-permute-start | bytes 823304 | tf_op jit(solution)/shard_map/ppermute | solution.py:31
  127.2 30.0 %collective-permute-start.24 = (bf16[128,2,1024]{2,1,0:T(2,128)(2,1)}, bf16[128,2,1024]{2,1,0:T(2,128)(2,1)S(1)}, u32[]{:S(2)}, u32[]{:S(2)}) collective-permute-start(bf16[128,2,1024]{2,1,0:T(2,128)(2,1)} %get-tuple-element.54), channel_id=1, source_target_pairs={{0,1},{1,2},{2,3},{3,4},{4,5},{5,6},{6,7},{7,8},{8,9},{9,10},{10,1... | collective-permute-start | bytes 1572872 | tf_op jit(solution)/shard_map/ppermute | solution.py:31
  127.3 31.0 %collective-permute-start.25 = (bf16[128,2,1024]{2,1,0:T(2,128)(2,1)}, bf16[128,2,1024]{2,1,0:T(2,128)(2,1)S(1)}, u32[]{:S(2)}, u32[]{:S(2)}) collective-permute-start(bf16[128,2,1024]{2,1,0:T(2,128)(2,1)} %get-tuple-element.55), channel_id=1, source_target_pairs={{0,2},{1,3},{2,4},{3,5},{4,6},{5,7},{6,8},{7,9},{8,10},{9,11},{10,... | collective-permute-start | bytes 1572872 | tf_op jit(solution)/shard_map/ppermute | solution.py:31
  127.4 33.0 %collective-permute-start.26 = (bf16[128,2,1024]{2,1,0:T(2,128)(2,1)}, bf16[128,2,1024]{2,1,0:T(2,128)(2,1)S(1)}, u32[]{:S(2)}, u32[]{:S(2)}) collective-permute-start(bf16[128,2,1024]{2,1,0:T(2,128)(2,1)} %get-tuple-element.56), channel_id=1, source_target_pairs={{0,3},{1,4},{2,5},{3,6},{4,7},{5,8},{6,9},{7,10},{8,11},{9,12},{10... | collective-permute-start | bytes 1572872 | tf_op jit(solution)/shard_map/ppermute | solution.py:31
  128.5 38.4 %collective-permute-start.27 = (bf16[128,2,1024]{2,1,0:T(2,128)(2,1)}, bf16[128,2,1024]{2,1,0:T(2,128)(2,1)S(1)}, u32[]{:S(2)}, u32[]{:S(2)}) collective-permute-start(bf16[128,2,1024]{2,1,0:T(2,128)(2,1)} %get-tuple-element.57), channel_id=1, source_target_pairs={{0,4},{1,5},{2,6},{3,7},{4,8},{5,9},{6,10},{7,11},{8,12},{9,13},{1... | collective-permute-start | bytes 1572872 | tf_op jit(solution)/shard_map/ppermute | solution.py:31
  137.4 34.3 %collective-permute-start.18 = (bf16[64,4096]{1,0:T(8,128)(2,1)}, bf16[64,4096]{1,0:T(8,128)(2,1)}, u32[]{:S(2)}, u32[]{:S(2)}) collective-permute-start(bf16[64,4096]{1,0:T(8,128)(2,1)} %get-tuple-element.50), channel_id=1, source_target_pairs={{0,2},{1,3},{2,0},{3,1},{4,6},{5,7},{6,4},{7,5},{8,10},{9,11},{10,... | collective-permute-start | bytes 1572872 | tf_op jit(solution)/shard_map/ppermute | solution.py:31
  157.2 21.0 %collective-permute-start.10 = (bf16[64,4096]{1,0:T(8,128)(2,1)}, bf16[64,4096]{1,0:T(8,128)(2,1)}, u32[]{:S(2)}, u32[]{:S(2)}) collective-permute-start(bf16[64,4096]{1,0:T(8,128)(2,1)} %get-tuple-element.43), channel_id=1, source_target_pairs={{0,2},{1,3},{2,0},{3,1},{4,6},{5,7},{6,4},{7,5},{8,10},{9,11},{10,... | collective-permute-start | bytes 1572872 | tf_op jit(solution)/shard_map/ppermute | solution.py:31
  158.3 21.2 %collective-permute-start.13 = (bf16[64,4096]{1,0:T(8,128)(2,1)}, bf16[64,4096]{1,0:T(8,128)(2,1)}, u32[]{:S(2)}, u32[]{:S(2)}) collective-permute-start(bf16[64,4096]{1,0:T(8,128)(2,1)} %get-tuple-element.46), channel_id=1, source_target_pairs={{0,4},{1,5},{2,6},{3,7},{4,0},{5,1},{6,2},{7,3},{8,12},{9,13},{10,... | collective-permute-start | bytes 1572872 | tf_op jit(solution)/shard_map/ppermute | solution.py:31
  160.4 29.1 %collective-permute-start.21 = (bf16[64,4096]{1,0:T(8,128)(2,1)}, bf16[64,4096]{1,0:T(8,128)(2,1)}, u32[]{:S(2)}, u32[]{:S(2)}) collective-permute-start(bf16[64,4096]{1,0:T(8,128)(2,1)} %get-tuple-element.53.refs_4_), channel_id=1, source_target_pairs={{0,2},{1,3},{2,0},{3,1},{4,6},{5,7},{6,4},{7,5},{8,10},{9,11},{10,... | collective-permute-start | bytes 1572872 | tf_op jit(solution)/shard_map/ppermute | solution.py:31
  173.1 17.7 %collective-permute-start.19 = (bf16[32,4096]{1,0:T(8,128)(2,1)S(1)}, bf16[32,4096]{1,0:T(8,128)(2,1)S(1)}, u32[]{:S(2)}, u32[]{:S(2)}) collective-permute-start(bf16[32,4096]{1,0:T(8,128)(2,1)S(1)} %slice.121), channel_id=1, source_target_pairs={{0,4},{1,5},{2,6},{3,7},{4,0},{5,1},{6,2},{7,3},{8,12},{9,13},{10,... | collective-permute-start | bytes 786440 | tf_op jit(solution)/shard_map/ppermute | solution.py:31
  180.7 14.2 %collective-permute-start.14 = (bf16[32,4096]{1,0:T(8,128)(2,1)S(1)}, bf16[32,4096]{1,0:T(8,128)(2,1)S(1)}, u32[]{:S(2)}, u32[]{:S(2)}) collective-permute-start(bf16[32,4096]{1,0:T(8,128)(2,1)S(1)} %slice.122), channel_id=1, source_target_pairs={{0,2},{1,3},{2,0},{3,1},{4,6},{5,7},{6,4},{7,5},{8,10},{9,11},{10,... | collective-permute-start | bytes 786440 | tf_op jit(solution)/shard_map/ppermute | solution.py:31
  190.7 13.3 %collective-permute-start.22 = (bf16[32,4096]{1,0:T(8,128)(2,1)S(1)}, bf16[32,4096]{1,0:T(8,128)(2,1)S(1)}, u32[]{:S(2)}, u32[]{:S(2)}) collective-permute-start(bf16[32,4096]{1,0:T(8,128)(2,1)S(1)} %slice.120), channel_id=1, source_target_pairs={{0,4},{1,5},{2,6},{3,7},{4,0},{5,1},{6,2},{7,3},{8,12},{9,13},{10,... | collective-permute-start | bytes 786440 | tf_op jit(solution)/shard_map/ppermute | solution.py:31
  191.1 21.2 %collective-permute-start.12 = (bf16[16,4096]{1,0:T(8,128)(2,1)S(1)}, bf16[16,4096]{1,0:T(8,128)(2,1)S(1)}, u32[]{:S(2)}, u32[]{:S(2)}) collective-permute-start(bf16[16,4096]{1,0:T(8,128)(2,1)S(1)} %slice.127), channel_id=1, source_target_pairs={{0,8},{1,9},{2,10},{3,11},{4,12},{5,13},{6,14},{7,15},{8,0},{9,1},... | collective-permute-start | bytes 393224 | tf_op jit(solution)/shard_map/ppermute | solution.py:31
  195.0 20.0 %collective-permute-start.15 = (bf16[16,4096]{1,0:T(8,128)(2,1)S(1)}, bf16[16,4096]{1,0:T(8,128)(2,1)S(1)}, u32[]{:S(2)}, u32[]{:S(2)}) collective-permute-start(bf16[16,4096]{1,0:T(8,128)(2,1)S(1)} %slice.126), channel_id=1, source_target_pairs={{0,8},{1,9},{2,10},{3,11},{4,12},{5,13},{6,14},{7,15},{8,0},{9,1},... | collective-permute-start | bytes 393224 | tf_op jit(solution)/shard_map/ppermute | solution.py:31
  (24 other events, 329.2 us)

commit v4 on v1

--- a/solution.py
+++ b/solution.py
@@ -21,7 +21,7 @@
 
 WIDE = 16
 NARROW = 8
-FIRST_SLOTS = 3
+FIRST_SLOTS = 5
 COLUMN_PARTS = 2
 
 ANY = pl.BlockSpec(memory_space=pl.ANY)
@@ -577,7 +577,7 @@
     send_ref[...] = send.astype(jnp.bfloat16)
 
 
-def project(parts, ws, tok, column_part, y_first, width=1024):
+def project(parts, ws, tok, column_part, y_first, width=2048):
     columns = ws[0].shape[1] // COLUMN_PARTS
     steps = columns // width
     fixed = lambda i: (0, 0)
@@ -667,7 +667,7 @@
     for b in range(2):
         merged = partial[b]
         for c in range(COLUMN_PARTS):
-            y_first = (b, c) != (1, 1)
+            y_first = (b, c) != (0, 1)
             keep, send, *a = project(merged, ws, tok, c, y_first)
             if a:
                 merged = a

time: 235 us -> 239 us (1.017)
  the two profiles are of different devices: /device:TPU:2 before, /device:TPU:0 now
where the time goes in v4:
time: 239 us; the launch traced here: 238 us
  Pallas kernels  92.7 us (39%)
  starting transfers between devices  77.5 us (32%)
  waiting for transfers between devices  55.3 us (23%)
  other arithmetic  8.46 us (4%)
  local copies, waits for them, and re-layouts  2.86 us (1%)
    ppermute x21, starting transfers between devices, permute_to(): return lax.ppermute(x, 'pages', [(i, target(i)) for i in range(n)])  68 us
    pallas_call x3, Pallas kernels, attend(): pl.pallas_call(functools.partial(attend_kernel, first_slot=first_slot, fi...  53.8 us
    all_to_all x2, waiting for transfers between devices, exchange(): lax.all_to_all(x, 'pages', 0, 0, axis_index_groups=groups, tiled=True)  28.4 us
    ppermute x21, waiting for transfers between devices, permute_to(): return lax.ppermute(x, 'pages', [(i, target(i)) for i in range(n)])  26.9 us
    pallas_call x4, Pallas kernels, project(): pl.pallas_call(functools.partial(project_kernel, n_parts=len(parts), n_ws...  21.2 us
    all_to_all x2, starting transfers between devices, exchange(): lax.all_to_all(x, 'pages', 0, 0, axis_index_groups=groups, tiled=True)  9.59 us
    pallas_call x2, Pallas kernels, split_heads(): pl.pallas_call(functools.partial(split_heads_kernel, first=first, count=c...  6.32 us
    add x8, other arithmetic, local(): total = keep + got.astype(jnp.float32)  4.86 us
  transfers between devices with their start and end apart: 23, of which 8 were waited for; matrix products, arithmetic and copies ran while one was open for 3% of the time, Pallas kernels for 37%

profile of v4, /device:TPU:0, one launch (start us, length us, event | category | flops | bytes accessed | tf_op | source)
XLA Modules:
  0.0 237.9 jit_solution(7138284524817176937)
XLA Ops:
  2.0 3.6 %split_heads.3 = bf16[8,648,2,128]{3,2,1,0:T(2,128)(2,1)} custom-call(bf16[8,128,2,1024]{3,2,1,0:T(2,128)(2,1)} %kv_ref.7, bf16[8,2,128]{2,1,0:T(2,128)(2,1)} %broadcast_in_dim.2.ids_ref), custom_call_target="tpu_custom_call" | custom-call | tf_op jit(solution)/shard_map/split_heads/pallas_call | solution.py:79
  5.5 5.3 %all-to-all-start.1 = ((bf16[8,648,2,128]{3,2,1,0:T(2,128)(2,1)}), bf16[8,648,2,128]{3,2,1,0:T(2,128)(2,1)S(1)}, u32[]{:S(2)}, u32[]{:S(2)}) async-start(bf16[8,648,2,128]{3,2,1,0:T(2,128)(2,1)} %split_heads.3), calls=%async_computation.1 | async-start | bytes 5308416 | tf_op jit(solution)/shard_map/all_to_all | solution.py:630
  11.3 2.7 %split_heads.2 = bf16[8,392,2,128]{3,2,1,0:T(2,128)(2,1)} custom-call(bf16[8,128,2,1024]{3,2,1,0:T(2,128)(2,1)} %kv_ref.7, bf16[8,2,128]{2,1,0:T(2,128)(2,1)} %broadcast_in_dim.2.ids_ref), custom_call_target="tpu_custom_call" | custom-call | tf_op jit(solution)/shard_map/split_heads/pallas_call | solution.py:79
  14.1 28.4 %all-to-all-done.1 = bf16[8,648,2,128]{3,2,1,0:T(2,128)(2,1)S(1)} async-done(((bf16[8,648,2,128]{3,2,1,0:T(2,128)(2,1)}), bf16[8,648,2,128]{3,2,1,0:T(2,128)(2,1)S(1)}, u32[]{:S(2)}, u32[]{:S(2)}) %all-to-all-start.1) | async-done | bytes 2654240 | tf_op jit(solution)/shard_map/all_to_all | solution.py:630
  42.5 4.3 %all-to-all-start = ((bf16[8,392,2,128]{3,2,1,0:T(2,128)(2,1)}), bf16[8,392,2,128]{3,2,1,0:T(2,128)(2,1)}, u32[]{:S(2)}, u32[]{:S(2)}) async-start(bf16[8,392,2,128]{3,2,1,0:T(2,128)(2,1)} %split_heads.2), calls=%async_computation | async-start | bytes 3211264 | tf_op jit(solution)/shard_map/all_to_all | solution.py:630
  49.3 4.3 %query_rows.1.q_ref = bf16[4,1024,128]{2,1,0:T(8,128)(2,1)} custom-call(s32[4]{0:T(128)} %pad_add_fusion.place, bf16[2,256,8192]{2,1,0:T(8,128)(2,1)} %q_ref.1), custom_call_target="tpu_custom_call" | custom-call | tf_op jit(solution)/shard_map/query_rows/pallas_call | solution.py:219
  53.7 35.6 %attend_first.1 = (f32[4,1024,256]{2,1,0:T(8,128)}, f32[4,1024,128]{2,1,0:T(8,128)}) custom-call(s32[4]{0:T(128)} %pad_add_fusion.place, bf16[8,1296,128]{2,1,0:T(8,128)(2,1)} %bitcast.12, bf16[4,1024,128]{2,1,0:T(8,128)(2,1)} %query_rows.1.q_ref), custom_call_target="tpu_custom_call" | custom-call | flops 21474836480 | bytes 2654208 | tf_op jit(solution)/shard_map/attend_first/pallas_call | solution.py:488
  89.2 9.1 %attend_last.3 = (bf16[1072,128]{1,0:T(8,128)(2,1)}, bf16[1072,128]{1,0:T(8,128)(2,1)}) custom-call(s32[4]{0:T(128)} %pad_add_fusion.place, bf16[8,784,128]{2,1,0:T(8,128)(2,1)} %bitcast.4.x_ref, bf16[4,1024,128]{2,1,0:T(8,128)(2,1)} %query_rows.1.q_ref, f32[4,1024,256]{2,1,0:T(8,128)} %get-tuple-element.22.refs_0_, f32[4,1024,128]{2,1,0:T(8,128)} %get-tuple-element.23.refs_1_), custom_call_target="tpu_custom_call" | custom-call | flops 6442450944 | bytes 1605632 | tf_op jit(solution)/shard_map/attend_last/pallas_call | solution.py:488
  100.0 3.1 %collective-permute-start.10 = (bf16[1072,128]{1,0:T(8,128)(2,1)}, bf16[1072,128]{1,0:T(8,128)(2,1)S(1)}, u32[]{:S(2)}, u32[]{:S(2)}) collective-permute-start(bf16[1072,128]{1,0:T(8,128)(2,1)} %get-tuple-element.32), channel_id=1, source_target_pairs={{0,1},{1,9},{2,3},{3,11},{4,5},{5,13},{6,7},{7,15},{8,0},{9,8},{10... | collective-permute-start | bytes 823304 | tf_op jit(solution)/shard_map/ppermute | solution.py:31
  103.0 9.1 %attend_last.2 = (bf16[1072,128]{1,0:T(8,128)(2,1)}, bf16[1072,128]{1,0:T(8,128)(2,1)}) custom-call(s32[4]{0:T(128)} %pad_add_fusion.place, bf16[8,784,128]{2,1,0:T(8,128)(2,1)} %bitcast.4.x_ref, bf16[4,1024,128]{2,1,0:T(8,128)(2,1)} %query_rows.1.q_ref, f32[4,1024,256]{2,1,0:T(8,128)} %get-tuple-element.22.refs_0_, f32[4,1024,128]{2,1,0:T(8,128)} %get-tuple-element.23.refs_1_), custom_call_target="tpu_custom_call" | custom-call | flops 6442450944 | bytes 1605632 | tf_op jit(solution)/shard_map/attend_last/pallas_call | solution.py:488
  114.4 3.1 %outgoing_pages.1 = (bf16[128,2,1024]{2,1,0:T(2,128)(2,1)}, bf16[128,2,1024]{2,1,0:T(2,128)(2,1)}, bf16[128,2,1024]{2,1,0:T(2,128)(2,1)}, bf16[128,2,1024]{2,1,0:T(2,128)(2,1)}) custom-call(s32[4]{0:T(128)} %bitcast.13, bf16[8,128,2,1024]{3,2,1,0:T(2,128)(2,1)} %kv_ref.7), custom_call_target="tpu_custom_call" | custom-call | tf_op jit(solution)/shard_map/outgoing_pages/pallas_call | solution.py:116
  120.0 42.2 %collective-permute-start.19 = (bf16[128,2,1024]{2,1,0:T(2,128)(2,1)}, bf16[128,2,1024]{2,1,0:T(2,128)(2,1)S(1)}, u32[]{:S(2)}, u32[]{:S(2)}) collective-permute-start(bf16[128,2,1024]{2,1,0:T(2,128)(2,1)} %get-tuple-element.40), channel_id=1, source_target_pairs={{0,3},{1,4},{2,5},{3,6},{4,7},{5,8},{6,9},{7,10},{8,11},{9,12},{10... | collective-permute-start | bytes 1572872 | tf_op jit(solution)/shard_map/ppermute | solution.py:31
  162.2 5.5 %project.6 = (f32[64,4096]{1,0:T(8,128)}, bf16[64,4096]{1,0:T(8,128)(2,1)}, bf16[128,1024]{1,0:T(8,128)(2,1)}) custom-call(bf16[1072,128]{1,0:T(8,128)(2,1)} %copy-done.9, bf16[1072,128]{1,0:T(8,128)(2,1)} %copy-done.11, bf16[512,8192]{1,0:T(8,128)(2,1)} %refs_1_.3, bf16[512,8192]{1,0:T(8,128)(2,1)} %collective-permute-done.2.refs_3_.refs_2_), custom_call_target="tpu_custom_call" | custom-call | flops 1073741824 | bytes 8388608 | tf_op jit(solution)/shard_map/project/pallas_call | solution.py:598
  168.4 5.3 %project.4 = (f32[64,4096]{1,0:T(8,128)}, bf16[64,4096]{1,0:T(8,128)(2,1)}, bf16[128,1024]{1,0:T(8,128)(2,1)}) custom-call(bf16[1072,128]{1,0:T(8,128)(2,1)} %copy-done.10, bf16[1072,128]{1,0:T(8,128)(2,1)} %copy-done.12, bf16[512,8192]{1,0:T(8,128)(2,1)} %refs_1_.3, bf16[512,8192]{1,0:T(8,128)(2,1)} %collective-permute-done.2.refs_3_.refs_2_), custom_call_target="tpu_custom_call" | custom-call | flops 1073741824 | bytes 8388608 | tf_op jit(solution)/shard_map/project/pallas_call | solution.py:598
  173.7 5.2 %project.5 = (f32[64,4096]{1,0:T(8,128)}, bf16[64,4096]{1,0:T(8,128)(2,1)}) custom-call(bf16[128,1024]{1,0:T(8,128)(2,1)} %get-tuple-element.28.refs_0_, bf16[512,8192]{1,0:T(8,128)(2,1)} %refs_1_.3, bf16[512,8192]{1,0:T(8,128)(2,1)} %collective-permute-done.2.refs_3_.refs_2_), custom_call_target="tpu_custom_call" | custom-call | flops 1073741824 | bytes 8388608 | tf_op jit(solution)/shard_map/project/pallas_call | solution.py:598
  178.9 5.2 %project.7 = (f32[64,4096]{1,0:T(8,128)}, bf16[64,4096]{1,0:T(8,128)(2,1)}) custom-call(bf16[128,1024]{1,0:T(8,128)(2,1)} %get-tuple-element.35.refs_0_, bf16[512,8192]{1,0:T(8,128)(2,1)} %refs_1_.3, bf16[512,8192]{1,0:T(8,128)(2,1)} %collective-permute-done.2.refs_3_.refs_2_), custom_call_target="tpu_custom_call" | custom-call | flops 1073741824 | bytes 8388608 | tf_op jit(solution)/shard_map/project/pallas_call | solution.py:598
  187.3 4.0 %arrange_pages.1 = bf16[8,128,2,1024]{3,2,1,0:T(2,128)(2,1)} custom-call(s32[8]{0:T(128)} %page_after.1, s32[4]{0:T(128)} %bitcast.14, bf16[8,128,2,1024]{3,2,1,0:T(2,128)(2,1)} %kv_ref.7, bf16[128,2,1024]{2,1,0:T(2,128)(2,1)} %copy-done.5, bf16[128,2,1024]{2,1,0:T(2,128)(2,1)} %copy-done.6, bf16[128,2,1024]{2,1,0:T(2,128)(2,1)} %copy-done.7, ...), custom_call_target="tpu_custom_call" | custom-call | tf_op jit(solution)/shard_map/arrange_pages/pallas_call | solution.py:174
  194.6 4.7 %collective-permute-done.3 = bf16[64,4096]{1,0:T(8,128)(2,1)} collective-permute-done((bf16[64,4096]{1,0:T(8,128)(2,1)}, bf16[64,4096]{1,0:T(8,128)(2,1)}, u32[]{:S(2)}, u32[]{:S(2)}) %collective-permute-start.3) | collective-permute-done | bytes 524320 | tf_op jit(solution)/shard_map/ppermute | solution.py:31
  203.2 7.3 %collective-permute-done.14 = bf16[64,4096]{1,0:T(8,128)(2,1)} collective-permute-done((bf16[64,4096]{1,0:T(8,128)(2,1)}, bf16[64,4096]{1,0:T(8,128)(2,1)}, u32[]{:S(2)}, u32[]{:S(2)}) %collective-permute-start.14) | collective-permute-done | bytes 524320 | tf_op jit(solution)/shard_map/ppermute | solution.py:31
  212.0 4.2 %collective-permute-start.13 = (bf16[16,4096]{1,0:T(8,128)(2,1)S(1)}, bf16[16,4096]{1,0:T(8,128)(2,1)S(1)}, u32[]{:S(2)}, u32[]{:S(2)}) collective-permute-start(bf16[16,4096]{1,0:T(8,128)(2,1)S(1)} %slice.125), channel_id=1, source_target_pairs={{0,8},{1,9},{2,10},{3,11},{4,12},{5,13},{6,14},{7,15},{8,0},{9,1},... | collective-permute-start | bytes 393224 | tf_op jit(solution)/shard_map/ppermute | solution.py:31
  216.5 3.0 %collective-permute-start.8 = (bf16[16,4096]{1,0:T(8,128)(2,1)S(1)}, bf16[16,4096]{1,0:T(8,128)(2,1)S(1)}, u32[]{:S(2)}, u32[]{:S(2)}) collective-permute-start(bf16[16,4096]{1,0:T(8,128)(2,1)S(1)} %slice.126), channel_id=1, source_target_pairs={{0,8},{1,9},{2,10},{3,11},{4,12},{5,13},{6,14},{7,15},{8,0},{9,1},... | collective-permute-start | bytes 393224 | tf_op jit(solution)/shard_map/ppermute | solution.py:31
  220.9 2.5 %collective-permute-start.16 = (bf16[16,4096]{1,0:T(8,128)(2,1)S(1)}, bf16[16,4096]{1,0:T(8,128)(2,1)S(1)}, u32[]{:S(2)}, u32[]{:S(2)}) collective-permute-start(bf16[16,4096]{1,0:T(8,128)(2,1)S(1)} %slice.124), channel_id=1, source_target_pairs={{0,8},{1,9},{2,10},{3,11},{4,12},{5,13},{6,14},{7,15},{8,0},{9,1},... | collective-permute-start | bytes 393224 | tf_op jit(solution)/shard_map/ppermute | solution.py:31
  223.4 6.9 %collective-permute-done.13 = bf16[16,4096]{1,0:T(8,128)(2,1)S(1)} collective-permute-done((bf16[16,4096]{1,0:T(8,128)(2,1)S(1)}, bf16[16,4096]{1,0:T(8,128)(2,1)S(1)}, u32[]{:S(2)}, u32[]{:S(2)}) %collective-permute-start.13) | collective-permute-done | bytes 131104 | tf_op jit(solution)/shard_map/ppermute | solution.py:31
  230.4 2.8 %collective-permute-done.5 = bf16[16,4096]{1,0:T(8,128)(2,1)S(1)} collective-permute-done((bf16[16,4096]{1,0:T(8,128)(2,1)S(1)}, bf16[16,4096]{1,0:T(8,128)(2,1)S(1)}, u32[]{:S(2)}, u32[]{:S(2)}) %collective-permute-start.5) | collective-permute-done | bytes 131104 | tf_op jit(solution)/shard_map/ppermute | solution.py:31
  (89 shorter events, 29.5 us)
Async XLA Ops:
  5.5 37.0 %all-to-all-start.1 = ((bf16[8,648,2,128]{3,2,1,0:T(2,128)(2,1)}), bf16[8,648,2,128]{3,2,1,0:T(2,128)(2,1)S(1)}, u32[]{:S(2)}, u32[]{:S(2)}) async-start(bf16[8,648,2,128]{3,2,1,0:T(2,128)(2,1)} %split_heads.3), calls=%async_computation.1 | async-start | bytes 5308416 | tf_op jit(solution)/shard_map/all_to_all | solution.py:630
  10.8 151.3 %collective-permute-start.2 = (bf16[512,8192]{1,0:T(8,128)(2,1)}, bf16[512,8192]{1,0:T(8,128)(2,1)}, u32[]{:S(2)}, u32[]{:S(2)}) collective-permute-start(bf16[512,8192]{1,0:T(8,128)(2,1)} %refs_1_.3), channel_id=1, source_target_pairs={{0,1},{1,0},{2,3},{3,2},{4,5},{5,4},{6,7},{7,6},{8,9},{9,8},{10,11... | collective-permute-start | bytes 25165832 | tf_op jit(solution)/shard_map/ppermute | solution.py:31
  42.5 46.7 %all-to-all-start = ((bf16[8,392,2,128]{3,2,1,0:T(2,128)(2,1)}), bf16[8,392,2,128]{3,2,1,0:T(2,128)(2,1)}, u32[]{:S(2)}, u32[]{:S(2)}) async-start(bf16[8,392,2,128]{3,2,1,0:T(2,128)(2,1)} %split_heads.2), calls=%async_computation | async-start | bytes 3211264 | tf_op jit(solution)/shard_map/all_to_all | solution.py:630
  98.3 19.2 %collective-permute-start.9 = (bf16[1072,128]{1,0:T(8,128)(2,1)}, bf16[1072,128]{1,0:T(8,128)(2,1)S(1)}, u32[]{:S(2)}, u32[]{:S(2)}) collective-permute-start(bf16[1072,128]{1,0:T(8,128)(2,1)} %get-tuple-element.31), channel_id=1, source_target_pairs={{0,0},{1,8},{2,2},{3,10},{4,4},{5,12},{6,6},{7,14},{8,1},{9,9},{10... | collective-permute-start | bytes 823304 | tf_op jit(solution)/shard_map/ppermute | solution.py:31
  100.0 17.7 %collective-permute-start.10 = (bf16[1072,128]{1,0:T(8,128)(2,1)}, bf16[1072,128]{1,0:T(8,128)(2,1)S(1)}, u32[]{:S(2)}, u32[]{:S(2)}) collective-permute-start(bf16[1072,128]{1,0:T(8,128)(2,1)} %get-tuple-element.32), channel_id=1, source_target_pairs={{0,1},{1,9},{2,3},{3,11},{4,5},{5,13},{6,7},{7,15},{8,0},{9,8},{10... | collective-permute-start | bytes 823304 | tf_op jit(solution)/shard_map/ppermute | solution.py:31
  112.2 7.8 %collective-permute-start = (bf16[1072,128]{1,0:T(8,128)(2,1)}, bf16[1072,128]{1,0:T(8,128)(2,1)S(1)}, u32[]{:S(2)}, u32[]{:S(2)}) collective-permute-start(bf16[1072,128]{1,0:T(8,128)(2,1)} %get-tuple-element.24), channel_id=1, source_target_pairs={{0,0},{1,8},{2,2},{3,10},{4,4},{5,12},{6,6},{7,14},{8,1},{9,9},{10... | collective-permute-start | bytes 823304 | tf_op jit(solution)/shard_map/ppermute | solution.py:31
  113.8 53.9 %collective-permute-start.1 = (bf16[1072,128]{1,0:T(8,128)(2,1)}, bf16[1072,128]{1,0:T(8,128)(2,1)S(1)}, u32[]{:S(2)}, u32[]{:S(2)}) collective-permute-start(bf16[1072,128]{1,0:T(8,128)(2,1)} %get-tuple-element.25), channel_id=1, source_target_pairs={{0,1},{1,9},{2,3},{3,11},{4,5},{5,13},{6,7},{7,15},{8,0},{9,8},{10... | collective-permute-start | bytes 823304 | tf_op jit(solution)/shard_map/ppermute | solution.py:31
  117.6 66.5 %collective-permute-start.17 = (bf16[128,2,1024]{2,1,0:T(2,128)(2,1)}, bf16[128,2,1024]{2,1,0:T(2,128)(2,1)S(1)}, u32[]{:S(2)}, u32[]{:S(2)}) collective-permute-start(bf16[128,2,1024]{2,1,0:T(2,128)(2,1)} %get-tuple-element.38), channel_id=1, source_target_pairs={{0,1},{1,2},{2,3},{3,4},{4,5},{5,6},{6,7},{7,8},{8,9},{9,10},{10,1... | collective-permute-start | bytes 1572872 | tf_op jit(solution)/shard_map/ppermute | solution.py:31
  117.6 67.9 %collective-permute-start.18 = (bf16[128,2,1024]{2,1,0:T(2,128)(2,1)}, bf16[128,2,1024]{2,1,0:T(2,128)(2,1)S(1)}, u32[]{:S(2)}, u32[]{:S(2)}) collective-permute-start(bf16[128,2,1024]{2,1,0:T(2,128)(2,1)} %get-tuple-element.39), channel_id=1, source_target_pairs={{0,2},{1,3},{2,4},{3,5},{4,6},{5,7},{6,8},{7,9},{8,10},{9,11},{10,... | collective-permute-start | bytes 1572872 | tf_op jit(solution)/shard_map/ppermute | solution.py:31
  120.0 47.7 %copy-start.10 = (bf16[1072,128]{1,0:T(8,128)(2,1)}, bf16[1072,128]{1,0:T(8,128)(2,1)S(1)}, u32[]{:S(2)}) copy-start(bf16[1072,128]{1,0:T(8,128)(2,1)S(1)} %collective-permute-done.refs_0_) | copy-start | bytes 823300
  120.0 65.6 %collective-permute-start.19 = (bf16[128,2,1024]{2,1,0:T(2,128)(2,1)}, bf16[128,2,1024]{2,1,0:T(2,128)(2,1)S(1)}, u32[]{:S(2)}, u32[]{:S(2)}) collective-permute-start(bf16[128,2,1024]{2,1,0:T(2,128)(2,1)} %get-tuple-element.40), channel_id=1, source_target_pairs={{0,3},{1,4},{2,5},{3,6},{4,7},{5,8},{6,9},{7,10},{8,11},{9,12},{10... | collective-permute-start | bytes 1572872 | tf_op jit(solution)/shard_map/ppermute | solution.py:31
  162.2 24.2 %collective-permute-start.20 = (bf16[128,2,1024]{2,1,0:T(2,128)(2,1)}, bf16[128,2,1024]{2,1,0:T(2,128)(2,1)S(1)}, u32[]{:S(2)}, u32[]{:S(2)}) collective-permute-start(bf16[128,2,1024]{2,1,0:T(2,128)(2,1)} %get-tuple-element.41), channel_id=1, source_target_pairs={{0,4},{1,5},{2,6},{3,7},{4,8},{5,9},{6,10},{7,11},{8,12},{9,13},{1... | collective-permute-start | bytes 1572872 | tf_op jit(solution)/shard_map/ppermute | solution.py:31
  167.7 23.6 %collective-permute-start.11 = (bf16[64,4096]{1,0:T(8,128)(2,1)}, bf16[64,4096]{1,0:T(8,128)(2,1)}, u32[]{:S(2)}, u32[]{:S(2)}) collective-permute-start(bf16[64,4096]{1,0:T(8,128)(2,1)} %get-tuple-element.34), channel_id=1, source_target_pairs={{0,2},{1,3},{2,0},{3,1},{4,6},{5,7},{6,4},{7,5},{8,10},{9,11},{10,... | collective-permute-start | bytes 1572872 | tf_op jit(solution)/shard_map/ppermute | solution.py:31
  184.1 15.2 %collective-permute-start.3 = (bf16[64,4096]{1,0:T(8,128)(2,1)}, bf16[64,4096]{1,0:T(8,128)(2,1)}, u32[]{:S(2)}, u32[]{:S(2)}) collective-permute-start(bf16[64,4096]{1,0:T(8,128)(2,1)} %get-tuple-element.27), channel_id=1, source_target_pairs={{0,2},{1,3},{2,0},{3,1},{4,6},{5,7},{6,4},{7,5},{8,10},{9,11},{10,... | collective-permute-start | bytes 1572872 | tf_op jit(solution)/shard_map/ppermute | solution.py:31
  185.6 15.1 %collective-permute-start.6 = (bf16[64,4096]{1,0:T(8,128)(2,1)}, bf16[64,4096]{1,0:T(8,128)(2,1)}, u32[]{:S(2)}, u32[]{:S(2)}) collective-permute-start(bf16[64,4096]{1,0:T(8,128)(2,1)} %get-tuple-element.30), channel_id=1, source_target_pairs={{0,4},{1,5},{2,6},{3,7},{4,0},{5,1},{6,2},{7,3},{8,12},{9,13},{10,... | collective-permute-start | bytes 1572872 | tf_op jit(solution)/shard_map/ppermute | solution.py:31
  185.6 24.9 %collective-permute-start.14 = (bf16[64,4096]{1,0:T(8,128)(2,1)}, bf16[64,4096]{1,0:T(8,128)(2,1)}, u32[]{:S(2)}, u32[]{:S(2)}) collective-permute-start(bf16[64,4096]{1,0:T(8,128)(2,1)} %get-tuple-element.37.refs_4_), channel_id=1, source_target_pairs={{0,2},{1,3},{2,0},{3,1},{4,6},{5,7},{6,4},{7,5},{8,10},{9,11},{10,... | collective-permute-start | bytes 1572872 | tf_op jit(solution)/shard_map/ppermute | solution.py:31
  192.6 19.3 %collective-permute-start.12 = (bf16[32,4096]{1,0:T(8,128)(2,1)S(1)}, bf16[32,4096]{1,0:T(8,128)(2,1)S(1)}, u32[]{:S(2)}, u32[]{:S(2)}) collective-permute-start(bf16[32,4096]{1,0:T(8,128)(2,1)S(1)} %slice.121), channel_id=1, source_target_pairs={{0,4},{1,5},{2,6},{3,7},{4,0},{5,1},{6,2},{7,3},{8,12},{9,13},{10,... | collective-permute-start | bytes 786440 | tf_op jit(solution)/shard_map/ppermute | solution.py:31
  200.4 15.8 %collective-permute-start.4 = (bf16[32,4096]{1,0:T(8,128)(2,1)S(1)}, bf16[32,4096]{1,0:T(8,128)(2,1)S(1)}, u32[]{:S(2)}, u32[]{:S(2)}) collective-permute-start(bf16[32,4096]{1,0:T(8,128)(2,1)S(1)} %slice.123), channel_id=1, source_target_pairs={{0,4},{1,5},{2,6},{3,7},{4,0},{5,1},{6,2},{7,3},{8,12},{9,13},{10,... | collective-permute-start | bytes 786440 | tf_op jit(solution)/shard_map/ppermute | solution.py:31
  201.9 14.5 %collective-permute-start.7 = (bf16[32,4096]{1,0:T(8,128)(2,1)S(1)}, bf16[32,4096]{1,0:T(8,128)(2,1)S(1)}, u32[]{:S(2)}, u32[]{:S(2)}) collective-permute-start(bf16[32,4096]{1,0:T(8,128)(2,1)S(1)} %slice.122), channel_id=1, source_target_pairs={{0,2},{1,3},{2,0},{3,1},{4,6},{5,7},{6,4},{7,5},{8,10},{9,11},{10,... | collective-permute-start | bytes 786440 | tf_op jit(solution)/shard_map/ppermute | solution.py:31
  211.7 9.2 %collective-permute-start.15 = (bf16[32,4096]{1,0:T(8,128)(2,1)S(1)}, bf16[32,4096]{1,0:T(8,128)(2,1)S(1)}, u32[]{:S(2)}, u32[]{:S(2)}) collective-permute-start(bf16[32,4096]{1,0:T(8,128)(2,1)S(1)} %slice.120), channel_id=1, source_target_pairs={{0,4},{1,5},{2,6},{3,7},{4,0},{5,1},{6,2},{7,3},{8,12},{9,13},{10,... | collective-permute-start | bytes 786440 | tf_op jit(solution)/shard_map/ppermute | solution.py:31
  212.0 18.3 %collective-permute-start.13 = (bf16[16,4096]{1,0:T(8,128)(2,1)S(1)}, bf16[16,4096]{1,0:T(8,128)(2,1)S(1)}, u32[]{:S(2)}, u32[]{:S(2)}) collective-permute-start(bf16[16,4096]{1,0:T(8,128)(2,1)S(1)} %slice.125), channel_id=1, source_target_pairs={{0,8},{1,9},{2,10},{3,11},{4,12},{5,13},{6,14},{7,15},{8,0},{9,1},... | collective-permute-start | bytes 393224 | tf_op jit(solution)/shard_map/ppermute | solution.py:31
  216.3 16.8 %collective-permute-start.5 = (bf16[16,4096]{1,0:T(8,128)(2,1)S(1)}, bf16[16,4096]{1,0:T(8,128)(2,1)S(1)}, u32[]{:S(2)}, u32[]{:S(2)}) collective-permute-start(bf16[16,4096]{1,0:T(8,128)(2,1)S(1)} %slice.127), channel_id=1, source_target_pairs={{0,8},{1,9},{2,10},{3,11},{4,12},{5,13},{6,14},{7,15},{8,0},{9,1},... | collective-permute-start | bytes 393224 | tf_op jit(solution)/shard_map/ppermute | solution.py:31
  216.5 19.1 %collective-permute-start.8 = (bf16[16,4096]{1,0:T(8,128)(2,1)S(1)}, bf16[16,4096]{1,0:T(8,128)(2,1)S(1)}, u32[]{:S(2)}, u32[]{:S(2)}) collective-permute-start(bf16[16,4096]{1,0:T(8,128)(2,1)S(1)} %slice.126), channel_id=1, source_target_pairs={{0,8},{1,9},{2,10},{3,11},{4,12},{5,13},{6,14},{7,15},{8,0},{9,1},... | collective-permute-start | bytes 393224 | tf_op jit(solution)/shard_map/ppermute | solution.py:31
  220.9 16.1 %collective-permute-start.16 = (bf16[16,4096]{1,0:T(8,128)(2,1)S(1)}, bf16[16,4096]{1,0:T(8,128)(2,1)S(1)}, u32[]{:S(2)}, u32[]{:S(2)}) collective-permute-start(bf16[16,4096]{1,0:T(8,128)(2,1)S(1)} %slice.124), channel_id=1, source_target_pairs={{0,8},{1,9},{2,10},{3,11},{4,12},{5,13},{6,14},{7,15},{8,0},{9,1},... | collective-permute-start | bytes 393224 | tf_op jit(solution)/shard_map/ppermute | solution.py:31
  (13 other events, 188.3 us)

commit v5 on v4

--- a/solution.py
+++ b/solution.py
@@ -682,9 +682,8 @@
             total = keep + got.astype(jnp.float32)
             half = total.shape[0] // 2
             keep = total[:half]
-            got = permute_to(
-                total[half:].astype(jnp.bfloat16), n, lambda i: i ^ (turn * ways)
-            )
+            send = total[half:].astype(jnp.bfloat16)
+            got = permute_to(send, n, lambda i: i ^ (turn * ways))
         results.append((keep + got.astype(jnp.float32)).astype(jnp.bfloat16))
     out = jnp.stack(
         [

time: 239 us -> 239 us (level)
  no operation moved by 1% of the time
where the time goes in v5:
time: 239 us; the launch traced here: 238 us
  Pallas kernels  92.7 us (39%)
  starting transfers between devices  77.5 us (32%)
  waiting for transfers between devices  55.3 us (23%)
  other arithmetic  8.46 us (4%)
  local copies, waits for them, and re-layouts  2.86 us (1%)
    ppermute x21, starting transfers between devices, permute_to(): return lax.ppermute(x, 'pages', [(i, target(i)) for i in range(n)])  68 us
    pallas_call x3, Pallas kernels, attend(): pl.pallas_call(functools.partial(attend_kernel, first_slot=first_slot, fi...  53.8 us
    all_to_all x2, waiting for transfers between devices, exchange(): lax.all_to_all(x, 'pages', 0, 0, axis_index_groups=groups, tiled=True)  28.4 us
    ppermute x21, waiting for transfers between devices, permute_to(): return lax.ppermute(x, 'pages', [(i, target(i)) for i in range(n)])  26.9 us
    pallas_call x4, Pallas kernels, project(): pl.pallas_call(functools.partial(project_kernel, n_parts=len(parts), n_ws...  21.2 us
    all_to_all x2, starting transfers between devices, exchange(): lax.all_to_all(x, 'pages', 0, 0, axis_index_groups=groups, tiled=True)  9.59 us
    pallas_call x2, Pallas kernels, split_heads(): pl.pallas_call(functools.partial(split_heads_kernel, first=first, count=c...  6.32 us
    add x8, other arithmetic, local(): total = keep + got.astype(jnp.float32)  4.86 us
  transfers between devices with their start and end apart: 23, of which 8 were waited for; matrix products, arithmetic and copies ran while one was open for 3% of the time, Pallas kernels for 37%

profile of v5, /device:TPU:0, one launch (start us, length us, event | category | flops | bytes accessed | tf_op | source)
XLA Modules:
  0.0 237.9 jit_solution(7138284524817176937)
XLA Ops:
  2.0 3.6 %split_heads.3 = bf16[8,648,2,128]{3,2,1,0:T(2,128)(2,1)} custom-call(bf16[8,128,2,1024]{3,2,1,0:T(2,128)(2,1)} %kv_ref.7, bf16[8,2,128]{2,1,0:T(2,128)(2,1)} %broadcast_in_dim.2.ids_ref), custom_call_target="tpu_custom_call" | custom-call | tf_op jit(solution)/shard_map/split_heads/pallas_call | solution.py:79
  5.5 5.3 %all-to-all-start.1 = ((bf16[8,648,2,128]{3,2,1,0:T(2,128)(2,1)}), bf16[8,648,2,128]{3,2,1,0:T(2,128)(2,1)S(1)}, u32[]{:S(2)}, u32[]{:S(2)}) async-start(bf16[8,648,2,128]{3,2,1,0:T(2,128)(2,1)} %split_heads.3), calls=%async_computation.1 | async-start | bytes 5308416 | tf_op jit(solution)/shard_map/all_to_all | solution.py:630
  11.3 2.7 %split_heads.2 = bf16[8,392,2,128]{3,2,1,0:T(2,128)(2,1)} custom-call(bf16[8,128,2,1024]{3,2,1,0:T(2,128)(2,1)} %kv_ref.7, bf16[8,2,128]{2,1,0:T(2,128)(2,1)} %broadcast_in_dim.2.ids_ref), custom_call_target="tpu_custom_call" | custom-call | tf_op jit(solution)/shard_map/split_heads/pallas_call | solution.py:79
  14.1 28.4 %all-to-all-done.1 = bf16[8,648,2,128]{3,2,1,0:T(2,128)(2,1)S(1)} async-done(((bf16[8,648,2,128]{3,2,1,0:T(2,128)(2,1)}), bf16[8,648,2,128]{3,2,1,0:T(2,128)(2,1)S(1)}, u32[]{:S(2)}, u32[]{:S(2)}) %all-to-all-start.1) | async-done | bytes 2654240 | tf_op jit(solution)/shard_map/all_to_all | solution.py:630
  42.5 4.3 %all-to-all-start = ((bf16[8,392,2,128]{3,2,1,0:T(2,128)(2,1)}), bf16[8,392,2,128]{3,2,1,0:T(2,128)(2,1)}, u32[]{:S(2)}, u32[]{:S(2)}) async-start(bf16[8,392,2,128]{3,2,1,0:T(2,128)(2,1)} %split_heads.2), calls=%async_computation | async-start | bytes 3211264 | tf_op jit(solution)/shard_map/all_to_all | solution.py:630
  49.3 4.3 %query_rows.1.q_ref = bf16[4,1024,128]{2,1,0:T(8,128)(2,1)} custom-call(s32[4]{0:T(128)} %pad_add_fusion.place, bf16[2,256,8192]{2,1,0:T(8,128)(2,1)} %q_ref.1), custom_call_target="tpu_custom_call" | custom-call | tf_op jit(solution)/shard_map/query_rows/pallas_call | solution.py:219
  53.7 35.6 %attend_first.1 = (f32[4,1024,256]{2,1,0:T(8,128)}, f32[4,1024,128]{2,1,0:T(8,128)}) custom-call(s32[4]{0:T(128)} %pad_add_fusion.place, bf16[8,1296,128]{2,1,0:T(8,128)(2,1)} %bitcast.12, bf16[4,1024,128]{2,1,0:T(8,128)(2,1)} %query_rows.1.q_ref), custom_call_target="tpu_custom_call" | custom-call | flops 21474836480 | bytes 2654208 | tf_op jit(solution)/shard_map/attend_first/pallas_call | solution.py:488
  89.2 9.1 %attend_last.3 = (bf16[1072,128]{1,0:T(8,128)(2,1)}, bf16[1072,128]{1,0:T(8,128)(2,1)}) custom-call(s32[4]{0:T(128)} %pad_add_fusion.place, bf16[8,784,128]{2,1,0:T(8,128)(2,1)} %bitcast.4.x_ref, bf16[4,1024,128]{2,1,0:T(8,128)(2,1)} %query_rows.1.q_ref, f32[4,1024,256]{2,1,0:T(8,128)} %get-tuple-element.22.refs_0_, f32[4,1024,128]{2,1,0:T(8,128)} %get-tuple-element.23.refs_1_), custom_call_target="tpu_custom_call" | custom-call | flops 6442450944 | bytes 1605632 | tf_op jit(solution)/shard_map/attend_last/pallas_call | solution.py:488
  100.0 3.1 %collective-permute-start.10 = (bf16[1072,128]{1,0:T(8,128)(2,1)}, bf16[1072,128]{1,0:T(8,128)(2,1)S(1)}, u32[]{:S(2)}, u32[]{:S(2)}) collective-permute-start(bf16[1072,128]{1,0:T(8,128)(2,1)} %get-tuple-element.32), channel_id=1, source_target_pairs={{0,1},{1,9},{2,3},{3,11},{4,5},{5,13},{6,7},{7,15},{8,0},{9,8},{10... | collective-permute-start | bytes 823304 | tf_op jit(solution)/shard_map/ppermute | solution.py:31
  103.0 9.1 %attend_last.2 = (bf16[1072,128]{1,0:T(8,128)(2,1)}, bf16[1072,128]{1,0:T(8,128)(2,1)}) custom-call(s32[4]{0:T(128)} %pad_add_fusion.place, bf16[8,784,128]{2,1,0:T(8,128)(2,1)} %bitcast.4.x_ref, bf16[4,1024,128]{2,1,0:T(8,128)(2,1)} %query_rows.1.q_ref, f32[4,1024,256]{2,1,0:T(8,128)} %get-tuple-element.22.refs_0_, f32[4,1024,128]{2,1,0:T(8,128)} %get-tuple-element.23.refs_1_), custom_call_target="tpu_custom_call" | custom-call | flops 6442450944 | bytes 1605632 | tf_op jit(solution)/shard_map/attend_last/pallas_call | solution.py:488
  114.4 3.1 %outgoing_pages.1 = (bf16[128,2,1024]{2,1,0:T(2,128)(2,1)}, bf16[128,2,1024]{2,1,0:T(2,128)(2,1)}, bf16[128,2,1024]{2,1,0:T(2,128)(2,1)}, bf16[128,2,1024]{2,1,0:T(2,128)(2,1)}) custom-call(s32[4]{0:T(128)} %bitcast.13, bf16[8,128,2,1024]{3,2,1,0:T(2,128)(2,1)} %kv_ref.7), custom_call_target="tpu_custom_call" | custom-call | tf_op jit(solution)/shard_map/outgoing_pages/pallas_call | solution.py:116
  120.0 42.2 %collective-permute-start.19 = (bf16[128,2,1024]{2,1,0:T(2,128)(2,1)}, bf16[128,2,1024]{2,1,0:T(2,128)(2,1)S(1)}, u32[]{:S(2)}, u32[]{:S(2)}) collective-permute-start(bf16[128,2,1024]{2,1,0:T(2,128)(2,1)} %get-tuple-element.40), channel_id=1, source_target_pairs={{0,3},{1,4},{2,5},{3,6},{4,7},{5,8},{6,9},{7,10},{8,11},{9,12},{10... | collective-permute-start | bytes 1572872 | tf_op jit(solution)/shard_map/ppermute | solution.py:31
  162.2 5.5 %project.6 = (f32[64,4096]{1,0:T(8,128)}, bf16[64,4096]{1,0:T(8,128)(2,1)}, bf16[128,1024]{1,0:T(8,128)(2,1)}) custom-call(bf16[1072,128]{1,0:T(8,128)(2,1)} %copy-done.9, bf16[1072,128]{1,0:T(8,128)(2,1)} %copy-done.11, bf16[512,8192]{1,0:T(8,128)(2,1)} %refs_1_.3, bf16[512,8192]{1,0:T(8,128)(2,1)} %collective-permute-done.2.refs_3_.refs_2_), custom_call_target="tpu_custom_call" | custom-call | flops 1073741824 | bytes 8388608 | tf_op jit(solution)/shard_map/project/pallas_call | solution.py:598
  168.4 5.3 %project.4 = (f32[64,4096]{1,0:T(8,128)}, bf16[64,4096]{1,0:T(8,128)(2,1)}, bf16[128,1024]{1,0:T(8,128)(2,1)}) custom-call(bf16[1072,128]{1,0:T(8,128)(2,1)} %copy-done.10, bf16[1072,128]{1,0:T(8,128)(2,1)} %copy-done.12, bf16[512,8192]{1,0:T(8,128)(2,1)} %refs_1_.3, bf16[512,8192]{1,0:T(8,128)(2,1)} %collective-permute-done.2.refs_3_.refs_2_), custom_call_target="tpu_custom_call" | custom-call | flops 1073741824 | bytes 8388608 | tf_op jit(solution)/shard_map/project/pallas_call | solution.py:598
  173.7 5.2 %project.5 = (f32[64,4096]{1,0:T(8,128)}, bf16[64,4096]{1,0:T(8,128)(2,1)}) custom-call(bf16[128,1024]{1,0:T(8,128)(2,1)} %get-tuple-element.28.refs_0_, bf16[512,8192]{1,0:T(8,128)(2,1)} %refs_1_.3, bf16[512,8192]{1,0:T(8,128)(2,1)} %collective-permute-done.2.refs_3_.refs_2_), custom_call_target="tpu_custom_call" | custom-call | flops 1073741824 | bytes 8388608 | tf_op jit(solution)/shard_map/project/pallas_call | solution.py:598
  178.9 5.2 %project.7 = (f32[64,4096]{1,0:T(8,128)}, bf16[64,4096]{1,0:T(8,128)(2,1)}) custom-call(bf16[128,1024]{1,0:T(8,128)(2,1)} %get-tuple-element.35.refs_0_, bf16[512,8192]{1,0:T(8,128)(2,1)} %refs_1_.3, bf16[512,8192]{1,0:T(8,128)(2,1)} %collective-permute-done.2.refs_3_.refs_2_), custom_call_target="tpu_custom_call" | custom-call | flops 1073741824 | bytes 8388608 | tf_op jit(solution)/shard_map/project/pallas_call | solution.py:598
  187.3 4.0 %arrange_pages.1 = bf16[8,128,2,1024]{3,2,1,0:T(2,128)(2,1)} custom-call(s32[8]{0:T(128)} %page_after.1, s32[4]{0:T(128)} %bitcast.14, bf16[8,128,2,1024]{3,2,1,0:T(2,128)(2,1)} %kv_ref.7, bf16[128,2,1024]{2,1,0:T(2,128)(2,1)} %copy-done.5, bf16[128,2,1024]{2,1,0:T(2,128)(2,1)} %copy-done.6, bf16[128,2,1024]{2,1,0:T(2,128)(2,1)} %copy-done.7, ...), custom_call_target="tpu_custom_call" | custom-call | tf_op jit(solution)/shard_map/arrange_pages/pallas_call | solution.py:174
  194.6 4.7 %collective-permute-done.3 = bf16[64,4096]{1,0:T(8,128)(2,1)} collective-permute-done((bf16[64,4096]{1,0:T(8,128)(2,1)}, bf16[64,4096]{1,0:T(8,128)(2,1)}, u32[]{:S(2)}, u32[]{:S(2)}) %collective-permute-start.3) | collective-permute-done | bytes 524320 | tf_op jit(solution)/shard_map/ppermute | solution.py:31
  203.2 7.3 %collective-permute-done.14 = bf16[64,4096]{1,0:T(8,128)(2,1)} collective-permute-done((bf16[64,4096]{1,0:T(8,128)(2,1)}, bf16[64,4096]{1,0:T(8,128)(2,1)}, u32[]{:S(2)}, u32[]{:S(2)}) %collective-permute-start.14) | collective-permute-done | bytes 524320 | tf_op jit(solution)/shard_map/ppermute | solution.py:31
  212.0 4.2 %collective-permute-start.13 = (bf16[16,4096]{1,0:T(8,128)(2,1)S(1)}, bf16[16,4096]{1,0:T(8,128)(2,1)S(1)}, u32[]{:S(2)}, u32[]{:S(2)}) collective-permute-start(bf16[16,4096]{1,0:T(8,128)(2,1)S(1)} %slice.125), channel_id=1, source_target_pairs={{0,8},{1,9},{2,10},{3,11},{4,12},{5,13},{6,14},{7,15},{8,0},{9,1},... | collective-permute-start | bytes 393224 | tf_op jit(solution)/shard_map/ppermute | solution.py:31
  216.5 3.0 %collective-permute-start.8 = (bf16[16,4096]{1,0:T(8,128)(2,1)S(1)}, bf16[16,4096]{1,0:T(8,128)(2,1)S(1)}, u32[]{:S(2)}, u32[]{:S(2)}) collective-permute-start(bf16[16,4096]{1,0:T(8,128)(2,1)S(1)} %slice.126), channel_id=1, source_target_pairs={{0,8},{1,9},{2,10},{3,11},{4,12},{5,13},{6,14},{7,15},{8,0},{9,1},... | collective-permute-start | bytes 393224 | tf_op jit(solution)/shard_map/ppermute | solution.py:31
  220.9 2.5 %collective-permute-start.16 = (bf16[16,4096]{1,0:T(8,128)(2,1)S(1)}, bf16[16,4096]{1,0:T(8,128)(2,1)S(1)}, u32[]{:S(2)}, u32[]{:S(2)}) collective-permute-start(bf16[16,4096]{1,0:T(8,128)(2,1)S(1)} %slice.124), channel_id=1, source_target_pairs={{0,8},{1,9},{2,10},{3,11},{4,12},{5,13},{6,14},{7,15},{8,0},{9,1},... | collective-permute-start | bytes 393224 | tf_op jit(solution)/shard_map/ppermute | solution.py:31
  223.4 6.9 %collective-permute-done.13 = bf16[16,4096]{1,0:T(8,128)(2,1)S(1)} collective-permute-done((bf16[16,4096]{1,0:T(8,128)(2,1)S(1)}, bf16[16,4096]{1,0:T(8,128)(2,1)S(1)}, u32[]{:S(2)}, u32[]{:S(2)}) %collective-permute-start.13) | collective-permute-done | bytes 131104 | tf_op jit(solution)/shard_map/ppermute | solution.py:31
  230.4 2.8 %collective-permute-done.5 = bf16[16,4096]{1,0:T(8,128)(2,1)S(1)} collective-permute-done((bf16[16,4096]{1,0:T(8,128)(2,1)S(1)}, bf16[16,4096]{1,0:T(8,128)(2,1)S(1)}, u32[]{:S(2)}, u32[]{:S(2)}) %collective-permute-start.5) | collective-permute-done | bytes 131104 | tf_op jit(solution)/shard_map/ppermute | solution.py:31
  (89 shorter events, 29.5 us)
Async XLA Ops:
  5.5 37.0 %all-to-all-start.1 = ((bf16[8,648,2,128]{3,2,1,0:T(2,128)(2,1)}), bf16[8,648,2,128]{3,2,1,0:T(2,128)(2,1)S(1)}, u32[]{:S(2)}, u32[]{:S(2)}) async-start(bf16[8,648,2,128]{3,2,1,0:T(2,128)(2,1)} %split_heads.3), calls=%async_computation.1 | async-start | bytes 5308416 | tf_op jit(solution)/shard_map/all_to_all | solution.py:630
  10.8 151.3 %collective-permute-start.2 = (bf16[512,8192]{1,0:T(8,128)(2,1)}, bf16[512,8192]{1,0:T(8,128)(2,1)}, u32[]{:S(2)}, u32[]{:S(2)}) collective-permute-start(bf16[512,8192]{1,0:T(8,128)(2,1)} %refs_1_.3), channel_id=1, source_target_pairs={{0,1},{1,0},{2,3},{3,2},{4,5},{5,4},{6,7},{7,6},{8,9},{9,8},{10,11... | collective-permute-start | bytes 25165832 | tf_op jit(solution)/shard_map/ppermute | solution.py:31
  42.5 46.7 %all-to-all-start = ((bf16[8,392,2,128]{3,2,1,0:T(2,128)(2,1)}), bf16[8,392,2,128]{3,2,1,0:T(2,128)(2,1)}, u32[]{:S(2)}, u32[]{:S(2)}) async-start(bf16[8,392,2,128]{3,2,1,0:T(2,128)(2,1)} %split_heads.2), calls=%async_computation | async-start | bytes 3211264 | tf_op jit(solution)/shard_map/all_to_all | solution.py:630
  98.3 19.2 %collective-permute-start.9 = (bf16[1072,128]{1,0:T(8,128)(2,1)}, bf16[1072,128]{1,0:T(8,128)(2,1)S(1)}, u32[]{:S(2)}, u32[]{:S(2)}) collective-permute-start(bf16[1072,128]{1,0:T(8,128)(2,1)} %get-tuple-element.31), channel_id=1, source_target_pairs={{0,0},{1,8},{2,2},{3,10},{4,4},{5,12},{6,6},{7,14},{8,1},{9,9},{10... | collective-permute-start | bytes 823304 | tf_op jit(solution)/shard_map/ppermute | solution.py:31
  100.0 17.7 %collective-permute-start.10 = (bf16[1072,128]{1,0:T(8,128)(2,1)}, bf16[1072,128]{1,0:T(8,128)(2,1)S(1)}, u32[]{:S(2)}, u32[]{:S(2)}) collective-permute-start(bf16[1072,128]{1,0:T(8,128)(2,1)} %get-tuple-element.32), channel_id=1, source_target_pairs={{0,1},{1,9},{2,3},{3,11},{4,5},{5,13},{6,7},{7,15},{8,0},{9,8},{10... | collective-permute-start | bytes 823304 | tf_op jit(solution)/shard_map/ppermute | solution.py:31
  112.2 7.8 %collective-permute-start = (bf16[1072,128]{1,0:T(8,128)(2,1)}, bf16[1072,128]{1,0:T(8,128)(2,1)S(1)}, u32[]{:S(2)}, u32[]{:S(2)}) collective-permute-start(bf16[1072,128]{1,0:T(8,128)(2,1)} %get-tuple-element.24), channel_id=1, source_target_pairs={{0,0},{1,8},{2,2},{3,10},{4,4},{5,12},{6,6},{7,14},{8,1},{9,9},{10... | collective-permute-start | bytes 823304 | tf_op jit(solution)/shard_map/ppermute | solution.py:31
  113.8 53.9 %collective-permute-start.1 = (bf16[1072,128]{1,0:T(8,128)(2,1)}, bf16[1072,128]{1,0:T(8,128)(2,1)S(1)}, u32[]{:S(2)}, u32[]{:S(2)}) collective-permute-start(bf16[1072,128]{1,0:T(8,128)(2,1)} %get-tuple-element.25), channel_id=1, source_target_pairs={{0,1},{1,9},{2,3},{3,11},{4,5},{5,13},{6,7},{7,15},{8,0},{9,8},{10... | collective-permute-start | bytes 823304 | tf_op jit(solution)/shard_map/ppermute | solution.py:31
  117.6 66.5 %collective-permute-start.17 = (bf16[128,2,1024]{2,1,0:T(2,128)(2,1)}, bf16[128,2,1024]{2,1,0:T(2,128)(2,1)S(1)}, u32[]{:S(2)}, u32[]{:S(2)}) collective-permute-start(bf16[128,2,1024]{2,1,0:T(2,128)(2,1)} %get-tuple-element.38), channel_id=1, source_target_pairs={{0,1},{1,2},{2,3},{3,4},{4,5},{5,6},{6,7},{7,8},{8,9},{9,10},{10,1... | collective-permute-start | bytes 1572872 | tf_op jit(solution)/shard_map/ppermute | solution.py:31
  117.6 67.9 %collective-permute-start.18 = (bf16[128,2,1024]{2,1,0:T(2,128)(2,1)}, bf16[128,2,1024]{2,1,0:T(2,128)(2,1)S(1)}, u32[]{:S(2)}, u32[]{:S(2)}) collective-permute-start(bf16[128,2,1024]{2,1,0:T(2,128)(2,1)} %get-tuple-element.39), channel_id=1, source_target_pairs={{0,2},{1,3},{2,4},{3,5},{4,6},{5,7},{6,8},{7,9},{8,10},{9,11},{10,... | collective-permute-start | bytes 1572872 | tf_op jit(solution)/shard_map/ppermute | solution.py:31
  120.0 47.7 %copy-start.10 = (bf16[1072,128]{1,0:T(8,128)(2,1)}, bf16[1072,128]{1,0:T(8,128)(2,1)S(1)}, u32[]{:S(2)}) copy-start(bf16[1072,128]{1,0:T(8,128)(2,1)S(1)} %collective-permute-done.refs_0_) | copy-start | bytes 823300
  120.0 65.6 %collective-permute-start.19 = (bf16[128,2,1024]{2,1,0:T(2,128)(2,1)}, bf16[128,2,1024]{2,1,0:T(2,128)(2,1)S(1)}, u32[]{:S(2)}, u32[]{:S(2)}) collective-permute-start(bf16[128,2,1024]{2,1,0:T(2,128)(2,1)} %get-tuple-element.40), channel_id=1, source_target_pairs={{0,3},{1,4},{2,5},{3,6},{4,7},{5,8},{6,9},{7,10},{8,11},{9,12},{10... | collective-permute-start | bytes 1572872 | tf_op jit(solution)/shard_map/ppermute | solution.py:31
  162.2 24.2 %collective-permute-start.20 = (bf16[128,2,1024]{2,1,0:T(2,128)(2,1)}, bf16[128,2,1024]{2,1,0:T(2,128)(2,1)S(1)}, u32[]{:S(2)}, u32[]{:S(2)}) collective-permute-start(bf16[128,2,1024]{2,1,0:T(2,128)(2,1)} %get-tuple-element.41), channel_id=1, source_target_pairs={{0,4},{1,5},{2,6},{3,7},{4,8},{5,9},{6,10},{7,11},{8,12},{9,13},{1... | collective-permute-start | bytes 1572872 | tf_op jit(solution)/shard_map/ppermute | solution.py:31
  167.7 23.6 %collective-permute-start.11 = (bf16[64,4096]{1,0:T(8,128)(2,1)}, bf16[64,4096]{1,0:T(8,128)(2,1)}, u32[]{:S(2)}, u32[]{:S(2)}) collective-permute-start(bf16[64,4096]{1,0:T(8,128)(2,1)} %get-tuple-element.34), channel_id=1, source_target_pairs={{0,2},{1,3},{2,0},{3,1},{4,6},{5,7},{6,4},{7,5},{8,10},{9,11},{10,... | collective-permute-start | bytes 1572872 | tf_op jit(solution)/shard_map/ppermute | solution.py:31
  184.1 15.2 %collective-permute-start.3 = (bf16[64,4096]{1,0:T(8,128)(2,1)}, bf16[64,4096]{1,0:T(8,128)(2,1)}, u32[]{:S(2)}, u32[]{:S(2)}) collective-permute-start(bf16[64,4096]{1,0:T(8,128)(2,1)} %get-tuple-element.27), channel_id=1, source_target_pairs={{0,2},{1,3},{2,0},{3,1},{4,6},{5,7},{6,4},{7,5},{8,10},{9,11},{10,... | collective-permute-start | bytes 1572872 | tf_op jit(solution)/shard_map/ppermute | solution.py:31
  185.6 15.1 %collective-permute-start.6 = (bf16[64,4096]{1,0:T(8,128)(2,1)}, bf16[64,4096]{1,0:T(8,128)(2,1)}, u32[]{:S(2)}, u32[]{:S(2)}) collective-permute-start(bf16[64,4096]{1,0:T(8,128)(2,1)} %get-tuple-element.30), channel_id=1, source_target_pairs={{0,4},{1,5},{2,6},{3,7},{4,0},{5,1},{6,2},{7,3},{8,12},{9,13},{10,... | collective-permute-start | bytes 1572872 | tf_op jit(solution)/shard_map/ppermute | solution.py:31
  185.6 24.9 %collective-permute-start.14 = (bf16[64,4096]{1,0:T(8,128)(2,1)}, bf16[64,4096]{1,0:T(8,128)(2,1)}, u32[]{:S(2)}, u32[]{:S(2)}) collective-permute-start(bf16[64,4096]{1,0:T(8,128)(2,1)} %get-tuple-element.37.refs_4_), channel_id=1, source_target_pairs={{0,2},{1,3},{2,0},{3,1},{4,6},{5,7},{6,4},{7,5},{8,10},{9,11},{10,... | collective-permute-start | bytes 1572872 | tf_op jit(solution)/shard_map/ppermute | solution.py:31
  192.6 19.3 %collective-permute-start.12 = (bf16[32,4096]{1,0:T(8,128)(2,1)S(1)}, bf16[32,4096]{1,0:T(8,128)(2,1)S(1)}, u32[]{:S(2)}, u32[]{:S(2)}) collective-permute-start(bf16[32,4096]{1,0:T(8,128)(2,1)S(1)} %slice.121), channel_id=1, source_target_pairs={{0,4},{1,5},{2,6},{3,7},{4,0},{5,1},{6,2},{7,3},{8,12},{9,13},{10,... | collective-permute-start | bytes 786440 | tf_op jit(solution)/shard_map/ppermute | solution.py:31
  200.4 15.8 %collective-permute-start.4 = (bf16[32,4096]{1,0:T(8,128)(2,1)S(1)}, bf16[32,4096]{1,0:T(8,128)(2,1)S(1)}, u32[]{:S(2)}, u32[]{:S(2)}) collective-permute-start(bf16[32,4096]{1,0:T(8,128)(2,1)S(1)} %slice.123), channel_id=1, source_target_pairs={{0,4},{1,5},{2,6},{3,7},{4,0},{5,1},{6,2},{7,3},{8,12},{9,13},{10,... | collective-permute-start | bytes 786440 | tf_op jit(solution)/shard_map/ppermute | solution.py:31
  201.9 14.5 %collective-permute-start.7 = (bf16[32,4096]{1,0:T(8,128)(2,1)S(1)}, bf16[32,4096]{1,0:T(8,128)(2,1)S(1)}, u32[]{:S(2)}, u32[]{:S(2)}) collective-permute-start(bf16[32,4096]{1,0:T(8,128)(2,1)S(1)} %slice.122), channel_id=1, source_target_pairs={{0,2},{1,3},{2,0},{3,1},{4,6},{5,7},{6,4},{7,5},{8,10},{9,11},{10,... | collective-permute-start | bytes 786440 | tf_op jit(solution)/shard_map/ppermute | solution.py:31
  211.7 9.2 %collective-permute-start.15 = (bf16[32,4096]{1,0:T(8,128)(2,1)S(1)}, bf16[32,4096]{1,0:T(8,128)(2,1)S(1)}, u32[]{:S(2)}, u32[]{:S(2)}) collective-permute-start(bf16[32,4096]{1,0:T(8,128)(2,1)S(1)} %slice.120), channel_id=1, source_target_pairs={{0,4},{1,5},{2,6},{3,7},{4,0},{5,1},{6,2},{7,3},{8,12},{9,13},{10,... | collective-permute-start | bytes 786440 | tf_op jit(solution)/shard_map/ppermute | solution.py:31
  212.0 18.3 %collective-permute-start.13 = (bf16[16,4096]{1,0:T(8,128)(2,1)S(1)}, bf16[16,4096]{1,0:T(8,128)(2,1)S(1)}, u32[]{:S(2)}, u32[]{:S(2)}) collective-permute-start(bf16[16,4096]{1,0:T(8,128)(2,1)S(1)} %slice.125), channel_id=1, source_target_pairs={{0,8},{1,9},{2,10},{3,11},{4,12},{5,13},{6,14},{7,15},{8,0},{9,1},... | collective-permute-start | bytes 393224 | tf_op jit(solution)/shard_map/ppermute | solution.py:31
  216.3 16.8 %collective-permute-start.5 = (bf16[16,4096]{1,0:T(8,128)(2,1)S(1)}, bf16[16,4096]{1,0:T(8,128)(2,1)S(1)}, u32[]{:S(2)}, u32[]{:S(2)}) collective-permute-start(bf16[16,4096]{1,0:T(8,128)(2,1)S(1)} %slice.127), channel_id=1, source_target_pairs={{0,8},{1,9},{2,10},{3,11},{4,12},{5,13},{6,14},{7,15},{8,0},{9,1},... | collective-permute-start | bytes 393224 | tf_op jit(solution)/shard_map/ppermute | solution.py:31
  216.5 19.1 %collective-permute-start.8 = (bf16[16,4096]{1,0:T(8,128)(2,1)S(1)}, bf16[16,4096]{1,0:T(8,128)(2,1)S(1)}, u32[]{:S(2)}, u32[]{:S(2)}) collective-permute-start(bf16[16,4096]{1,0:T(8,128)(2,1)S(1)} %slice.126), channel_id=1, source_target_pairs={{0,8},{1,9},{2,10},{3,11},{4,12},{5,13},{6,14},{7,15},{8,0},{9,1},... | collective-permute-start | bytes 393224 | tf_op jit(solution)/shard_map/ppermute | solution.py:31
  220.9 16.1 %collective-permute-start.16 = (bf16[16,4096]{1,0:T(8,128)(2,1)S(1)}, bf16[16,4096]{1,0:T(8,128)(2,1)S(1)}, u32[]{:S(2)}, u32[]{:S(2)}) collective-permute-start(bf16[16,4096]{1,0:T(8,128)(2,1)S(1)} %slice.124), channel_id=1, source_target_pairs={{0,8},{1,9},{2,10},{3,11},{4,12},{5,13},{6,14},{7,15},{8,0},{9,1},... | collective-permute-start | bytes 393224 | tf_op jit(solution)/shard_map/ppermute | solution.py:31
  (13 other events, 188.3 us)

commit v6 on v5

--- a/solution.py
+++ b/solution.py
@@ -40,25 +40,20 @@
     return (p % 2) * 4 + (p // 2 % 2) * 2 + p // 4
 
 
-def split_heads_kernel(kv_ref, ids_ref, out_ref, buf, in_sems, out_sems, *, first, count):
-    extra = ids_ref.shape[0]
+def split_heads_kernel(pages, kv_ref, out_ref, buf, in_sems, out_sems, *, first, count):
     loads = []
     for d in range(KV_HEADS):
         lanes = pl.ds(head_of(d) * HEAD_DIM, HEAD_DIM)
-        row = [
-            pltpu.make_async_copy(
-                kv_ref.at[first + i, :, :, lanes],
-                buf.at[d, pl.ds(i * PAGE_TOK, PAGE_TOK)],
-                in_sems.at[d, i],
-            )
-            for i in range(count)
-        ]
-        row.append(
-            pltpu.make_async_copy(
-                ids_ref, buf.at[d, pl.ds(count * PAGE_TOK, extra)], in_sems.at[d, count]
-            )
+        loads.append(
+            [
+                pltpu.make_async_copy(
+                    kv_ref.at[first + i, :, :, lanes],
+                    buf.at[d, pl.ds(i * PAGE_TOK, PAGE_TOK)],
+                    in_sems.at[d, i],
+                )
+                for i in range(count)
+            ]
         )
-        loads.append(row)
     stores = [
         pltpu.make_async_copy(buf.at[d], out_ref.at[d], out_sems.at[d])
         for d in range(KV_HEADS)
@@ -66,6 +61,11 @@
     for row in loads:
         for load in row:
             load.start()
+    for t in range(kv_ref.shape[0]):
+        line = jnp.full((2, HEAD_DIM), pages[t], jnp.int32)
+        line = line.astype(jnp.float32).astype(buf.dtype)
+        for d in range(KV_HEADS):
+            buf[d, count * PAGE_TOK + t] = line
     for row, store in zip(loads, stores):
         for load in row:
             load.wait()
@@ -74,20 +74,24 @@
         store.wait()
 
 
-def split_heads(kv_cache, ids, first, count):
-    shape = (KV_HEADS, count * PAGE_TOK + ids.shape[0], 2, HEAD_DIM)
+def split_heads(kv_cache, pages, first, count):
+    shape = (KV_HEADS, count * PAGE_TOK + kv_cache.shape[0], 2, HEAD_DIM)
     return pl.pallas_call(
         functools.partial(split_heads_kernel, first=first, count=count),
         out_shape=jax.ShapeDtypeStruct(shape, kv_cache.dtype),
-        in_specs=[ANY, ANY],
-        out_specs=ANY,
-        scratch_shapes=[
-            pltpu.VMEM(shape, kv_cache.dtype),
-            pltpu.SemaphoreType.DMA((KV_HEADS, count + 1)),
-            pltpu.SemaphoreType.DMA((KV_HEADS,)),
-        ],
+        grid_spec=pltpu.PrefetchScalarGridSpec(
+            num_scalar_prefetch=1,
+            grid=(),
+            in_specs=[ANY],
+            out_specs=ANY,
+            scratch_shapes=[
+                pltpu.VMEM(shape, kv_cache.dtype),
+                pltpu.SemaphoreType.DMA((KV_HEADS, count)),
+                pltpu.SemaphoreType.DMA((KV_HEADS,)),
+            ],
+        ),
         name="split_heads",
-    )(kv_cache, ids)
+    )(pages, kv_cache)
 
 
 def outgoing_kernel(move_out, kv_ref, *refs):
@@ -629,12 +633,10 @@
     def exchange(x):
         return lax.all_to_all(x, "pages", 0, 0, axis_index_groups=groups, tiled=True)
 
-    ids = jnp.broadcast_to(slot_page_before[:, None, None], (slots, 2, HEAD_DIM))
-    ids = ids.astype(kv_cache.dtype)
     cuts = [(0, FIRST_SLOTS), (FIRST_SLOTS, slots - FIRST_SLOTS)]
     arrived = []
     for at, count in cuts:
-        piece = split_heads(kv_cache, ids, at, count)
+        piece = split_heads(kv_cache, slot_page_before, at, count)
         got = exchange(piece)
         arrived.append(got.reshape(KV_HEADS, -1, HEAD_DIM))
     place = jnp.stack([head, way, positions[0, 0], positions[1, 0]]).astype(jnp.int32)

time: 239 us -> 238 us (level)
  transfers between devices with their start and end apart: 23 -> 23, of which waited for: 8 -> 8; matrix products, arithmetic and copies ran while one was open for 3% -> 3% of each run, Pallas kernels for 37% -> 38%
where the time goes in v6:
time: 238 us; the launch traced here: 237 us
  Pallas kernels  93 us (39%)
  starting transfers between devices  77.5 us (33%)
  waiting for transfers between devices  55 us (23%)
  other arithmetic  7.8 us (3%)
    ppermute x21, starting transfers between devices, permute_to(): return lax.ppermute(x, 'pages', [(i, target(i)) for i in range(n)])  68 us
    pallas_call x3, Pallas kernels, attend(): pl.pallas_call(functools.partial(attend_kernel, first_slot=first_slot, fi...  53.8 us
    all_to_all x2, waiting for transfers between devices, exchange(): lax.all_to_all(x, 'pages', 0, 0, axis_index_groups=groups, tiled=True)  28.1 us
    ppermute x21, waiting for transfers between devices, permute_to(): return lax.ppermute(x, 'pages', [(i, target(i)) for i in range(n)])  26.9 us
    pallas_call x4, Pallas kernels, project(): pl.pallas_call(functools.partial(project_kernel, n_parts=len(parts), n_ws...  21.2 us
    all_to_all x2, starting transfers between devices, exchange(): lax.all_to_all(x, 'pages', 0, 0, axis_index_groups=groups, tiled=True)  9.59 us
    pallas_call x2, Pallas kernels, split_heads(): pl.pallas_call(functools.partial(split_heads_kernel, first=first, count=c...  6.65 us
    add x8, other arithmetic, local(): total = keep + got.astype(jnp.float32)  4.86 us
  transfers between devices with their start and end apart: 23, of which 8 were waited for; matrix products, arithmetic and copies ran while one was open for 3% of the time, Pallas kernels for 38%

profile of v6, /device:TPU:0, one launch (start us, length us, event | category | flops | bytes accessed | tf_op | source)
XLA Modules:
  0.0 236.6 jit_solution(15026039489246509464)
XLA Ops:
  0.6 3.6 %split_heads.3 = bf16[8,648,2,128]{3,2,1,0:T(2,128)(2,1)} custom-call(s32[8]{0:T(128)} %pages.3, bf16[8,128,2,1024]{3,2,1,0:T(2,128)(2,1)} %kv_ref.7), custom_call_target="tpu_custom_call" | custom-call | tf_op jit(solution)/shard_map/split_heads/pallas_call | solution.py:79
  4.2 5.3 %all-to-all-start.1 = ((bf16[8,648,2,128]{3,2,1,0:T(2,128)(2,1)}), bf16[8,648,2,128]{3,2,1,0:T(2,128)(2,1)S(1)}, u32[]{:S(2)}, u32[]{:S(2)}) async-start(bf16[8,648,2,128]{3,2,1,0:T(2,128)(2,1)} %split_heads.3), calls=%async_computation.1 | async-start | bytes 5308416 | tf_op jit(solution)/shard_map/all_to_all | solution.py:634
  10.0 3.1 %split_heads.2 = bf16[8,392,2,128]{3,2,1,0:T(2,128)(2,1)} custom-call(s32[8]{0:T(128)} %pages.3, bf16[8,128,2,1024]{3,2,1,0:T(2,128)(2,1)} %kv_ref.7), custom_call_target="tpu_custom_call" | custom-call | tf_op jit(solution)/shard_map/split_heads/pallas_call | solution.py:79
  13.1 28.1 %all-to-all-done.1 = bf16[8,648,2,128]{3,2,1,0:T(2,128)(2,1)S(1)} async-done(((bf16[8,648,2,128]{3,2,1,0:T(2,128)(2,1)}), bf16[8,648,2,128]{3,2,1,0:T(2,128)(2,1)S(1)}, u32[]{:S(2)}, u32[]{:S(2)}) %all-to-all-start.1) | async-done | bytes 2654240 | tf_op jit(solution)/shard_map/all_to_all | solution.py:634
  41.2 4.3 %all-to-all-start = ((bf16[8,392,2,128]{3,2,1,0:T(2,128)(2,1)}), bf16[8,392,2,128]{3,2,1,0:T(2,128)(2,1)}, u32[]{:S(2)}, u32[]{:S(2)}) async-start(bf16[8,392,2,128]{3,2,1,0:T(2,128)(2,1)} %split_heads.2), calls=%async_computation | async-start | bytes 3211264 | tf_op jit(solution)/shard_map/all_to_all | solution.py:634
  48.0 4.3 %query_rows.1.q_ref = bf16[4,1024,128]{2,1,0:T(8,128)(2,1)} custom-call(s32[4]{0:T(128)} %pad_add_fusion.place, bf16[2,256,8192]{2,1,0:T(8,128)(2,1)} %q_ref.1), custom_call_target="tpu_custom_call" | custom-call | tf_op jit(solution)/shard_map/query_rows/pallas_call | solution.py:223
  52.4 35.6 %attend_first.1 = (f32[4,1024,256]{2,1,0:T(8,128)}, f32[4,1024,128]{2,1,0:T(8,128)}) custom-call(s32[4]{0:T(128)} %pad_add_fusion.place, bf16[8,1296,128]{2,1,0:T(8,128)(2,1)} %bitcast.12, bf16[4,1024,128]{2,1,0:T(8,128)(2,1)} %query_rows.1.q_ref), custom_call_target="tpu_custom_call" | custom-call | flops 21474836480 | bytes 2654208 | tf_op jit(solution)/shard_map/attend_first/pallas_call | solution.py:492
  87.9 9.1 %attend_last.3 = (bf16[1072,128]{1,0:T(8,128)(2,1)}, bf16[1072,128]{1,0:T(8,128)(2,1)}) custom-call(s32[4]{0:T(128)} %pad_add_fusion.place, bf16[8,784,128]{2,1,0:T(8,128)(2,1)} %bitcast.4.x_ref, bf16[4,1024,128]{2,1,0:T(8,128)(2,1)} %query_rows.1.q_ref, f32[4,1024,256]{2,1,0:T(8,128)} %get-tuple-element.22.refs_0_, f32[4,1024,128]{2,1,0:T(8,128)} %get-tuple-element.23.refs_1_), custom_call_target="tpu_custom_call" | custom-call | flops 6442450944 | bytes 1605632 | tf_op jit(solution)/shard_map/attend_last/pallas_call | solution.py:492
  98.6 3.1 %collective-permute-start.10 = (bf16[1072,128]{1,0:T(8,128)(2,1)}, bf16[1072,128]{1,0:T(8,128)(2,1)S(1)}, u32[]{:S(2)}, u32[]{:S(2)}) collective-permute-start(bf16[1072,128]{1,0:T(8,128)(2,1)} %get-tuple-element.32), channel_id=1, source_target_pairs={{0,1},{1,9},{2,3},{3,11},{4,5},{5,13},{6,7},{7,15},{8,0},{9,8},{10... | collective-permute-start | bytes 823304 | tf_op jit(solution)/shard_map/ppermute | solution.py:31
  101.7 9.1 %attend_last.2 = (bf16[1072,128]{1,0:T(8,128)(2,1)}, bf16[1072,128]{1,0:T(8,128)(2,1)}) custom-call(s32[4]{0:T(128)} %pad_add_fusion.place, bf16[8,784,128]{2,1,0:T(8,128)(2,1)} %bitcast.4.x_ref, bf16[4,1024,128]{2,1,0:T(8,128)(2,1)} %query_rows.1.q_ref, f32[4,1024,256]{2,1,0:T(8,128)} %get-tuple-element.22.refs_0_, f32[4,1024,128]{2,1,0:T(8,128)} %get-tuple-element.23.refs_1_), custom_call_target="tpu_custom_call" | custom-call | flops 6442450944 | bytes 1605632 | tf_op jit(solution)/shard_map/attend_last/pallas_call | solution.py:492
  113.1 3.1 %outgoing_pages.1 = (bf16[128,2,1024]{2,1,0:T(2,128)(2,1)}, bf16[128,2,1024]{2,1,0:T(2,128)(2,1)}, bf16[128,2,1024]{2,1,0:T(2,128)(2,1)}, bf16[128,2,1024]{2,1,0:T(2,128)(2,1)}) custom-call(s32[4]{0:T(128)} %bitcast.13, bf16[8,128,2,1024]{3,2,1,0:T(2,128)(2,1)} %kv_ref.7), custom_call_target="tpu_custom_call" | custom-call | tf_op jit(solution)/shard_map/outgoing_pages/pallas_call | solution.py:120
  118.7 42.2 %collective-permute-start.19 = (bf16[128,2,1024]{2,1,0:T(2,128)(2,1)}, bf16[128,2,1024]{2,1,0:T(2,128)(2,1)S(1)}, u32[]{:S(2)}, u32[]{:S(2)}) collective-permute-start(bf16[128,2,1024]{2,1,0:T(2,128)(2,1)} %get-tuple-element.40), channel_id=1, source_target_pairs={{0,3},{1,4},{2,5},{3,6},{4,7},{5,8},{6,9},{7,10},{8,11},{9,12},{10... | collective-permute-start | bytes 1572872 | tf_op jit(solution)/shard_map/ppermute | solution.py:31
  160.9 5.5 %project.6 = (f32[64,4096]{1,0:T(8,128)}, bf16[64,4096]{1,0:T(8,128)(2,1)}, bf16[128,1024]{1,0:T(8,128)(2,1)}) custom-call(bf16[1072,128]{1,0:T(8,128)(2,1)} %copy-done.9, bf16[1072,128]{1,0:T(8,128)(2,1)} %copy-done.11, bf16[512,8192]{1,0:T(8,128)(2,1)} %refs_1_.3, bf16[512,8192]{1,0:T(8,128)(2,1)} %collective-permute-done.2.refs_3_.refs_2_), custom_call_target="tpu_custom_call" | custom-call | flops 1073741824 | bytes 8388608 | tf_op jit(solution)/shard_map/project/pallas_call | solution.py:602
  167.1 5.3 %project.4 = (f32[64,4096]{1,0:T(8,128)}, bf16[64,4096]{1,0:T(8,128)(2,1)}, bf16[128,1024]{1,0:T(8,128)(2,1)}) custom-call(bf16[1072,128]{1,0:T(8,128)(2,1)} %copy-done.10, bf16[1072,128]{1,0:T(8,128)(2,1)} %copy-done.12, bf16[512,8192]{1,0:T(8,128)(2,1)} %refs_1_.3, bf16[512,8192]{1,0:T(8,128)(2,1)} %collective-permute-done.2.refs_3_.refs_2_), custom_call_target="tpu_custom_call" | custom-call | flops 1073741824 | bytes 8388608 | tf_op jit(solution)/shard_map/project/pallas_call | solution.py:602
  172.4 5.2 %project.5 = (f32[64,4096]{1,0:T(8,128)}, bf16[64,4096]{1,0:T(8,128)(2,1)}) custom-call(bf16[128,1024]{1,0:T(8,128)(2,1)} %get-tuple-element.28.refs_0_, bf16[512,8192]{1,0:T(8,128)(2,1)} %refs_1_.3, bf16[512,8192]{1,0:T(8,128)(2,1)} %collective-permute-done.2.refs_3_.refs_2_), custom_call_target="tpu_custom_call" | custom-call | flops 1073741824 | bytes 8388608 | tf_op jit(solution)/shard_map/project/pallas_call | solution.py:602
  177.6 5.2 %project.7 = (f32[64,4096]{1,0:T(8,128)}, bf16[64,4096]{1,0:T(8,128)(2,1)}) custom-call(bf16[128,1024]{1,0:T(8,128)(2,1)} %get-tuple-element.35.refs_0_, bf16[512,8192]{1,0:T(8,128)(2,1)} %refs_1_.3, bf16[512,8192]{1,0:T(8,128)(2,1)} %collective-permute-done.2.refs_3_.refs_2_), custom_call_target="tpu_custom_call" | custom-call | flops 1073741824 | bytes 8388608 | tf_op jit(solution)/shard_map/project/pallas_call | solution.py:602
  185.9 4.0 %arrange_pages.1 = bf16[8,128,2,1024]{3,2,1,0:T(2,128)(2,1)} custom-call(s32[8]{0:T(128)} %page_after.1, s32[4]{0:T(128)} %bitcast.14, bf16[8,128,2,1024]{3,2,1,0:T(2,128)(2,1)} %kv_ref.7, bf16[128,2,1024]{2,1,0:T(2,128)(2,1)} %copy-done.5, bf16[128,2,1024]{2,1,0:T(2,128)(2,1)} %copy-done.6, bf16[128,2,1024]{2,1,0:T(2,128)(2,1)} %copy-done.7, ...), custom_call_target="tpu_custom_call" | custom-call | tf_op jit(solution)/shard_map/arrange_pages/pallas_call | solution.py:178
  193.2 4.7 %collective-permute-done.3 = bf16[64,4096]{1,0:T(8,128)(2,1)} collective-permute-done((bf16[64,4096]{1,0:T(8,128)(2,1)}, bf16[64,4096]{1,0:T(8,128)(2,1)}, u32[]{:S(2)}, u32[]{:S(2)}) %collective-permute-start.3) | collective-permute-done | bytes 524320 | tf_op jit(solution)/shard_map/ppermute | solution.py:31
  201.9 7.3 %collective-permute-done.14 = bf16[64,4096]{1,0:T(8,128)(2,1)} collective-permute-done((bf16[64,4096]{1,0:T(8,128)(2,1)}, bf16[64,4096]{1,0:T(8,128)(2,1)}, u32[]{:S(2)}, u32[]{:S(2)}) %collective-permute-start.14) | collective-permute-done | bytes 524320 | tf_op jit(solution)/shard_map/ppermute | solution.py:31
  210.7 4.2 %collective-permute-start.13 = (bf16[16,4096]{1,0:T(8,128)(2,1)S(1)}, bf16[16,4096]{1,0:T(8,128)(2,1)S(1)}, u32[]{:S(2)}, u32[]{:S(2)}) collective-permute-start(bf16[16,4096]{1,0:T(8,128)(2,1)S(1)} %slice.125), channel_id=1, source_target_pairs={{0,8},{1,9},{2,10},{3,11},{4,12},{5,13},{6,14},{7,15},{8,0},{9,1},... | collective-permute-start | bytes 393224 | tf_op jit(solution)/shard_map/ppermute | solution.py:31
  215.2 3.0 %collective-permute-start.8 = (bf16[16,4096]{1,0:T(8,128)(2,1)S(1)}, bf16[16,4096]{1,0:T(8,128)(2,1)S(1)}, u32[]{:S(2)}, u32[]{:S(2)}) collective-permute-start(bf16[16,4096]{1,0:T(8,128)(2,1)S(1)} %slice.126), channel_id=1, source_target_pairs={{0,8},{1,9},{2,10},{3,11},{4,12},{5,13},{6,14},{7,15},{8,0},{9,1},... | collective-permute-start | bytes 393224 | tf_op jit(solution)/shard_map/ppermute | solution.py:31
  219.6 2.5 %collective-permute-start.16 = (bf16[16,4096]{1,0:T(8,128)(2,1)S(1)}, bf16[16,4096]{1,0:T(8,128)(2,1)S(1)}, u32[]{:S(2)}, u32[]{:S(2)}) collective-permute-start(bf16[16,4096]{1,0:T(8,128)(2,1)S(1)} %slice.124), channel_id=1, source_target_pairs={{0,8},{1,9},{2,10},{3,11},{4,12},{5,13},{6,14},{7,15},{8,0},{9,1},... | collective-permute-start | bytes 393224 | tf_op jit(solution)/shard_map/ppermute | solution.py:31
  222.1 6.9 %collective-permute-done.13 = bf16[16,4096]{1,0:T(8,128)(2,1)S(1)} collective-permute-done((bf16[16,4096]{1,0:T(8,128)(2,1)S(1)}, bf16[16,4096]{1,0:T(8,128)(2,1)S(1)}, u32[]{:S(2)}, u32[]{:S(2)}) %collective-permute-start.13) | collective-permute-done | bytes 131104 | tf_op jit(solution)/shard_map/ppermute | solution.py:31
  229.1 2.8 %collective-permute-done.5 = bf16[16,4096]{1,0:T(8,128)(2,1)S(1)} collective-permute-done((bf16[16,4096]{1,0:T(8,128)(2,1)S(1)}, bf16[16,4096]{1,0:T(8,128)(2,1)S(1)}, u32[]{:S(2)}, u32[]{:S(2)}) %collective-permute-start.5) | collective-permute-done | bytes 131104 | tf_op jit(solution)/shard_map/ppermute | solution.py:31
  (87 shorter events, 28.2 us)
Async XLA Ops:
  4.2 37.0 %all-to-all-start.1 = ((bf16[8,648,2,128]{3,2,1,0:T(2,128)(2,1)}), bf16[8,648,2,128]{3,2,1,0:T(2,128)(2,1)S(1)}, u32[]{:S(2)}, u32[]{:S(2)}) async-start(bf16[8,648,2,128]{3,2,1,0:T(2,128)(2,1)} %split_heads.3), calls=%async_computation.1 | async-start | bytes 5308416 | tf_op jit(solution)/shard_map/all_to_all | solution.py:634
  9.5 151.3 %collective-permute-start.2 = (bf16[512,8192]{1,0:T(8,128)(2,1)}, bf16[512,8192]{1,0:T(8,128)(2,1)}, u32[]{:S(2)}, u32[]{:S(2)}) collective-permute-start(bf16[512,8192]{1,0:T(8,128)(2,1)} %refs_1_.3), channel_id=1, source_target_pairs={{0,1},{1,0},{2,3},{3,2},{4,5},{5,4},{6,7},{7,6},{8,9},{9,8},{10,11... | collective-permute-start | bytes 25165832 | tf_op jit(solution)/shard_map/ppermute | solution.py:31
  41.2 46.7 %all-to-all-start = ((bf16[8,392,2,128]{3,2,1,0:T(2,128)(2,1)}), bf16[8,392,2,128]{3,2,1,0:T(2,128)(2,1)}, u32[]{:S(2)}, u32[]{:S(2)}) async-start(bf16[8,392,2,128]{3,2,1,0:T(2,128)(2,1)} %split_heads.2), calls=%async_computation | async-start | bytes 3211264 | tf_op jit(solution)/shard_map/all_to_all | solution.py:634
  97.0 19.2 %collective-permute-start.9 = (bf16[1072,128]{1,0:T(8,128)(2,1)}, bf16[1072,128]{1,0:T(8,128)(2,1)S(1)}, u32[]{:S(2)}, u32[]{:S(2)}) collective-permute-start(bf16[1072,128]{1,0:T(8,128)(2,1)} %get-tuple-element.31), channel_id=1, source_target_pairs={{0,0},{1,8},{2,2},{3,10},{4,4},{5,12},{6,6},{7,14},{8,1},{9,9},{10... | collective-permute-start | bytes 823304 | tf_op jit(solution)/shard_map/ppermute | solution.py:31
  98.6 17.7 %collective-permute-start.10 = (bf16[1072,128]{1,0:T(8,128)(2,1)}, bf16[1072,128]{1,0:T(8,128)(2,1)S(1)}, u32[]{:S(2)}, u32[]{:S(2)}) collective-permute-start(bf16[1072,128]{1,0:T(8,128)(2,1)} %get-tuple-element.32), channel_id=1, source_target_pairs={{0,1},{1,9},{2,3},{3,11},{4,5},{5,13},{6,7},{7,15},{8,0},{9,8},{10... | collective-permute-start | bytes 823304 | tf_op jit(solution)/shard_map/ppermute | solution.py:31
  110.9 7.8 %collective-permute-start = (bf16[1072,128]{1,0:T(8,128)(2,1)}, bf16[1072,128]{1,0:T(8,128)(2,1)S(1)}, u32[]{:S(2)}, u32[]{:S(2)}) collective-permute-start(bf16[1072,128]{1,0:T(8,128)(2,1)} %get-tuple-element.24), channel_id=1, source_target_pairs={{0,0},{1,8},{2,2},{3,10},{4,4},{5,12},{6,6},{7,14},{8,1},{9,9},{10... | collective-permute-start | bytes 823304 | tf_op jit(solution)/shard_map/ppermute | solution.py:31
  112.5 53.9 %collective-permute-start.1 = (bf16[1072,128]{1,0:T(8,128)(2,1)}, bf16[1072,128]{1,0:T(8,128)(2,1)S(1)}, u32[]{:S(2)}, u32[]{:S(2)}) collective-permute-start(bf16[1072,128]{1,0:T(8,128)(2,1)} %get-tuple-element.25), channel_id=1, source_target_pairs={{0,1},{1,9},{2,3},{3,11},{4,5},{5,13},{6,7},{7,15},{8,0},{9,8},{10... | collective-permute-start | bytes 823304 | tf_op jit(solution)/shard_map/ppermute | solution.py:31
  116.2 66.5 %collective-permute-start.17 = (bf16[128,2,1024]{2,1,0:T(2,128)(2,1)}, bf16[128,2,1024]{2,1,0:T(2,128)(2,1)S(1)}, u32[]{:S(2)}, u32[]{:S(2)}) collective-permute-start(bf16[128,2,1024]{2,1,0:T(2,128)(2,1)} %get-tuple-element.38), channel_id=1, source_target_pairs={{0,1},{1,2},{2,3},{3,4},{4,5},{5,6},{6,7},{7,8},{8,9},{9,10},{10,1... | collective-permute-start | bytes 1572872 | tf_op jit(solution)/shard_map/ppermute | solution.py:31
  116.3 67.9 %collective-permute-start.18 = (bf16[128,2,1024]{2,1,0:T(2,128)(2,1)}, bf16[128,2,1024]{2,1,0:T(2,128)(2,1)S(1)}, u32[]{:S(2)}, u32[]{:S(2)}) collective-permute-start(bf16[128,2,1024]{2,1,0:T(2,128)(2,1)} %get-tuple-element.39), channel_id=1, source_target_pairs={{0,2},{1,3},{2,4},{3,5},{4,6},{5,7},{6,8},{7,9},{8,10},{9,11},{10,... | collective-permute-start | bytes 1572872 | tf_op jit(solution)/shard_map/ppermute | solution.py:31
  118.7 47.7 %copy-start.10 = (bf16[1072,128]{1,0:T(8,128)(2,1)}, bf16[1072,128]{1,0:T(8,128)(2,1)S(1)}, u32[]{:S(2)}) copy-start(bf16[1072,128]{1,0:T(8,128)(2,1)S(1)} %collective-permute-done.refs_0_) | copy-start | bytes 823300
  118.7 65.6 %collective-permute-start.19 = (bf16[128,2,1024]{2,1,0:T(2,128)(2,1)}, bf16[128,2,1024]{2,1,0:T(2,128)(2,1)S(1)}, u32[]{:S(2)}, u32[]{:S(2)}) collective-permute-start(bf16[128,2,1024]{2,1,0:T(2,128)(2,1)} %get-tuple-element.40), channel_id=1, source_target_pairs={{0,3},{1,4},{2,5},{3,6},{4,7},{5,8},{6,9},{7,10},{8,11},{9,12},{10... | collective-permute-start | bytes 1572872 | tf_op jit(solution)/shard_map/ppermute | solution.py:31
  160.9 24.2 %collective-permute-start.20 = (bf16[128,2,1024]{2,1,0:T(2,128)(2,1)}, bf16[128,2,1024]{2,1,0:T(2,128)(2,1)S(1)}, u32[]{:S(2)}, u32[]{:S(2)}) collective-permute-start(bf16[128,2,1024]{2,1,0:T(2,128)(2,1)} %get-tuple-element.41), channel_id=1, source_target_pairs={{0,4},{1,5},{2,6},{3,7},{4,8},{5,9},{6,10},{7,11},{8,12},{9,13},{1... | collective-permute-start | bytes 1572872 | tf_op jit(solution)/shard_map/ppermute | solution.py:31
  166.4 23.6 %collective-permute-start.11 = (bf16[64,4096]{1,0:T(8,128)(2,1)}, bf16[64,4096]{1,0:T(8,128)(2,1)}, u32[]{:S(2)}, u32[]{:S(2)}) collective-permute-start(bf16[64,4096]{1,0:T(8,128)(2,1)} %get-tuple-element.34), channel_id=1, source_target_pairs={{0,2},{1,3},{2,0},{3,1},{4,6},{5,7},{6,4},{7,5},{8,10},{9,11},{10,... | collective-permute-start | bytes 1572872 | tf_op jit(solution)/shard_map/ppermute | solution.py:31
  182.8 15.2 %collective-permute-start.3 = (bf16[64,4096]{1,0:T(8,128)(2,1)}, bf16[64,4096]{1,0:T(8,128)(2,1)}, u32[]{:S(2)}, u32[]{:S(2)}) collective-permute-start(bf16[64,4096]{1,0:T(8,128)(2,1)} %get-tuple-element.27), channel_id=1, source_target_pairs={{0,2},{1,3},{2,0},{3,1},{4,6},{5,7},{6,4},{7,5},{8,10},{9,11},{10,... | collective-permute-start | bytes 1572872 | tf_op jit(solution)/shard_map/ppermute | solution.py:31
  184.3 15.1 %collective-permute-start.6 = (bf16[64,4096]{1,0:T(8,128)(2,1)}, bf16[64,4096]{1,0:T(8,128)(2,1)}, u32[]{:S(2)}, u32[]{:S(2)}) collective-permute-start(bf16[64,4096]{1,0:T(8,128)(2,1)} %get-tuple-element.30), channel_id=1, source_target_pairs={{0,4},{1,5},{2,6},{3,7},{4,0},{5,1},{6,2},{7,3},{8,12},{9,13},{10,... | collective-permute-start | bytes 1572872 | tf_op jit(solution)/shard_map/ppermute | solution.py:31
  184.3 24.9 %collective-permute-start.14 = (bf16[64,4096]{1,0:T(8,128)(2,1)}, bf16[64,4096]{1,0:T(8,128)(2,1)}, u32[]{:S(2)}, u32[]{:S(2)}) collective-permute-start(bf16[64,4096]{1,0:T(8,128)(2,1)} %get-tuple-element.37.refs_4_), channel_id=1, source_target_pairs={{0,2},{1,3},{2,0},{3,1},{4,6},{5,7},{6,4},{7,5},{8,10},{9,11},{10,... | collective-permute-start | bytes 1572872 | tf_op jit(solution)/shard_map/ppermute | solution.py:31
  191.3 19.3 %collective-permute-start.12 = (bf16[32,4096]{1,0:T(8,128)(2,1)S(1)}, bf16[32,4096]{1,0:T(8,128)(2,1)S(1)}, u32[]{:S(2)}, u32[]{:S(2)}) collective-permute-start(bf16[32,4096]{1,0:T(8,128)(2,1)S(1)} %slice.121), channel_id=1, source_target_pairs={{0,4},{1,5},{2,6},{3,7},{4,0},{5,1},{6,2},{7,3},{8,12},{9,13},{10,... | collective-permute-start | bytes 786440 | tf_op jit(solution)/shard_map/ppermute | solution.py:31
  199.1 15.8 %collective-permute-start.4 = (bf16[32,4096]{1,0:T(8,128)(2,1)S(1)}, bf16[32,4096]{1,0:T(8,128)(2,1)S(1)}, u32[]{:S(2)}, u32[]{:S(2)}) collective-permute-start(bf16[32,4096]{1,0:T(8,128)(2,1)S(1)} %slice.123), channel_id=1, source_target_pairs={{0,4},{1,5},{2,6},{3,7},{4,0},{5,1},{6,2},{7,3},{8,12},{9,13},{10,... | collective-permute-start | bytes 786440 | tf_op jit(solution)/shard_map/ppermute | solution.py:31
  200.6 14.5 %collective-permute-start.7 = (bf16[32,4096]{1,0:T(8,128)(2,1)S(1)}, bf16[32,4096]{1,0:T(8,128)(2,1)S(1)}, u32[]{:S(2)}, u32[]{:S(2)}) collective-permute-start(bf16[32,4096]{1,0:T(8,128)(2,1)S(1)} %slice.122), channel_id=1, source_target_pairs={{0,2},{1,3},{2,0},{3,1},{4,6},{5,7},{6,4},{7,5},{8,10},{9,11},{10,... | collective-permute-start | bytes 786440 | tf_op jit(solution)/shard_map/ppermute | solution.py:31
  210.3 9.2 %collective-permute-start.15 = (bf16[32,4096]{1,0:T(8,128)(2,1)S(1)}, bf16[32,4096]{1,0:T(8,128)(2,1)S(1)}, u32[]{:S(2)}, u32[]{:S(2)}) collective-permute-start(bf16[32,4096]{1,0:T(8,128)(2,1)S(1)} %slice.120), channel_id=1, source_target_pairs={{0,4},{1,5},{2,6},{3,7},{4,0},{5,1},{6,2},{7,3},{8,12},{9,13},{10,... | collective-permute-start | bytes 786440 | tf_op jit(solution)/shard_map/ppermute | solution.py:31
  210.7 18.3 %collective-permute-start.13 = (bf16[16,4096]{1,0:T(8,128)(2,1)S(1)}, bf16[16,4096]{1,0:T(8,128)(2,1)S(1)}, u32[]{:S(2)}, u32[]{:S(2)}) collective-permute-start(bf16[16,4096]{1,0:T(8,128)(2,1)S(1)} %slice.125), channel_id=1, source_target_pairs={{0,8},{1,9},{2,10},{3,11},{4,12},{5,13},{6,14},{7,15},{8,0},{9,1},... | collective-permute-start | bytes 393224 | tf_op jit(solution)/shard_map/ppermute | solution.py:31
  215.0 16.8 %collective-permute-start.5 = (bf16[16,4096]{1,0:T(8,128)(2,1)S(1)}, bf16[16,4096]{1,0:T(8,128)(2,1)S(1)}, u32[]{:S(2)}, u32[]{:S(2)}) collective-permute-start(bf16[16,4096]{1,0:T(8,128)(2,1)S(1)} %slice.127), channel_id=1, source_target_pairs={{0,8},{1,9},{2,10},{3,11},{4,12},{5,13},{6,14},{7,15},{8,0},{9,1},... | collective-permute-start | bytes 393224 | tf_op jit(solution)/shard_map/ppermute | solution.py:31
  215.2 19.1 %collective-permute-start.8 = (bf16[16,4096]{1,0:T(8,128)(2,1)S(1)}, bf16[16,4096]{1,0:T(8,128)(2,1)S(1)}, u32[]{:S(2)}, u32[]{:S(2)}) collective-permute-start(bf16[16,4096]{1,0:T(8,128)(2,1)S(1)} %slice.126), channel_id=1, source_target_pairs={{0,8},{1,9},{2,10},{3,11},{4,12},{5,13},{6,14},{7,15},{8,0},{9,1},... | collective-permute-start | bytes 393224 | tf_op jit(solution)/shard_map/ppermute | solution.py:31
  219.6 16.1 %collective-permute-start.16 = (bf16[16,4096]{1,0:T(8,128)(2,1)S(1)}, bf16[16,4096]{1,0:T(8,128)(2,1)S(1)}, u32[]{:S(2)}, u32[]{:S(2)}) collective-permute-start(bf16[16,4096]{1,0:T(8,128)(2,1)S(1)} %slice.124), channel_id=1, source_target_pairs={{0,8},{1,9},{2,10},{3,11},{4,12},{5,13},{6,14},{7,15},{8,0},{9,1},... | collective-permute-start | bytes 393224 | tf_op jit(solution)/shard_map/ppermute | solution.py:31
  (13 other events, 188.3 us)
